TPU v7x, 32 devices: a whole 2x2x4 slice. The times are simulated.
32 devices in a mesh: dp: 4 (over y, x), tensor: 8 (over z, core).
Axes of the slice: x: 2, y: 2, z: 4, core: 2. Of those that a mesh axis runs over, the one named last changes fastest.
Arguments:
- activations: bfloat16 [1024, 16384], P('dp', 'tensor'), may hold values from -6 to 6
- angles: float32 [14, 8192], P(None, 'tensor'), may hold values from -3.140625 to 3.140625
- clip_bits: int32 [64, 16384], P('dp', 'tensor'), may hold values from 0 to 65535, as said below
- codes: bfloat16 [16384, 10240], P('tensor', 'dp'), may hold values from -127 to 127, as said below
- exponents: int32 [10240], replicated, may hold values from -16 to -13
- cotangent: bfloat16 [1024, 10240], P('dp', 'tensor'), may hold values from -6 to 6
Outputs:
- input_grad: bfloat16 [1024, 16384], P('dp', 'tensor')
- angle_grad: float32 [14, 8192], P(None, 'tensor')
Inputs may be any that keep to these rules, and one draw needn't show every extreme that they name: Bit k (0 to 15) of clip_bits[w, i] is the clip mask of token 16 w + k at feature i; higher bits are zero. `codes`: every entry is a whole number.
All inputs are finite; a program needn't handle non-finite values.
Results may differ from a plain program's by a relative error of at most 0.003.
Values may be sent and summed in bfloat16 or wider, within the bound.
No kernel may reach another device: no remote copies, remote signals or barrier semaphores. Data moves between devices by JAX's collectives and lax.ppermute only.
A program may use at most 128 MiB of HBM per device.

v0:
```python
import functools

import jax
import jax.numpy as jnp
from jax import lax
from jax.experimental import pallas as pl
from jax.experimental.pallas import tpu as pltpu
from jax.sharding import PartitionSpec as P


LANES = 128
LANE_BITS = 7
HIGH = lax.Precision.HIGHEST


CHUNKS = 2
STEP = 16
FRACTION = 14.0


def swap(value, axis, mask):
    pairs = [(source, source ^ mask) for source in range(lax.axis_size(axis))]
    return lax.ppermute(value, axis, pairs)


def pick(stacked, index):
    return lax.dynamic_index_in_dim(stacked, index, 0, keepdims=False)


def drop_bit(index, bit):
    return ((index >> (bit + 1)) << bit) | (index & ((1 << bit) - 1))


def lane_selectors(sections):
    lane = jnp.arange(LANES, dtype=jnp.int32)
    rows = []
    signs = []
    for section in range(sections):
        pair = drop_bit(lane, section)
        hot = pair[None, :] == jnp.arange(LANES // 2, dtype=jnp.int32)[:, None]
        rows.append(hot.astype(jnp.float32))
        signs.append(jnp.where((lane >> section) & 1 == 0, -1.0, 1.0).astype(jnp.float32))
    return jnp.stack(rows), jnp.stack(signs)


def local_tables(cosine, sine, width):
    local = cosine.shape[0]
    tiles = width // LANES
    hot, signs = lane_selectors(LANE_BITS)

    def lanes(values):
        shaped = values[:LANE_BITS].reshape(LANE_BITS, tiles, LANES // 2)
        return jnp.einsum("stk,skl->stl", shaped, hot, precision=HIGH)

    def whole(section, values, sign):
        step = 1 << (section - LANE_BITS)
        shaped = values.reshape(tiles // (2 * step), 1, step, LANES)
        return jnp.concatenate([sign * shaped, shaped], axis=1).reshape(1, tiles, LANES)

    cos_rows = [lanes(cosine)]
    sin_rows = [lanes(sine) * signs[:, None, :]]
    for section in range(LANE_BITS, local):
        cos_rows.append(whole(section, cosine[section], 1.0))
        sin_rows.append(whole(section, sine[section], -1.0))
    cos_table = jnp.concatenate(cos_rows, axis=0).reshape(local, width)
    sin_table = jnp.concatenate(sin_rows, axis=0).reshape(local, width)
    return cos_table, sin_table


def lane_partner(value, section):
    half = 1 << section
    lane = lax.broadcasted_iota(jnp.int32, value.shape, 1)
    up = pltpu.roll(value, half, 1)
    if 2 * half == LANES:
        return up
    down = pltpu.roll(value, LANES - half, 1)
    return jnp.where((lane & half) == 0, down, up)


def tile_at(tile):
    return pl.ds(tile * LANES, LANES)


def encode(values, store):
    most = functools.reduce(jnp.maximum, [jnp.abs(value) for value in values])
    most = jnp.max(most, axis=1, keepdims=True)
    power = jnp.ceil(jnp.log2(jnp.maximum(most, 1e-30)))
    factor = jnp.exp2(FRACTION - power)
    for tile, value in enumerate(values):
        store(tile, jnp.round(value * factor).astype(jnp.int32).astype(jnp.int16))
    power = jnp.broadcast_to(power, values[0].shape)
    store(len(values), power.astype(jnp.int32).astype(jnp.int16))


def widen(codes):
    return codes.astype(jnp.int32).astype(jnp.float32)


def scale_of(ref, at, width):
    return jnp.exp2(widen(ref[at, pl.ds(width, LANES)]) - FRACTION)


def product_kernel(ways, place_ref, *refs):
    token_refs = refs[:ways]
    code_refs = refs[ways : 2 * ways]
    scale_refs = refs[2 * ways : 3 * ways]
    out_refs = refs[3 * ways :]
    total = None
    for tokens, codes, scale in zip(token_refs, code_refs, scale_refs):
        weight = codes[...] * scale[0]
        part = lax.dot_general(
            tokens[...],
            weight,
            (((1,), (1,)), ((), ())),
            preferred_element_type=jnp.float32,
        )
        total = part if total is None else total + part
    rows = out_refs[0].shape[0]
    for index, ref in enumerate(out_refs):
        ref[...] = total[index * rows : (index + 1) * rows].astype(ref.dtype)


def product(place, tokens, codes, scale, outs, dtype):
    ways = len(tokens)
    width = codes.shape[0]
    rows, part = tokens[0].shape
    block = min(width, 256)
    code_spec = lambda j: pl.BlockSpec((block, part), lambda i, p: (i, p[0] ^ j))
    scale_spec = lambda j: pl.BlockSpec((1, 1, part), lambda i, p: (p[1] + (p[0] ^ j), 0, 0))
    return pl.pallas_call(
        functools.partial(product_kernel, ways),
        grid_spec=pltpu.PrefetchScalarGridSpec(
            num_scalar_prefetch=1,
            grid=(width // block,),
            in_specs=[pl.BlockSpec((rows, part), lambda i, p: (0, 0))] * ways
            + [code_spec(j) for j in range(ways)]
            + [scale_spec(j) for j in range(ways)],
            out_specs=[pl.BlockSpec((rows // outs, block), lambda i, p: (0, i))] * outs,
        ),
        out_shape=[jax.ShapeDtypeStruct((rows // outs, width), dtype)] * outs,
        cost_estimate=pl.CostEstimate(
            flops=2 * rows * part * ways * width,
            bytes_accessed=2 * part * ways * width,
            transcendentals=0,
        ),
        name="product",
    )(place, *tokens, *[codes] * ways, *[scale] * ways)


def forward_kernel(local, act_ref, cos_ref, sin_ref, states_ref, code_ref):
    rows, width = act_ref.shape
    tiles = width // LANES

    def block(index, carry):
        at = pl.ds(pl.multiple_of(index * STEP, STEP), STEP)
        field = []
        for tile in range(tiles):
            value = act_ref[at, tile_at(tile)].astype(jnp.float32)
            for section in range(LANE_BITS):
                other = lane_partner(value, section)
                cosine = cos_ref[section : section + 1, tile_at(tile)]
                signed = sin_ref[section : section + 1, tile_at(tile)]
                value = cosine * value + signed * other
                states_ref[section, at, tile_at(tile)] = value
            field.append(value)
        for section in range(LANE_BITS, local):
            gap = 1 << (section - LANE_BITS)
            for tile in range(tiles):
                if tile & gap:
                    continue
                cosine = cos_ref[section : section + 1, tile_at(tile)]
                signed = sin_ref[section : section + 1, tile_at(tile)]
                low, high = field[tile], field[tile + gap]
                field[tile] = cosine * low + signed * high
                field[tile + gap] = cosine * high - signed * low
            for tile in range(tiles):
                states_ref[section, at, tile_at(tile)] = field[tile]

        def store(tile, codes):
            code_ref[at, tile_at(tile)] = codes

        encode(field, store)
        return carry

    lax.fori_loop(0, rows // STEP, block, 0)


def forward_local(acts, cos_table, sin_table):
    rows, width = acts.shape
    local = cos_table.shape[0]
    block = min(rows, 32)
    table = pl.BlockSpec((local, width), lambda i: (0, 0))
    return pl.pallas_call(
        functools.partial(forward_kernel, local),
        grid=(rows // block,),
        in_specs=[pl.BlockSpec((block, width), lambda i: (i, 0)), table, table],
        out_specs=[
            pl.BlockSpec((local, block, width), lambda i: (0, i, 0)),
            pl.BlockSpec((block, width + LANES), lambda i: (i, 0)),
        ],
        out_shape=[
            jax.ShapeDtypeStruct((local, rows, width), jnp.float32),
            jax.ShapeDtypeStruct((rows, width + LANES), jnp.int16),
        ],
        cost_estimate=pl.CostEstimate(
            flops=6 * local * rows * width,
            bytes_accessed=4 * (local + 1) * rows * width,
            transcendentals=0,
        ),
        name="forward_local",
    )(acts, cos_table, sin_table)


def core_kernel(place_ref, state_ref, other_ref, trig_ref, pair_ref, *code_refs):
    width = state_ref.shape[2]
    count = len(code_refs)
    depth = state_ref.shape[1]
    tiles = width // LANES
    half = width // 2
    place = place_ref[0]
    start = place_ref[1] * half
    cosine_at = lambda at: trig_ref[0:1, at]
    signed_at = lambda at: trig_ref[1:2, at]
    for piece in range(count):
        source = place ^ piece
        mine = state_ref.at[source]
        other = other_ref.at[source]
        at = pl.ds(0, depth)
        scale = scale_of(other, at, width)
        field = []
        for tile in range(tiles):
            lanes = tile_at(tile)
            value = mine[at, lanes]
            partner = widen(other[at, lanes]) * scale
            field.append(cosine_at(lanes) * value + signed_at(lanes) * partner)

        def store(tile, codes):
            code_refs[piece][at, tile_at(tile)] = codes

        encode(field, store)
        for tile in range(tiles // 2):
            lanes = pl.ds(pl.multiple_of(start + tile * LANES, LANES), LANES)
            value = mine[at, lanes]
            partner = widen(other[at, lanes]) * scale
            cosine, signed = cosine_at(lanes), signed_at(lanes)
            pair_ref[0, source, at, tile_at(tile)] = cosine * value + signed * partner
            pair_ref[1, source, at, tile_at(tile)] = cosine * partner - signed * value


def core_forward(place, states, other, trig, count, chunks):
    local, rows, width = states.shape
    depth = rows // (chunks * count)
    view = states.reshape(local, chunks, count, depth, width)
    codes = other.reshape(chunks, count, depth, width + LANES)
    per = depth // STEP
    outs = pl.pallas_call(
        core_kernel,
        grid_spec=pltpu.PrefetchScalarGridSpec(
            num_scalar_prefetch=1,
            grid=(chunks, per),
            in_specs=[
                pl.BlockSpec(
                    (None, None, count, STEP, width), lambda i, j, p: (local - 1, i, 0, j, 0)
                ),
                pl.BlockSpec((None, count, STEP, width + LANES), lambda i, j, p: (i, 0, j, 0)),
                pl.BlockSpec((2, width), lambda i, j, p: (0, 0)),
            ],
            out_specs=[
                pl.BlockSpec((2, None, count, STEP, width // 2), lambda i, j, p: (0, i, 0, j, 0))
            ]
            + [pl.BlockSpec((STEP, width + LANES), lambda i, j, p: (i * per + j, 0))] * count,
        ),
        out_shape=[jax.ShapeDtypeStruct((2, chunks, count, depth, width // 2), jnp.float32)]
        + [jax.ShapeDtypeStruct((chunks * depth, width + LANES), jnp.int16)] * count,
        cost_estimate=pl.CostEstimate(
            flops=10 * rows * width, bytes_accessed=12 * rows * width, transcendentals=0
        ),
        name="core_forward",
    )(place, view, codes, trig)
    return outs[0].reshape(2, rows, width // 2), outs[1:]


def gather_kernel(count, place_ref, *refs):
    code_refs = refs[-count:]
    first_ref = refs[0]
    part_refs = refs[1 : -count - 1]
    words_ref = refs[-count - 1]
    width = first_ref.shape[2]
    place = place_ref[0]
    token = lax.broadcasted_iota(jnp.int32, (STEP, LANES), 0)
    for piece in range(count):
        source = place ^ piece
        values = []
        for tile in range(width // LANES):
            lanes = tile_at(tile)
            value = first_ref[source, :, lanes]
            for ref in part_refs:
                value = value + ref[source, :, lanes].astype(jnp.float32)
            words = words_ref[source, 0, :, lanes]
            bits = jnp.bitwise_and(jnp.right_shift(jnp.broadcast_to(words, token.shape), token), 1)
            values.append(value * bits.astype(jnp.float32))

        def store(tile, codes):
            code_refs[piece][:, tile_at(tile)] = codes

        encode(values, store)


def gather_parts(place, parts, words, count):
    rows, width = parts[0].shape
    depth = rows // count
    piece = pl.BlockSpec((count, STEP, width), lambda i, p: (0, i, 0))
    return pl.pallas_call(
        functools.partial(gather_kernel, count),
        grid_spec=pltpu.PrefetchScalarGridSpec(
            num_scalar_prefetch=1,
            grid=(depth // STEP,),
            in_specs=[piece] * len(parts)
            + [pl.BlockSpec((count, 1, 1, width), lambda i, p: (0, i, 0, 0))],
            out_specs=[pl.BlockSpec((STEP, width + LANES), lambda i, p: (i, 0))] * count,
        ),
        out_shape=[jax.ShapeDtypeStruct((depth, width + LANES), jnp.int16)] * count,
        cost_estimate=pl.CostEstimate(
            flops=12 * rows * width, bytes_accessed=12 * rows * width, transcendentals=0
        ),
        name="gather_parts",
    )(
        place,
        *[part.reshape(count, depth, width) for part in parts],
        words.reshape(count, depth // STEP, 1, width),
    )


def cross_kernel(count, bits, *refs):
    grad_refs = refs[:count]
    field_refs = refs[count : 2 * count]
    cos_ref, sin_ref = refs[2 * count : 2 * count + 2]
    out_refs = refs[2 * count + 2 : 3 * count + 2]
    term_ref, held_ref, sum_ref = refs[3 * count + 2 :]
    width = cos_ref.shape[2]
    tiles = width // LANES
    rows = pl.ds(0, STEP)
    index = pl.program_id(0)

    @pl.when(index == 0)
    def _():
        sum_ref[...] = jnp.zeros_like(sum_ref)

    grad_scales = [scale_of(ref, rows, width) for ref in grad_refs]
    field_scales = [scale_of(ref, rows, width) for ref in field_refs]
    for tile in range(tiles):
        lanes = tile_at(tile)
        levels = [[widen(r[rows, lanes]) * s for r, s in zip(field_refs, field_scales)]]
        for bit in range(bits - 1):
            field = list(levels[-1])
            for low in range(count):
                if low & (1 << bit):
                    continue
                high = low | (1 << bit)
                pair = drop_bit(low, bit)
                cosine = cos_ref[bit, pair : pair + 1, lanes]
                sine = sin_ref[bit, pair : pair + 1, lanes]
                v_low, v_high = field[low], field[high]
                field[low] = cosine * v_low - sine * v_high
                field[high] = sine * v_low + cosine * v_high
            levels.append(field)
        grad = [widen(r[rows, lanes]) * s for r, s in zip(grad_refs, grad_scales)]
        for bit in reversed(range(bits)):
            before = levels[bit]
            for low in range(count):
                if low & (1 << bit):
                    continue
                high = low | (1 << bit)
                pair = drop_bit(low, bit)
                cosine = cos_ref[bit, pair : pair + 1, lanes]
                sine = sin_ref[bit, pair : pair + 1, lanes]
                g_low, g_high = grad[low], grad[high]
                grad[low] = cosine * g_low + sine * g_high
                grad[high] = cosine * g_high - sine * g_low
                term = grad[high] * before[low] - grad[low] * before[high]
                sum_ref[bit, pair, :, lanes] += jnp.sum(term.reshape(STEP // 8, 8, LANES), axis=0)
        for piece in range(count):
            held_ref[piece, :, lanes] = grad[piece]

    for piece in range(count):

        def store(tile, codes):
            out_refs[piece][:, tile_at(tile)] = codes

        encode([held_ref[piece, :, tile_at(tile)] for tile in range(tiles)], store)

    @pl.when(index == pl.num_programs(0) - 1)
    def _():
        term_ref[...] = jnp.sum(sum_ref[...], axis=2)


def cross_sections(grads, fields, cos_table, sin_table, offset):
    count = len(grads)
    bits, pairs, width = cos_table.shape
    rows, wide = grads[0].shape
    piece = pl.BlockSpec((STEP, wide), lambda i: (i, 0))
    moved = pl.BlockSpec((STEP, wide), lambda i: (i + offset * (rows // STEP), 0))
    table = pl.BlockSpec(cos_table.shape, lambda i: (0, 0, 0))
    outs = pl.pallas_call(
        functools.partial(cross_kernel, count, bits),
        grid=(rows // STEP,),
        in_specs=[piece] * count + [moved] * count + [table] * 2,
        out_specs=[piece] * count + [table],
        out_shape=[jax.ShapeDtypeStruct((rows, wide), jnp.int16)] * count
        + [jax.ShapeDtypeStruct(cos_table.shape, jnp.float32)],
        scratch_shapes=[
            pltpu.VMEM((count, STEP, width), jnp.float32),
            pltpu.VMEM((bits, pairs, 8, width), jnp.float32),
        ],
        cost_estimate=pl.CostEstimate(
            flops=20 * bits * count * rows * width,
            bytes_accessed=6 * count * rows * width,
            transcendentals=0,
        ),
        name="cross_sections",
    )(*grads, *fields, cos_table, sin_table)
    return outs[:count], outs[count]


def backward_kernel(
    local, place_ref, grad_ref, other_ref, states_ref, pair_ref, trig_ref, cos_ref, sin_ref,
    hot_ref, lane_in, tile_in, core_in, whole_ref,
    out_ref, lane_out, tile_out, core_out, lane_sum, tile_sum, core_sum,
):
    rows, width = out_ref.shape
    tiles = width // LANES
    half = width // 2
    index = pl.program_id(0)
    start = place_ref[1] * half

    @pl.when(index == 0)
    def _():
        lane_sum[...] = jnp.zeros_like(lane_sum)
        tile_sum[...] = jnp.zeros_like(tile_sum)
        core_sum[...] = jnp.zeros_like(core_sum)

    def folded(value):
        return jnp.sum(value.reshape(STEP // 8, 8, LANES), axis=0)

    def block(number, carry):
        at = pl.ds(pl.multiple_of(number * STEP, STEP), STEP)
        scale = scale_of(grad_ref, at, width)
        other_scale = scale_of(other_ref, at, width)
        for tile in range(tiles // 2):
            lanes = pl.ds(pl.multiple_of(start + tile * LANES, LANES), LANES)
            mine = widen(grad_ref[at, lanes]) * scale
            partner = widen(other_ref[at, lanes]) * other_scale
            term = partner * pair_ref[0, at, tile_at(tile)] - mine * pair_ref[1, at, tile_at(tile)]
            core_sum[tile] += folded(term)
        grad = []
        for tile in range(tiles):
            lanes = tile_at(tile)
            mine = widen(grad_ref[at, lanes]) * scale
            partner = widen(other_ref[at, lanes]) * other_scale
            grad.append(trig_ref[0:1, lanes] * mine - trig_ref[1:2, lanes] * partner)
        for section in reversed(range(LANE_BITS, local)):
            gap = 1 << (section - LANE_BITS)
            for tile in range(tiles):
                if tile & gap:
                    continue
                cosine = cos_ref[section : section + 1, tile_at(tile)]
                signed = sin_ref[section : section + 1, tile_at(tile)]
                low, high = grad[tile], grad[tile + gap]
                before_low = states_ref[section, at, tile_at(tile)]
                before_high = states_ref[section, at, tile_at(tile + gap)]
                term = folded(high * before_low - low * before_high)
                place = drop_bit(tile, section - LANE_BITS)
                tile_sum[section - LANE_BITS, place] += term
                grad[tile] = cosine * low - signed * high
                grad[tile + gap] = cosine * high + signed * low
        for tile in range(tiles):
            value = grad[tile]
            for section in reversed(range(LANE_BITS)):
                cosine = cos_ref[section : section + 1, tile_at(tile)]
                signed = sin_ref[section : section + 1, tile_at(tile)]
                other = lane_partner(value, section)
                state = states_ref[section, at, tile_at(tile)]
                lane_sum[section, tile] += folded(other * state)
                value = cosine * value - signed * other
            out_ref[at, tile_at(tile)] = value.astype(out_ref.dtype)
        return carry

    lax.fori_loop(0, rows // STEP, block, 0)

    @pl.when(index == pl.num_programs(0) - 1)
    def _():
        for section in range(LANE_BITS):
            summed = jnp.sum(lane_sum[section], axis=1)
            lane_out[section] = lane_in[section] + lax.dot_general(
                summed,
                hot_ref[section],
                (((1,), (1,)), ((), ())),
                precision=HIGH,
                preferred_element_type=jnp.float32,
            )
        for section in range(local - LANE_BITS):
            tile_out[section] = tile_in[section] + jnp.sum(tile_sum[section], axis=1)
        core_out[...] = core_in[...] + jnp.sum(core_sum[...], axis=1)


def backward_local(
    place, grad, other, states, pair, trig, cos_table, sin_table, hot, sums, whole, chunk, count,
):
    depth = grad.shape[0] // count
    local, rows, width = states.shape
    tiles = width // LANES
    high = local - LANE_BITS
    base = chunk * count
    block = min(depth, 32)
    per = depth // block
    fixed = lambda shape: pl.BlockSpec(shape, lambda i, p: (0,) * len(shape))
    row_of = lambda i, p: (base + (p[0] ^ (i // per))) * per + i % per
    shapes = [(LANE_BITS, tiles, LANES // 2), (high, tiles // 2, LANES), (tiles // 2, LANES)]
    return pl.pallas_call(
        functools.partial(backward_kernel, local),
        grid_spec=pltpu.PrefetchScalarGridSpec(
            num_scalar_prefetch=1,
            grid=(count * per,),
            in_specs=[
                pl.BlockSpec((block, width + LANES), lambda i, p: (i, 0)),
                pl.BlockSpec((block, width + LANES), lambda i, p: (i, 0)),
                pl.BlockSpec((local, block, width), lambda i, p: (0, row_of(i, p), 0)),
                pl.BlockSpec((2, block, width // 2), lambda i, p: (0, row_of(i, p), 0)),
                fixed((2, width)),
                fixed((local, width)),
                fixed((local, width)),
                fixed(hot.shape),
            ]
            + [fixed(shape) for shape in shapes]
            + [pl.BlockSpec(memory_space=pl.ANY)],
            out_specs=[pl.BlockSpec((block, width), lambda i, p: (row_of(i, p), 0))]
            + [fixed(shape) for shape in shapes],
            scratch_shapes=[
                pltpu.VMEM((LANE_BITS, tiles, 8, LANES), jnp.float32),
                pltpu.VMEM((high, tiles // 2, 8, LANES), jnp.float32),
                pltpu.VMEM((tiles // 2, 8, LANES), jnp.float32),
            ],
        ),
        out_shape=[jax.ShapeDtypeStruct((rows, width), jnp.bfloat16)]
        + [jax.ShapeDtypeStruct(shape, jnp.float32) for shape in shapes],
        input_output_aliases={12: 0},
        cost_estimate=pl.CostEstimate(
            flops=8 * local * depth * count * width,
            bytes_accessed=4 * (local + 2) * depth * count * width,
            transcendentals=0,
        ),
        name="backward_local",
    )(place, grad, other, states, pair, trig, cos_table, sin_table, hot, *sums, whole)


def tree_sum(parts):
    while len(parts) > 1:
        parts = [parts[k] + parts[k + 1] for k in range(0, len(parts), 2)]
    return parts[0]


def gather_shares(value, me, bits):
    for bit in range(bits):
        other = swap(value, "tensor", 1 << bit)
        first = ((me >> bit) & 1) == 0
        value = jnp.concatenate(
            [jnp.where(first, value, other), jnp.where(first, other, value)], axis=0
        )
        if bit == 0:
            pair = value
    return value, pair


def scatter_shares(value, me, bits):
    for bit in reversed(range(bits)):
        halves = value.reshape((2, -1) + value.shape[1:])
        own = (me >> bit) & 1
        value = pick(halves, own) + swap(pick(halves, 1 - own), "tensor", 1 << bit)
    return value[0]


def body(activations, angles, clip_bits, codes, exponents, cotangent):
    rows, width = activations.shape
    sections, share = angles.shape
    groups = lax.axis_size("dp")
    devices = lax.axis_size("tensor")
    ways = devices // groups
    columns = codes.shape[1]
    part = columns // ways
    local = width.bit_length() - 1
    cross = sections - local
    count = devices // 2
    me = lax.axis_index("tensor")
    mine = lax.axis_index("dp")
    level = me // ways
    core = me & 1
    line = me >> 1
    chunks = chunks_of(rows, count)
    chunk_rows = rows // chunks
    place = jnp.stack([line, core])

    remote = []
    near = []
    for q in range(chunks):
        own = cotangent[q * chunk_rows : (q + 1) * chunk_rows]
        blocks = jnp.stack([own] + [swap(own, "tensor", m * ways) for m in range(1, groups)])
        arrived = jnp.concatenate(
            [swap(pick(blocks, level ^ mine ^ m), "dp", m) for m in range(1, groups)],
            axis=0,
        )
        close = pick(blocks, level ^ mine)
        remote.append([arrived] + [swap(arrived, "tensor", m) for m in range(1, ways)])
        near.append([close] + [swap(close, "tensor", m) for m in range(1, ways)])

    scale = jnp.exp2(exponents.astype(jnp.float32)).astype(jnp.bfloat16)
    scale = scale.reshape(-1, 1, part)
    column_place = jnp.stack([me % ways, mine * ways])

    cosine = jnp.cos(angles)
    sine = jnp.sin(angles)
    cos_table, sin_table = local_tables(cosine[:local], sine[:local], width)
    states, last_codes = forward_local(activations, cos_table, sin_table)

    trig = jnp.stack([cosine[local:], sine[local:]])[None]
    trig, first_trig = gather_shares(trig, me, cross)
    flip = (1 - 2 * core).astype(jnp.float32)
    core_trig = jnp.moveaxis(first_trig[:, :, 0], 0, 1).reshape(2, width)
    core_trig = core_trig * jnp.stack([jnp.float32(1), -flip])[:, None]
    trig = jnp.moveaxis(trig, 0, 2).reshape(2, cross, devices // 2, width)
    jj = jnp.arange(count // 2, dtype=jnp.int32)
    cross_cos, cross_sin, flips = [], [], []
    for bit in range(cross - 1):
        pair = (drop_bit(line, bit) ^ jj) * 2 + core
        flips.append((1 - 2 * ((line >> bit) & 1)).astype(jnp.float32))
        cross_cos.append(jnp.take(trig[0, bit + 1], pair, axis=0))
        cross_sin.append(jnp.take(trig[1, bit + 1], pair, axis=0) * flips[-1])
    cross_cos = jnp.stack(cross_cos)
    cross_sin = jnp.stack(cross_sin)

    partner_codes = swap(last_codes, "tensor", 1)
    pair_states, fields = core_forward(place, states, partner_codes, core_trig, count, chunks)
    fields = [fields[0]] + [swap(fields[m], "tensor", 2 * m) for m in range(1, count)]

    hot, signs = lane_selectors(LANE_BITS)
    hot = -hot * signs[:, None, :]
    tiles = width // LANES
    sums = [
        jnp.zeros((LANE_BITS, tiles, LANES // 2), jnp.float32),
        jnp.zeros((local - LANE_BITS, tiles // 2, LANES), jnp.float32),
        jnp.zeros((tiles // 2, LANES), jnp.float32),
    ]
    whole = jnp.zeros((rows, width), jnp.bfloat16)
    cross_terms = []
    backs = []
    word_rows = chunk_rows // 16
    for q in range(chunks):
        sent = product(column_place, remote[q], codes, scale, groups - 1, jnp.bfloat16)
        kept = product(column_place, near[q], codes, scale, 1, jnp.float32)
        parts = list(kept) + [swap(sent[m - 1], "dp", m) for m in range(1, groups)]
        words = clip_bits[q * word_rows : (q + 1) * word_rows]
        grads = gather_parts(place, parts, words, count)
        grads = [grads[0]] + [swap(grads[m], "tensor", 2 * m) for m in range(1, count)]
        grads, terms = cross_sections(grads, fields, cross_cos, cross_sin, q)
        cross_terms.append(terms)
        backs.append([grads[0]] + [swap(grads[m], "tensor", 2 * m) for m in range(1, count)])

    for q in range(chunks):
        grad = jnp.concatenate(backs[q], axis=0)
        outs = backward_local(
            place, grad, swap(grad, "tensor", 1), states,
            pair_states, core_trig, cos_table, sin_table, hot, sums, whole, q, count,
        )
        whole, sums = outs[0], outs[1:]

    terms = functools.reduce(jnp.add, cross_terms)
    natural = jnp.stack(
        [
            jnp.take(terms[bit], drop_bit(line, bit) ^ jj, axis=0) * flips[bit]
            for bit in range(cross - 1)
        ]
    )
    natural = natural.reshape(cross - 1, count // 2, 1, 2, share)
    natural = jnp.where(
        jnp.arange(2, dtype=jnp.int32)[None, None, :, None, None] == core, natural, 0.0
    )
    natural = jnp.moveaxis(natural.reshape(cross - 1, devices, share), 1, 0)
    owned = scatter_shares(natural, me, cross)

    final = jnp.concatenate(
        [
            sums[0].reshape(LANE_BITS, share),
            sums[1].reshape(local - LANE_BITS, share),
            sums[2].reshape(1, share) * flip,
            owned,
        ],
        axis=0,
    )
    angle_grad = tree_sum([final] + [swap(final, "dp", m) for m in range(1, groups)])
    return (whole, angle_grad)


def chunks_of(rows, count):
    chunks = CHUNKS
    while rows // (chunks * count) < STEP:
        chunks //= 2
    return chunks


def solution(mesh):
    placed = (
        P("dp", "tensor"),
        P(None, "tensor"),
        P("dp", "tensor"),
        P("tensor", "dp"),
        P(),
        P("dp", "tensor"),
    )

    return jax.shard_map(
        body,
        mesh=mesh,
        in_specs=placed,
        out_specs=(P("dp", "tensor"), P(None, "tensor")),
        check_vma=False,
    )
```

profile of v0, /device:TPU:8, one launch (start us, length us, event | category | flops | bytes accessed | tf_op | source)
XLA Modules:
  0.0 267.2 jit_solution(7908660064817301070)
XLA Ops:
  2.6 2.6 collective-permute-start.26
  6.4 3.6 %collective-permute-start.1 = (bf16[128,1280]{1,0:T(8,128)(2,1)}, bf16[128,1280]{1,0:T(8,128)(2,1)S(1)}, u32[]{:S(2)}, u32[]{:S(2)}) collective-permute-start(bf16[128,1280]{1,0:T(8,128)(2,1)} %get-tuple-element.97), channel_id=1, source_target_pairs={{0,4},{1,5},{2,6},{3,7},{4,0},{5,1},{6,2},{7,3},{8,12},{9,13},{10,... | collective-permute-start | bytes 983048 | tf_op jit(solution)/shard_map/ppermute | solution.py:23
  17.4 14.4 %forward_local.1 = (f32[11,256,2048]{2,1,0:T(8,128)}, s16[256,2176]{1,0:T(8,128)(2,1)}) custom-call(bf16[256,2048]{1,0:T(8,128)(2,1)} %act_ref.1, f32[11,2048]{1,0:T(8,128)} %concatenate.87.cos_ref, f32[11,2048]{1,0:T(8,128)} %concatenate.97.sin_ref), custom_call_target="tpu_custom_call" | custom-call | flops 34603008 | bytes 25165824 | tf_op jit(solution)/shard_map/forward_local/pallas_call | solution.py:193
  32.0 4.2 %collective-permute-done.19 = f32[2,2,3,1024]{3,2,1,0:T(4,128)S(1)} collective-permute-done((f32[2,2,3,1024]{3,2,1,0:T(4,128)S(1)}, f32[2,2,3,1024]{3,2,1,0:T(4,128)S(1)}, u32[]{:S(2)}, u32[]{:S(2)}) %collective-permute-start.19) | collective-permute-done | bytes 49184 | tf_op jit(solution)/shard_map/ppermute | solution.py:23
  37.2 15.5 %collective-permute-done.20 = f32[4,2,3,1024]{3,2,1,0:T(4,128)S(1)} collective-permute-done((f32[4,2,3,1024]{3,2,1,0:T(4,128)S(1)}, f32[4,2,3,1024]{3,2,1,0:T(4,128)S(1)}, u32[]{:S(2)}, u32[]{:S(2)}) %collective-permute-start.20) | collective-permute-done | bytes 98336 | tf_op jit(solution)/shard_map/ppermute | solution.py:23
  54.5 2.7 collective-permute-start.2
  57.5 2.5 collective-permute-start.31
  60.5 3.1 %collective-permute-done = bf16[128,1280]{1,0:T(8,128)(2,1)S(1)} collective-permute-done((bf16[128,1280]{1,0:T(8,128)(2,1)}, bf16[128,1280]{1,0:T(8,128)(2,1)S(1)}, u32[]{:S(2)}, u32[]{:S(2)}) %collective-permute-start) | collective-permute-done | bytes 327712 | tf_op jit(solution)/shard_map/ppermute | solution.py:23
  65.0 7.0 %collective-permute-done.2 = bf16[128,1280]{1,0:T(8,128)(2,1)S(1)} collective-permute-done((bf16[128,1280]{1,0:T(8,128)(2,1)}, bf16[128,1280]{1,0:T(8,128)(2,1)S(1)}, u32[]{:S(2)}, u32[]{:S(2)}) %collective-permute-start.2) | collective-permute-done | bytes 327712 | tf_op jit(solution)/shard_map/ppermute | solution.py:23
  72.3 2.5 collective-permute-start.6
  78.4 11.4 %collective-permute-done.4 = bf16[128,1280]{1,0:T(8,128)(2,1)S(1)} collective-permute-done((bf16[128,1280]{1,0:T(8,128)(2,1)S(1)}, bf16[128,1280]{1,0:T(8,128)(2,1)S(1)}, u32[]{:S(2)}, u32[]{:S(2)}) %collective-permute-start.4) | collective-permute-done | bytes 327712 | tf_op jit(solution)/shard_map/ppermute | solution.py:23
  91.1 11.2 %product.7 = (bf16[128,2048]{1,0:T(8,128)(2,1)}, bf16[128,2048]{1,0:T(8,128)(2,1)}, bf16[128,2048]{1,0:T(8,128)(2,1)}) custom-call(s32[2]{0:T(128)} %pad_add_fusion.1.place_ref, bf16[384,1280]{1,0:T(8,128)(2,1)} %copy-done, bf16[384,1280]{1,0:T(8,128)(2,1)} %collective-permute-done.32.refs_1_, bf16[2048,2560]{1,0:T(8,128)(2,1)} %refs_3_.7, ...), custom_call_target="tpu_custom_call" | custom-call | flops 4026531840 | bytes 10485760 | tf_op jit(solution)/shard_map/product/pallas_call | solution.py:130
  107.0 11.2 %product.5 = (bf16[128,2048]{1,0:T(8,128)(2,1)}, bf16[128,2048]{1,0:T(8,128)(2,1)}, bf16[128,2048]{1,0:T(8,128)(2,1)}) custom-call(s32[2]{0:T(128)} %pad_add_fusion.1.place_ref, bf16[384,1280]{1,0:T(8,128)(2,1)} %copy-done.1, bf16[384,1280]{1,0:T(8,128)(2,1)} %collective-permute-done.7.refs_1_, bf16[2048,2560]{1,0:T(8,128)(2,1)} %refs_3_.7, ...), custom_call_target="tpu_custom_call" | custom-call | flops 4026531840 | bytes 10485760 | tf_op jit(solution)/shard_map/product/pallas_call | solution.py:130
  122.5 10.1 %product.6 = f32[128,2048]{1,0:T(8,128)} custom-call(s32[2]{0:T(128)} %pad_add_fusion.1.place_ref, bf16[128,1280]{1,0:T(8,128)(2,1)} %copy-done.3, bf16[128,1280]{1,0:T(8,128)(2,1)} %collective-permute-done.28.refs_1_, bf16[2048,2560]{1,0:T(8,128)(2,1)} %refs_3_.7, bf16[2048,2560]{1,0:T(8,128)(2,1)} %refs_3_.7, ...), custom_call_target="tpu_custom_call" | custom-call | flops 1342177280 | bytes 10485760 | tf_op jit(solution)/shard_map/product/pallas_call | solution.py:130
  132.6 5.5 %core_forward.1 = (f32[2,2,4,32,1024]{4,3,2,1,0:T(8,128)}, s16[64,2176]{1,0:T(8,128)(2,1)}, s16[64,2176]{1,0:T(8,128)(2,1)}, s16[64,2176]{1,0:T(8,128)(2,1)}, s16[64,2176]{1,0:T(8,128)(2,1)}) custom-call(s32[2]{0:T(128)} %pad_add_fusion.place_ref, f32[11,2,4,32,2048]{4,3,2,1,0:T(8,128)} %bitcast.149, s16[2,4,32,2176]{3,2,1,0:T(8,128)(2,1)} %bitcast.43.other_ref, ...), custom_call_target="tpu_custom_call" | custom-call | flops 5242880 | bytes 6291456 | tf_op jit(solution)/shard_map/core_forward/pallas_call | solution.py:256
  139.1 3.5 %gather_parts.3 = (s16[32,2176]{1,0:T(8,128)(2,1)}, s16[32,2176]{1,0:T(8,128)(2,1)}, s16[32,2176]{1,0:T(8,128)(2,1)}, s16[32,2176]{1,0:T(8,128)(2,1)}) custom-call(s32[2]{0:T(128)} %pad_add_fusion.place_ref, f32[4,32,2048]{2,1,0:T(8,128)} %bitcast.152, bf16[4,32,2048]{2,1,0:T(8,128)(2,1)} %bitcast.154, bf16[4,32,2048]{2,1,0:T(8,128)(2,1)} %bitcast.155, ...), custom_call_target="tpu_custom_call" | custom-call | flops 3145728 | bytes 3145728 | tf_op jit(solution)/shard_map/gather_parts/pallas_call | solution.py:313
  142.6 3.2 %collective-permute-start.17 = (s16[64,2176]{1,0:T(8,128)(2,1)S(1)}, s16[64,2176]{1,0:T(8,128)(2,1)S(1)}, u32[]{:S(2)}, u32[]{:S(2)}) collective-permute-start(s16[64,2176]{1,0:T(8,128)(2,1)S(1)} %copy-done.28), channel_id=1, source_target_pairs={{0,4},{1,5},{2,6},{3,7},{4,0},{5,1},{6,2},{7,3},{8,12},{9,13},{10,... | collective-permute-start | bytes 835592 | tf_op jit(solution)/shard_map/ppermute | solution.py:23
  149.7 10.2 %product.4 = f32[128,2048]{1,0:T(8,128)} custom-call(s32[2]{0:T(128)} %pad_add_fusion.1.place_ref, bf16[128,1280]{1,0:T(8,128)(2,1)} %copy-done.2, bf16[128,1280]{1,0:T(8,128)(2,1)} %collective-permute-done.3.refs_1_, bf16[2048,2560]{1,0:T(8,128)(2,1)} %refs_3_.7, bf16[2048,2560]{1,0:T(8,128)(2,1)} %refs_3_.7, bf16[8,1,1280]{2,1,0:T(2,128)(2,1)} %reshape.663.refs_4_.refs_5_, ...), custom_call_target="tpu_custom_call" | custom-call | flops 1342177280 | bytes 10485760 | tf_op jit(solution)/shard_map/product/pallas_call | solution.py:130
  160.5 3.5 %gather_parts.2 = (s16[32,2176]{1,0:T(8,128)(2,1)}, s16[32,2176]{1,0:T(8,128)(2,1)}, s16[32,2176]{1,0:T(8,128)(2,1)}, s16[32,2176]{1,0:T(8,128)(2,1)}) custom-call(s32[2]{0:T(128)} %pad_add_fusion.place_ref, f32[4,32,2048]{2,1,0:T(8,128)} %bitcast.153, bf16[4,32,2048]{2,1,0:T(8,128)(2,1)} %bitcast.156, bf16[4,32,2048]{2,1,0:T(8,128)(2,1)} %bitcast.157, ...), custom_call_target="tpu_custom_call" | custom-call | flops 3145728 | bytes 3145728 | tf_op jit(solution)/shard_map/gather_parts/pallas_call | solution.py:313
  167.4 2.8 %collective-permute-start.11 = (s16[32,2176]{1,0:T(8,128)(2,1)}, s16[32,2176]{1,0:T(8,128)(2,1)S(1)}, u32[]{:S(2)}, u32[]{:S(2)}) collective-permute-start(s16[32,2176]{1,0:T(8,128)(2,1)} %get-tuple-element.47), channel_id=1, source_target_pairs={{0,2},{1,3},{2,0},{3,1},{4,6},{5,7},{6,4},{7,5},{8,10},{9,11},{10,... | collective-permute-start | bytes 417800 | tf_op jit(solution)/shard_map/ppermute | solution.py:23
  170.2 6.0 %collective-permute-done.18.refs_7_ = s16[64,2176]{1,0:T(8,128)(2,1)S(1)} collective-permute-done((s16[64,2176]{1,0:T(8,128)(2,1)S(1)}, s16[64,2176]{1,0:T(8,128)(2,1)S(1)}, u32[]{:S(2)}, u32[]{:S(2)}) %collective-permute-start.18) | collective-permute-done | bytes 278560 | tf_op jit(solution)/shard_map/ppermute | solution.py:23
  178.1 10.1 %collective-permute-done.38.refs_3_ = s16[32,2176]{1,0:T(8,128)(2,1)S(1)} collective-permute-done((s16[32,2176]{1,0:T(8,128)(2,1)S(1)}, s16[32,2176]{1,0:T(8,128)(2,1)S(1)}, u32[]{:S(2)}, u32[]{:S(2)}) %collective-permute-start.38) | collective-permute-done | bytes 139296 | tf_op jit(solution)/shard_map/ppermute | solution.py:23
  188.8 3.0 %cross_sections.3 = (s16[32,2176]{1,0:T(8,128)(2,1)}, s16[32,2176]{1,0:T(8,128)(2,1)}, s16[32,2176]{1,0:T(8,128)(2,1)}, s16[32,2176]{1,0:T(8,128)(2,1)}, f32[2,2,2048]{2,1,0:T(2,128)}) custom-call(s16[32,2176]{1,0:T(8,128)(2,1)} %get-tuple-element.64.refs_0_, s16[32,2176]{1,0:T(8,128)(2,1)} %copy-done.17, s16[32,2176]{1,0:T(8,128)(2,1)} %copy-done.19, ...), custom_call_target="tpu_custom_call" | custom-call | flops 10485760 | bytes 1572864 | tf_op jit(solution)/shard_map/cross_sections/pallas_call | solution.py:404
  193.3 3.1 %cross_sections.2 = (s16[32,2176]{1,0:T(8,128)(2,1)}, s16[32,2176]{1,0:T(8,128)(2,1)}, s16[32,2176]{1,0:T(8,128)(2,1)}, s16[32,2176]{1,0:T(8,128)(2,1)}, f32[2,2,2048]{2,1,0:T(2,128)}) custom-call(s16[32,2176]{1,0:T(8,128)(2,1)} %get-tuple-element.46.refs_0_, s16[32,2176]{1,0:T(8,128)(2,1)} %copy-done.18, s16[32,2176]{1,0:T(8,128)(2,1)} %copy-done.20, ...), custom_call_target="tpu_custom_call" | custom-call | flops 10485760 | bytes 1572864 | tf_op jit(solution)/shard_map/cross_sections/pallas_call | solution.py:404
  199.4 3.1 %collective-permute-start.39 = (s16[32,2176]{1,0:T(8,128)(2,1)S(1)}, s16[32,2176]{1,0:T(8,128)(2,1)S(1)}, u32[]{:S(2)}, u32[]{:S(2)}) collective-permute-start(s16[32,2176]{1,0:T(8,128)(2,1)S(1)} %copy-done.31), channel_id=1, source_target_pairs={{0,2},{1,3},{2,0},{3,1},{4,6},{5,7},{6,4},{7,5},{8,10},{9,11},{10,... | collective-permute-start | bytes 417800 | tf_op jit(solution)/shard_map/ppermute | solution.py:23
  204.0 2.9 %collective-permute-start.21 = (s16[32,2176]{1,0:T(8,128)(2,1)}, s16[32,2176]{1,0:T(8,128)(2,1)S(1)}, u32[]{:S(2)}, u32[]{:S(2)}) collective-permute-start(s16[32,2176]{1,0:T(8,128)(2,1)} %get-tuple-element.57), channel_id=1, source_target_pairs={{0,2},{1,3},{2,0},{3,1},{4,6},{5,7},{6,4},{7,5},{8,10},{9,11},{10,... | collective-permute-start | bytes 417800 | tf_op jit(solution)/shard_map/ppermute | solution.py:23
  207.1 8.7 %collective-permute-done.44 = f32[2,2,1024]{2,1,0:T(2,128)S(1)} collective-permute-done((f32[2,2,1024]{2,1,0:T(2,128)S(1)}, f32[2,2,1024]{2,1,0:T(2,128)S(1)}, u32[]{:S(2)}, u32[]{:S(2)}) %collective-permute-start.44) | collective-permute-done | bytes 16416 | tf_op jit(solution)/shard_map/ppermute | solution.py:23
  218.4 7.0 %collective-permute-done.22 = s16[32,2176]{1,0:T(8,128)(2,1)S(1)} collective-permute-done((s16[32,2176]{1,0:T(8,128)(2,1)S(1)}, s16[32,2176]{1,0:T(8,128)(2,1)S(1)}, u32[]{:S(2)}, u32[]{:S(2)}) %collective-permute-start.22) | collective-permute-done | bytes 139296 | tf_op jit(solution)/shard_map/ppermute | solution.py:23
  225.4 4.4 %collective-permute-done.23 = s16[32,2176]{1,0:T(8,128)(2,1)S(1)} collective-permute-done((s16[32,2176]{1,0:T(8,128)(2,1)S(1)}, s16[32,2176]{1,0:T(8,128)(2,1)S(1)}, u32[]{:S(2)}, u32[]{:S(2)}) %collective-permute-start.23) | collective-permute-done | bytes 139296 | tf_op jit(solution)/shard_map/ppermute | solution.py:23
  235.6 10.3 %backward_local.2 = (bf16[256,2048]{1,0:T(8,128)(2,1)}, f32[7,16,64]{2,1,0:T(8,128)}, f32[4,8,128]{2,1,0:T(8,128)}, f32[8,128]{1,0:T(8,128)}) custom-call(s32[2]{0:T(128)} %pad_add_fusion.place_ref, s16[128,2176]{1,0:T(8,128)(2,1)} %copy-done.7, s16[128,2176]{1,0:T(8,128)(2,1)} %copy-done.10, ...), custom_call_target="tpu_custom_call", output_to_operand_aliasing={{0}: (12, {})} | custom-call | flops 23068672 | bytes 13631488 | tf_op jit(solution)/shard_map/backward_local/pallas_call | solution.py:519
  246.7 10.3 %backward_local.3 = (bf16[256,2048]{1,0:T(8,128)(2,1)}, f32[7,16,64]{2,1,0:T(8,128)}, f32[4,8,128]{2,1,0:T(8,128)}, f32[8,128]{1,0:T(8,128)}) custom-call(s32[2]{0:T(128)} %pad_add_fusion.place_ref, s16[128,2176]{1,0:T(8,128)(2,1)} %copy-done.8, s16[128,2176]{1,0:T(8,128)(2,1)} %copy-done.9, ...), custom_call_target="tpu_custom_call", output_to_operand_aliasing={{0}: (12, {})} | custom-call | flops 23068672 | bytes 13631488 | tf_op jit(solution)/shard_map/backward_local/pallas_call | solution.py:519
  263.6 2.9 %collective-permute-done.48 = f32[14,1024]{1,0:T(8,128)S(1)} collective-permute-done((f32[14,1024]{1,0:T(8,128)S(1)}, f32[14,1024]{1,0:T(8,128)S(1)}, u32[]{:S(2)}, u32[]{:S(2)}) %collective-permute-start.48) | collective-permute-done | bytes 57376 | tf_op jit(solution)/shard_map/ppermute | solution.py:23
  (282 shorter events, 63.4 us)
Async XLA Ops:
  2.6 51.9 %collective-permute-start.26 = (bf16[128,1280]{1,0:T(8,128)(2,1)S(1)}, bf16[128,1280]{1,0:T(8,128)(2,1)S(1)}, u32[]{:S(2)}, u32[]{:S(2)}) collective-permute-start(bf16[128,1280]{1,0:T(8,128)(2,1)S(1)} %get-tuple-element.96), channel_id=1, source_target_pairs={{0,4},{1,5},{2,6},{3,7},{4,0},{5,1},{6,2},{7,3},{8,12},{9,13},{10,... | collective-permute-start | bytes 983048 | tf_op jit(solution)/shard_map/ppermute | solution.py:23
  5.2 52.0 %collective-permute-start.25 = (bf16[128,1280]{1,0:T(8,128)(2,1)S(1)}, bf16[128,1280]{1,0:T(8,128)(2,1)S(1)}, u32[]{:S(2)}, u32[]{:S(2)}) collective-permute-start(bf16[128,1280]{1,0:T(8,128)(2,1)S(1)} %get-tuple-element.96), channel_id=1, source_target_pairs={{0,2},{1,3},{2,0},{3,1},{4,6},{5,7},{6,4},{7,5},{8,10},{9,11},{10,... | collective-permute-start | bytes 983048 | tf_op jit(solution)/shard_map/ppermute | solution.py:23
  5.6 51.5 %collective-permute-start.27 = (bf16[128,1280]{1,0:T(8,128)(2,1)S(1)}, bf16[128,1280]{1,0:T(8,128)(2,1)S(1)}, u32[]{:S(2)}, u32[]{:S(2)}) collective-permute-start(bf16[128,1280]{1,0:T(8,128)(2,1)S(1)} %get-tuple-element.96), channel_id=1, source_target_pairs={{0,6},{1,7},{2,4},{3,5},{4,2},{5,3},{6,0},{7,1},{8,14},{9,15},{10,... | collective-permute-start | bytes 983048 | tf_op jit(solution)/shard_map/ppermute | solution.py:23
  6.4 25.5 %collective-permute-start.15 = (f32[1,2,3,1024]{3,2,1,0:T(4,128)S(1)}, f32[1,2,3,1024]{3,2,1,0:T(4,128)S(1)}, u32[]{:S(2)}, u32[]{:S(2)}) collective-permute-start(f32[1,2,3,1024]{3,2,1,0:T(4,128)S(1)} %maximum_bitcast_fusion.1), channel_id=1, source_target_pairs={{0,1},{1,0},{2,3},{3,2},{4,5},{5,4},{6,7},{7,6},{8,9},{9,8},{10,11... | collective-permute-start | bytes 73736 | tf_op jit(solution)/shard_map/ppermute | solution.py:23
  6.4 53.5 %collective-permute-start.1 = (bf16[128,1280]{1,0:T(8,128)(2,1)}, bf16[128,1280]{1,0:T(8,128)(2,1)S(1)}, u32[]{:S(2)}, u32[]{:S(2)}) collective-permute-start(bf16[128,1280]{1,0:T(8,128)(2,1)} %get-tuple-element.97), channel_id=1, source_target_pairs={{0,4},{1,5},{2,6},{3,7},{4,0},{5,1},{6,2},{7,3},{8,12},{9,13},{10,... | collective-permute-start | bytes 983048 | tf_op jit(solution)/shard_map/ppermute | solution.py:23
  36.3 16.4 %collective-permute-start.20 = (f32[4,2,3,1024]{3,2,1,0:T(4,128)S(1)}, f32[4,2,3,1024]{3,2,1,0:T(4,128)S(1)}, u32[]{:S(2)}, u32[]{:S(2)}) collective-permute-start(f32[4,2,3,1024]{3,2,1,0:T(4,128)S(1)} %pad_maximum_fusion.2), channel_id=1, source_target_pairs={{0,4},{1,5},{2,6},{3,7},{4,0},{5,1},{6,2},{7,3},{8,12},{9,13},{10,... | collective-permute-start | bytes 294920 | tf_op jit(solution)/shard_map/ppermute | solution.py:23
  54.5 17.5 %collective-permute-start.2 = (bf16[128,1280]{1,0:T(8,128)(2,1)}, bf16[128,1280]{1,0:T(8,128)(2,1)S(1)}, u32[]{:S(2)}, u32[]{:S(2)}) collective-permute-start(bf16[128,1280]{1,0:T(8,128)(2,1)} %get-tuple-element.97), channel_id=1, source_target_pairs={{0,6},{1,7},{2,4},{3,5},{4,2},{5,3},{6,0},{7,1},{8,14},{9,15},{10,... | collective-permute-start | bytes 983048 | tf_op jit(solution)/shard_map/ppermute | solution.py:23
  57.2 61.8 %collective-permute-start.14 = (s16[256,2176]{1,0:T(8,128)(2,1)}, s16[256,2176]{1,0:T(8,128)(2,1)}, u32[]{:S(2)}, u32[]{:S(2)}) collective-permute-start(s16[256,2176]{1,0:T(8,128)(2,1)} %get-tuple-element.51), channel_id=1, source_target_pairs={{0,1},{1,0},{2,3},{3,2},{4,5},{5,4},{6,7},{7,6},{8,9},{9,8},{10,11... | collective-permute-start | bytes 3342344 | tf_op jit(solution)/shard_map/ppermute | solution.py:23
  57.5 20.8 %collective-permute-start.31 = (bf16[128,1280]{1,0:T(8,128)(2,1)S(1)}, bf16[128,1280]{1,0:T(8,128)(2,1)S(1)}, u32[]{:S(2)}, u32[]{:S(2)}) collective-permute-start(bf16[128,1280]{1,0:T(8,128)(2,1)S(1)} %get-tuple-element.86), channel_id=1, source_target_pairs={{0,24},{8,16},{16,8},{24,0},{1,25},{9,17},{17,9},{25,1},{2,26},{10... | collective-permute-start | bytes 983048 | tf_op jit(solution)/shard_map/ppermute | solution.py:23
  60.0 16.7 %collective-permute-start.30 = (bf16[128,1280]{1,0:T(8,128)(2,1)S(1)}, bf16[128,1280]{1,0:T(8,128)(2,1)S(1)}, u32[]{:S(2)}, u32[]{:S(2)}) collective-permute-start(bf16[128,1280]{1,0:T(8,128)(2,1)S(1)} %get-tuple-element.87), channel_id=1, source_target_pairs={{0,16},{8,24},{16,0},{24,8},{1,17},{9,25},{17,1},{25,9},{2,18},{10... | collective-permute-start | bytes 983048 | tf_op jit(solution)/shard_map/ppermute | solution.py:23
  72.3 17.5 %collective-permute-start.6 = (bf16[128,1280]{1,0:T(8,128)(2,1)S(1)}, bf16[128,1280]{1,0:T(8,128)(2,1)S(1)}, u32[]{:S(2)}, u32[]{:S(2)}) collective-permute-start(bf16[128,1280]{1,0:T(8,128)(2,1)S(1)} %get-tuple-element.90), channel_id=1, source_target_pairs={{0,24},{8,16},{16,8},{24,0},{1,25},{9,17},{17,9},{25,1},{2,26},{10... | collective-permute-start | bytes 983048 | tf_op jit(solution)/shard_map/ppermute | solution.py:23
  89.9 16.7 %collective-permute-start.7 = (bf16[384,1280]{1,0:T(8,128)(2,1)S(1)}, bf16[384,1280]{1,0:T(8,128)(2,1)}, u32[]{:S(2)}, u32[]{:S(2)}) collective-permute-start(bf16[384,1280]{1,0:T(8,128)(2,1)S(1)} %constant_dynamic-update-slice_fusion.refs_0_), channel_id=1, source_target_pairs={{0,1},{1,0},{2,3},{3,2},{4,5},{5,4},{6,7},{7,6},{8,9},{9,8},{10,11... | collective-permute-start | bytes 2949128 | tf_op jit(solution)/shard_map/ppermute | solution.py:23
  102.3 18.1 %collective-permute-start.33 = (bf16[128,2048]{1,0:T(8,128)(2,1)}, bf16[128,2048]{1,0:T(8,128)(2,1)S(1)}, u32[]{:S(2)}, u32[]{:S(2)}) collective-permute-start(bf16[128,2048]{1,0:T(8,128)(2,1)} %get-tuple-element.61), channel_id=1, source_target_pairs={{0,8},{8,0},{16,24},{24,16},{1,9},{9,1},{17,25},{25,17},{2,10},{10... | collective-permute-start | bytes 1572872 | tf_op jit(solution)/shard_map/ppermute | solution.py:23
  103.9 17.9 %collective-permute-start.34 = (bf16[128,2048]{1,0:T(8,128)(2,1)}, bf16[128,2048]{1,0:T(8,128)(2,1)S(1)}, u32[]{:S(2)}, u32[]{:S(2)}) collective-permute-start(bf16[128,2048]{1,0:T(8,128)(2,1)} %get-tuple-element.62), channel_id=1, source_target_pairs={{0,16},{8,24},{16,0},{24,8},{1,17},{9,25},{17,1},{25,9},{2,18},{10... | collective-permute-start | bytes 1572872 | tf_op jit(solution)/shard_map/ppermute | solution.py:23
  106.6 36.0 %collective-permute-start.3 = (bf16[128,1280]{1,0:T(8,128)(2,1)S(1)}, bf16[128,1280]{1,0:T(8,128)(2,1)}, u32[]{:S(2)}, u32[]{:S(2)}) collective-permute-start(bf16[128,1280]{1,0:T(8,128)(2,1)S(1)} %get-tuple-element.93.refs_0_), channel_id=1, source_target_pairs={{0,1},{1,0},{2,3},{3,2},{4,5},{5,4},{6,7},{7,6},{8,9},{9,8},{10,11... | collective-permute-start | bytes 983048 | tf_op jit(solution)/shard_map/ppermute | solution.py:23
  118.2 19.8 %collective-permute-start.35 = (bf16[128,2048]{1,0:T(8,128)(2,1)}, bf16[128,2048]{1,0:T(8,128)(2,1)}, u32[]{:S(2)}, u32[]{:S(2)}) collective-permute-start(bf16[128,2048]{1,0:T(8,128)(2,1)} %get-tuple-element.63), channel_id=1, source_target_pairs={{0,24},{8,16},{16,8},{24,0},{1,25},{9,17},{17,9},{25,1},{2,26},{10... | collective-permute-start | bytes 1572872 | tf_op jit(solution)/shard_map/ppermute | solution.py:23
  118.9 26.9 %collective-permute-start.8 = (bf16[128,2048]{1,0:T(8,128)(2,1)}, bf16[128,2048]{1,0:T(8,128)(2,1)S(1)}, u32[]{:S(2)}, u32[]{:S(2)}) collective-permute-start(bf16[128,2048]{1,0:T(8,128)(2,1)} %get-tuple-element.43), channel_id=1, source_target_pairs={{0,8},{8,0},{16,24},{24,16},{1,9},{9,1},{17,25},{25,17},{2,10},{10... | collective-permute-start | bytes 1572872 | tf_op jit(solution)/shard_map/ppermute | solution.py:23
  120.4 26.9 %collective-permute-start.9 = (bf16[128,2048]{1,0:T(8,128)(2,1)}, bf16[128,2048]{1,0:T(8,128)(2,1)S(1)}, u32[]{:S(2)}, u32[]{:S(2)}) collective-permute-start(bf16[128,2048]{1,0:T(8,128)(2,1)} %get-tuple-element.44), channel_id=1, source_target_pairs={{0,16},{8,24},{16,0},{24,8},{1,17},{9,25},{17,1},{25,9},{2,18},{10... | collective-permute-start | bytes 1572872 | tf_op jit(solution)/shard_map/ppermute | solution.py:23
  121.8 38.1 %collective-permute-start.10 = (bf16[128,2048]{1,0:T(8,128)(2,1)}, bf16[128,2048]{1,0:T(8,128)(2,1)}, u32[]{:S(2)}, u32[]{:S(2)}) collective-permute-start(bf16[128,2048]{1,0:T(8,128)(2,1)} %get-tuple-element.45), channel_id=1, source_target_pairs={{0,24},{8,16},{16,8},{24,0},{1,25},{9,17},{17,9},{25,1},{2,26},{10... | collective-permute-start | bytes 1572872 | tf_op jit(solution)/shard_map/ppermute | solution.py:23
  138.1 25.9 %collective-permute-start.16 = (s16[64,2176]{1,0:T(8,128)(2,1)}, s16[64,2176]{1,0:T(8,128)(2,1)S(1)}, u32[]{:S(2)}, u32[]{:S(2)}) collective-permute-start(s16[64,2176]{1,0:T(8,128)(2,1)} %get-tuple-element.53), channel_id=1, source_target_pairs={{0,2},{1,3},{2,0},{3,1},{4,6},{5,7},{6,4},{7,5},{8,10},{9,11},{10,... | collective-permute-start | bytes 835592 | tf_op jit(solution)/shard_map/ppermute | solution.py:23
  142.6 24.9 %collective-permute-start.17 = (s16[64,2176]{1,0:T(8,128)(2,1)S(1)}, s16[64,2176]{1,0:T(8,128)(2,1)S(1)}, u32[]{:S(2)}, u32[]{:S(2)}) collective-permute-start(s16[64,2176]{1,0:T(8,128)(2,1)S(1)} %copy-done.28), channel_id=1, source_target_pairs={{0,4},{1,5},{2,6},{3,7},{4,0},{5,1},{6,2},{7,3},{8,12},{9,13},{10,... | collective-permute-start | bytes 835592 | tf_op jit(solution)/shard_map/ppermute | solution.py:23
  145.8 30.5 %collective-permute-start.18 = (s16[64,2176]{1,0:T(8,128)(2,1)S(1)}, s16[64,2176]{1,0:T(8,128)(2,1)S(1)}, u32[]{:S(2)}, u32[]{:S(2)}) collective-permute-start(s16[64,2176]{1,0:T(8,128)(2,1)S(1)} %copy-done.27), channel_id=1, source_target_pairs={{0,6},{1,7},{2,4},{3,5},{4,2},{5,3},{6,0},{7,1},{8,14},{9,15},{10,... | collective-permute-start | bytes 835592 | tf_op jit(solution)/shard_map/ppermute | solution.py:23
  147.3 29.0 %collective-permute-start.36 = (s16[32,2176]{1,0:T(8,128)(2,1)}, s16[32,2176]{1,0:T(8,128)(2,1)S(1)}, u32[]{:S(2)}, u32[]{:S(2)}) collective-permute-start(s16[32,2176]{1,0:T(8,128)(2,1)} %get-tuple-element.65), channel_id=1, source_target_pairs={{0,2},{1,3},{2,0},{3,1},{4,6},{5,7},{6,4},{7,5},{8,10},{9,11},{10,... | collective-permute-start | bytes 417800 | tf_op jit(solution)/shard_map/ppermute | solution.py:23
  160.0 18.1 %collective-permute-start.37 = (s16[32,2176]{1,0:T(8,128)(2,1)S(1)}, s16[32,2176]{1,0:T(8,128)(2,1)S(1)}, u32[]{:S(2)}, u32[]{:S(2)}) collective-permute-start(s16[32,2176]{1,0:T(8,128)(2,1)S(1)} %copy-done.35), channel_id=1, source_target_pairs={{0,4},{1,5},{2,6},{3,7},{4,0},{5,1},{6,2},{7,3},{8,12},{9,13},{10,... | collective-permute-start | bytes 417800 | tf_op jit(solution)/shard_map/ppermute | solution.py:23
  164.0 24.2 %collective-permute-start.38 = (s16[32,2176]{1,0:T(8,128)(2,1)S(1)}, s16[32,2176]{1,0:T(8,128)(2,1)S(1)}, u32[]{:S(2)}, u32[]{:S(2)}) collective-permute-start(s16[32,2176]{1,0:T(8,128)(2,1)S(1)} %copy-done.34), channel_id=1, source_target_pairs={{0,6},{1,7},{2,4},{3,5},{4,2},{5,3},{6,0},{7,1},{8,14},{9,15},{10,... | collective-permute-start | bytes 417800 | tf_op jit(solution)/shard_map/ppermute | solution.py:23
  167.4 24.4 %collective-permute-start.11 = (s16[32,2176]{1,0:T(8,128)(2,1)}, s16[32,2176]{1,0:T(8,128)(2,1)S(1)}, u32[]{:S(2)}, u32[]{:S(2)}) collective-permute-start(s16[32,2176]{1,0:T(8,128)(2,1)} %get-tuple-element.47), channel_id=1, source_target_pairs={{0,2},{1,3},{2,0},{3,1},{4,6},{5,7},{6,4},{7,5},{8,10},{9,11},{10,... | collective-permute-start | bytes 417800 | tf_op jit(solution)/shard_map/ppermute | solution.py:23
  176.2 15.6 %collective-permute-start.12 = (s16[32,2176]{1,0:T(8,128)(2,1)}, s16[32,2176]{1,0:T(8,128)(2,1)S(1)}, u32[]{:S(2)}, u32[]{:S(2)}) collective-permute-start(s16[32,2176]{1,0:T(8,128)(2,1)} %get-tuple-element.48), channel_id=1, source_target_pairs={{0,4},{1,5},{2,6},{3,7},{4,0},{5,1},{6,2},{7,3},{8,12},{9,13},{10,... | collective-permute-start | bytes 417800 | tf_op jit(solution)/shard_map/ppermute | solution.py:23
  176.3 16.3 %collective-permute-start.13 = (s16[32,2176]{1,0:T(8,128)(2,1)}, s16[32,2176]{1,0:T(8,128)(2,1)S(1)}, u32[]{:S(2)}, u32[]{:S(2)}) collective-permute-start(s16[32,2176]{1,0:T(8,128)(2,1)} %get-tuple-element.49), channel_id=1, source_target_pairs={{0,6},{1,7},{2,4},{3,5},{4,2},{5,3},{6,0},{7,1},{8,14},{9,15},{10,... | collective-permute-start | bytes 417800 | tf_op jit(solution)/shard_map/ppermute | solution.py:23
  199.4 30.4 %collective-permute-start.39 = (s16[32,2176]{1,0:T(8,128)(2,1)S(1)}, s16[32,2176]{1,0:T(8,128)(2,1)S(1)}, u32[]{:S(2)}, u32[]{:S(2)}) collective-permute-start(s16[32,2176]{1,0:T(8,128)(2,1)S(1)} %copy-done.31), channel_id=1, source_target_pairs={{0,2},{1,3},{2,0},{3,1},{4,6},{5,7},{6,4},{7,5},{8,10},{9,11},{10,... | collective-permute-start | bytes 417800 | tf_op jit(solution)/shard_map/ppermute | solution.py:23
  202.5 27.4 %collective-permute-start.40 = (s16[32,2176]{1,0:T(8,128)(2,1)S(1)}, s16[32,2176]{1,0:T(8,128)(2,1)S(1)}, u32[]{:S(2)}, u32[]{:S(2)}) collective-permute-start(s16[32,2176]{1,0:T(8,128)(2,1)S(1)} %copy-done.30), channel_id=1, source_target_pairs={{0,4},{1,5},{2,6},{3,7},{4,0},{5,1},{6,2},{7,3},{8,12},{9,13},{10,... | collective-permute-start | bytes 417800 | tf_op jit(solution)/shard_map/ppermute | solution.py:23
  202.6 27.3 %collective-permute-start.41 = (s16[32,2176]{1,0:T(8,128)(2,1)S(1)}, s16[32,2176]{1,0:T(8,128)(2,1)S(1)}, u32[]{:S(2)}, u32[]{:S(2)}) collective-permute-start(s16[32,2176]{1,0:T(8,128)(2,1)S(1)} %copy-done.29), channel_id=1, source_target_pairs={{0,6},{1,7},{2,4},{3,5},{4,2},{5,3},{6,0},{7,1},{8,14},{9,15},{10,... | collective-permute-start | bytes 417800 | tf_op jit(solution)/shard_map/ppermute | solution.py:23
  229.8 16.1 %collective-permute-start.24 = (s16[128,2176]{1,0:T(8,128)(2,1)S(1)}, s16[128,2176]{1,0:T(8,128)(2,1)S(1)}, u32[]{:S(2)}, u32[]{:S(2)}) collective-permute-start(s16[128,2176]{1,0:T(8,128)(2,1)S(1)} %constant_dynamic-update-slice_fusion.10.grad_ref), channel_id=1, source_target_pairs={{0,1},{1,0},{2,3},{3,2},{4,5},{5,4},{6,7},{7,6},{8,9},{9,8},{10,11... | collective-permute-start | bytes 1671176 | tf_op jit(solution)/shard_map/ppermute | solution.py:23
  (53 other events, 557.9 us)
where the time goes:
time: 269 us; the launch traced here: 267 us
  Pallas kernels  96 us (36%)
  waiting for transfers between devices  86.6 us (32%)
  starting transfers between devices  56.7 us (21%)
  local copies, waits for them, and re-layouts  18.3 us (7%)
  other arithmetic  7.44 us (3%)
    ppermute x49, waiting for transfers between devices, swap(): return lax.ppermute(value, axis, pairs)  86.6 us
    ppermute x49, starting transfers between devices, swap(): return lax.ppermute(value, axis, pairs)  56.7 us
    pallas_call x4, Pallas kernels, product(): pl.pallas_call(functools.partial(product_kernel, ways), grid_spec=pltpu.P...  42.7 us
    pallas_call x2, Pallas kernels, backward_local(): pl.pallas_call(functools.partial(backward_kernel, local), grid_spec=pltpu...  20.5 us
    pallas_call x1, Pallas kernels, forward_local(): pl.pallas_call(functools.partial(forward_kernel, local), grid=(rows // bl...  14.4 us
    pallas_call x2, Pallas kernels, gather_parts(): pl.pallas_call(functools.partial(gather_kernel, count), grid_spec=pltpu.P...  6.91 us
    pallas_call x2, Pallas kernels, cross_sections(): pl.pallas_call(functools.partial(cross_kernel, count, bits), grid=(rows /...  6.01 us
    pallas_call x1, Pallas kernels, core_forward(): pl.pallas_call(core_kernel, grid_spec=pltpu.PrefetchScalarGridSpec(num_sc...  5.48 us
  transfers between devices with their start and end apart: 49, of which 16 were waited for; matrix products, arithmetic and copies ran while one was open for 6% of the time, Pallas kernels for 31%

commit v1 on v0

--- a/solution.py
+++ b/solution.py
@@ -124,7 +124,7 @@
     ways = len(tokens)
     width = codes.shape[0]
     rows, part = tokens[0].shape
-    block = min(width, 256)
+    block = min(width, 512)
     code_spec = lambda j: pl.BlockSpec((block, part), lambda i, p: (i, p[0] ^ j))
     scale_spec = lambda j: pl.BlockSpec((1, 1, part), lambda i, p: (p[1] + (p[0] ^ j), 0, 0))
     return pl.pallas_call(
@@ -559,16 +559,12 @@
     return parts[0]
 
 
-def gather_shares(value, me, bits):
-    for bit in range(bits):
-        other = swap(value, "tensor", 1 << bit)
-        first = ((me >> bit) & 1) == 0
-        value = jnp.concatenate(
-            [jnp.where(first, value, other), jnp.where(first, other, value)], axis=0
-        )
-        if bit == 0:
-            pair = value
-    return value, pair
+def gather_shares(value, line, core, count):
+    near = jnp.stack([value] + [swap(value, "tensor", 2 * m) for m in range(1, count)])
+    near = jnp.take(near, line ^ jnp.arange(count, dtype=jnp.int32), axis=0)
+    other = swap(near, "tensor", 1)
+    first = core == 0
+    return jnp.stack([jnp.where(first, near, other), jnp.where(first, other, near)], axis=1)
 
 
 def scatter_shares(value, me, bits):
@@ -608,9 +604,10 @@
             [swap(pick(blocks, level ^ mine ^ m), "dp", m) for m in range(1, groups)],
             axis=0,
         )
-        close = pick(blocks, level ^ mine)
+        near.append(pick(blocks, level ^ mine))
         remote.append([arrived] + [swap(arrived, "tensor", m) for m in range(1, ways)])
-        near.append([close] + [swap(close, "tensor", m) for m in range(1, ways)])
+    near = jnp.concatenate(near, axis=0)
+    near = [near] + [swap(near, "tensor", m) for m in range(1, ways)]
 
     scale = jnp.exp2(exponents.astype(jnp.float32)).astype(jnp.bfloat16)
     scale = scale.reshape(-1, 1, part)
@@ -621,12 +618,13 @@
     cos_table, sin_table = local_tables(cosine[:local], sine[:local], width)
     states, last_codes = forward_local(activations, cos_table, sin_table)
 
-    trig = jnp.stack([cosine[local:], sine[local:]])[None]
-    trig, first_trig = gather_shares(trig, me, cross)
+    trig = jnp.stack([cosine[local:], sine[local:]])
+    trig = gather_shares(trig, line, core, count)
+    trig = jnp.moveaxis(trig.reshape(devices, 2, cross, share), 0, 2)
+    trig = trig.reshape(2, cross, devices // 2, width)
     flip = (1 - 2 * core).astype(jnp.float32)
-    core_trig = jnp.moveaxis(first_trig[:, :, 0], 0, 1).reshape(2, width)
+    core_trig = lax.dynamic_index_in_dim(trig[:, 0], line, 1, keepdims=False)
     core_trig = core_trig * jnp.stack([jnp.float32(1), -flip])[:, None]
-    trig = jnp.moveaxis(trig, 0, 2).reshape(2, cross, devices // 2, width)
     jj = jnp.arange(count // 2, dtype=jnp.int32)
     cross_cos, cross_sin, flips = [], [], []
     for bit in range(cross - 1):
@@ -653,10 +651,10 @@
     cross_terms = []
     backs = []
     word_rows = chunk_rows // 16
+    kept = product(column_place, near, codes, scale, chunks, jnp.float32)
     for q in range(chunks):
         sent = product(column_place, remote[q], codes, scale, groups - 1, jnp.bfloat16)
-        kept = product(column_place, near[q], codes, scale, 1, jnp.float32)
-        parts = list(kept) + [swap(sent[m - 1], "dp", m) for m in range(1, groups)]
+        parts = [kept[q]] + [swap(sent[m - 1], "dp", m) for m in range(1, groups)]
         words = clip_bits[q * word_rows : (q + 1) * word_rows]
         grads = gather_parts(place, parts, words, count)
         grads = [grads[0]] + [swap(grads[m], "tensor", 2 * m) for m in range(1, count)]

time: 269 us -> 270 us (level)
  Pallas kernels: 96 us -> 80.4 us
  waiting for transfers between devices: 86.6 us -> 100 us
    pallas_call x4 -> x3, Pallas kernels: 42.7 us -> 27 us  [product(): pl.pallas_call(functools.partial(product_kernel, ways), grid_spec=pltpu.P...]
    ppermute x49, waiting for transfers between devices: 86.6 us -> 100 us  [swap(): return lax.ppermute(value, axis, pairs)]
  transfers between devices with their start and end apart: 49 -> 49, of which waited for: 16 -> 15; matrix products, arithmetic and copies ran while one was open for 6% -> 7% of each run, Pallas kernels for 31% -> 25%
where the time goes in v1:
time: 270 us; the launch traced here: 268 us
  waiting for transfers between devices  100 us (37%)
  Pallas kernels  80.4 us (30%)
  starting transfers between devices  57.3 us (21%)
  local copies, waits for them, and re-layouts  19.9 us (7%)
  other arithmetic  7.7 us (3%)
    ppermute x49, waiting for transfers between devices, swap(): return lax.ppermute(value, axis, pairs)  100 us
    ppermute x49, starting transfers between devices, swap(): return lax.ppermute(value, axis, pairs)  57.3 us
    pallas_call x3, Pallas kernels, product(): pl.pallas_call(functools.partial(product_kernel, ways), grid_spec=pltpu.P...  27 us
    pallas_call x2, Pallas kernels, backward_local(): pl.pallas_call(functools.partial(backward_kernel, local), grid_spec=pltpu...  20.7 us
    pallas_call x1, Pallas kernels, forward_local(): pl.pallas_call(functools.partial(forward_kernel, local), grid=(rows // bl...  14.5 us
    pallas_call x2, Pallas kernels, gather_parts(): pl.pallas_call(functools.partial(gather_kernel, count), grid_spec=pltpu.P...  6.76 us
    pallas_call x2, Pallas kernels, cross_sections(): pl.pallas_call(functools.partial(cross_kernel, count, bits), grid=(rows /...  6 us
    pallas_call x1, Pallas kernels, core_forward(): pl.pallas_call(core_kernel, grid_spec=pltpu.PrefetchScalarGridSpec(num_sc...  5.48 us
  transfers between devices with their start and end apart: 49, of which 15 were waited for; matrix products, arithmetic and copies ran while one was open for 7% of the time, Pallas kernels for 25%

profile of v1, /device:TPU:8, one launch (start us, length us, event | category | flops | bytes accessed | tf_op | source)
XLA Modules:
  0.0 267.9 jit_solution(13332510585085901849)
XLA Ops:
  1.8 2.7 collective-permute-start.19
  7.2 3.5 %collective-permute-start.4 = (bf16[128,1280]{1,0:T(8,128)(2,1)S(1)}, bf16[128,1280]{1,0:T(8,128)(2,1)S(1)}, u32[]{:S(2)}, u32[]{:S(2)}) collective-permute-start(bf16[128,1280]{1,0:T(8,128)(2,1)S(1)} %get-tuple-element.100), channel_id=1, source_target_pairs={{0,4},{1,5},{2,6},{3,7},{4,0},{5,1},{6,2},{7,3},{8,12},{9,13},{10,... | collective-permute-start | bytes 983048 | tf_op jit(solution)/shard_map/ppermute | solution.py:23
  17.7 14.5 %forward_local.1 = (f32[11,256,2048]{2,1,0:T(8,128)}, s16[256,2176]{1,0:T(8,128)(2,1)}) custom-call(bf16[256,2048]{1,0:T(8,128)(2,1)} %act_ref.1, f32[11,2048]{1,0:T(8,128)} %concatenate.82.cos_ref, f32[11,2048]{1,0:T(8,128)} %concatenate.92.sin_ref), custom_call_target="tpu_custom_call" | custom-call | flops 34603008 | bytes 25165824 | tf_op jit(solution)/shard_map/forward_local/pallas_call | solution.py:193
  32.8 3.8 %collective-permute-start.1 = (bf16[128,1280]{1,0:T(8,128)(2,1)}, bf16[128,1280]{1,0:T(8,128)(2,1)S(1)}, u32[]{:S(2)}, u32[]{:S(2)}) collective-permute-start(bf16[128,1280]{1,0:T(8,128)(2,1)} %get-tuple-element.101), channel_id=1, source_target_pairs={{0,4},{1,5},{2,6},{3,7},{4,0},{5,1},{6,2},{7,3},{8,12},{9,13},{10,... | collective-permute-start | bytes 983048 | tf_op jit(solution)/shard_map/ppermute | solution.py:23
  42.4 16.9 %collective-permute-done.5 = bf16[128,1280]{1,0:T(8,128)(2,1)S(1)} collective-permute-done((bf16[128,1280]{1,0:T(8,128)(2,1)S(1)}, bf16[128,1280]{1,0:T(8,128)(2,1)S(1)}, u32[]{:S(2)}, u32[]{:S(2)}) %collective-permute-start.5) | collective-permute-done | bytes 327712 | tf_op jit(solution)/shard_map/ppermute | solution.py:23
  59.5 2.5 collective-permute-start.9
  62.0 5.8 %collective-permute-done.1 = bf16[128,1280]{1,0:T(8,128)(2,1)S(1)} collective-permute-done((bf16[128,1280]{1,0:T(8,128)(2,1)}, bf16[128,1280]{1,0:T(8,128)(2,1)S(1)}, u32[]{:S(2)}, u32[]{:S(2)}) %collective-permute-start.1) | collective-permute-done | bytes 327712 | tf_op jit(solution)/shard_map/ppermute | solution.py:23
  70.8 4.8 %collective-permute-done.2 = bf16[128,1280]{1,0:T(8,128)(2,1)S(1)} collective-permute-done((bf16[128,1280]{1,0:T(8,128)(2,1)}, bf16[128,1280]{1,0:T(8,128)(2,1)S(1)}, u32[]{:S(2)}, u32[]{:S(2)}) %collective-permute-start.2) | collective-permute-done | bytes 327712 | tf_op jit(solution)/shard_map/ppermute | solution.py:23
  75.9 2.5 collective-permute-start.31
  79.7 11.8 %collective-permute-done.29 = bf16[128,1280]{1,0:T(8,128)(2,1)S(1)} collective-permute-done((bf16[128,1280]{1,0:T(8,128)(2,1)S(1)}, bf16[128,1280]{1,0:T(8,128)(2,1)S(1)}, u32[]{:S(2)}, u32[]{:S(2)}) %collective-permute-start.29) | collective-permute-done | bytes 327712 | tf_op jit(solution)/shard_map/ppermute | solution.py:23
  92.5 9.4 %product.4 = (bf16[128,2048]{1,0:T(8,128)(2,1)}, bf16[128,2048]{1,0:T(8,128)(2,1)}, bf16[128,2048]{1,0:T(8,128)(2,1)}) custom-call(s32[2]{0:T(128)} %pad_add_fusion.1.place_ref, bf16[384,1280]{1,0:T(8,128)(2,1)} %copy-done.1, bf16[384,1280]{1,0:T(8,128)(2,1)} %collective-permute-done.10.refs_1_, bf16[2048,2560]{1,0:T(8,128)(2,1)} %refs_3_.5, ...), custom_call_target="tpu_custom_call" | custom-call | flops 4026531840 | bytes 10485760 | tf_op jit(solution)/shard_map/product/pallas_call | solution.py:130
  103.4 9.3 %product.5 = (bf16[128,2048]{1,0:T(8,128)(2,1)}, bf16[128,2048]{1,0:T(8,128)(2,1)}, bf16[128,2048]{1,0:T(8,128)(2,1)}) custom-call(s32[2]{0:T(128)} %pad_add_fusion.1.place_ref, bf16[384,1280]{1,0:T(8,128)(2,1)} %copy-done.2, bf16[384,1280]{1,0:T(8,128)(2,1)} %collective-permute-done.32.refs_1_, bf16[2048,2560]{1,0:T(8,128)(2,1)} %refs_3_.5, ...), custom_call_target="tpu_custom_call" | custom-call | flops 4026531840 | bytes 10485760 | tf_op jit(solution)/shard_map/product/pallas_call | solution.py:130
  119.2 5.5 %core_forward.1 = (f32[2,2,4,32,1024]{4,3,2,1,0:T(8,128)}, s16[64,2176]{1,0:T(8,128)(2,1)}, s16[64,2176]{1,0:T(8,128)(2,1)}, s16[64,2176]{1,0:T(8,128)(2,1)}, s16[64,2176]{1,0:T(8,128)(2,1)}) custom-call(s32[2]{0:T(128)} %pad_add_fusion.place_ref, f32[11,2,4,32,2048]{4,3,2,1,0:T(8,128)} %bitcast.152, s16[2,4,32,2176]{3,2,1,0:T(8,128)(2,1)} %bitcast.48.other_ref, ...), custom_call_target="tpu_custom_call" | custom-call | flops 5242880 | bytes 6291456 | tf_op jit(solution)/shard_map/core_forward/pallas_call | solution.py:256
  124.7 3.2 %collective-permute-done.33 = bf16[128,2048]{1,0:T(8,128)(2,1)S(1)} collective-permute-done((bf16[128,2048]{1,0:T(8,128)(2,1)}, bf16[128,2048]{1,0:T(8,128)(2,1)S(1)}, u32[]{:S(2)}, u32[]{:S(2)}) %collective-permute-start.33) | collective-permute-done | bytes 524320 | tf_op jit(solution)/shard_map/ppermute | solution.py:23
  127.9 2.4 collective-permute-start.22
  130.3 20.5 %collective-permute-done.34 = bf16[128,2048]{1,0:T(8,128)(2,1)} collective-permute-done((bf16[128,2048]{1,0:T(8,128)(2,1)}, bf16[128,2048]{1,0:T(8,128)(2,1)}, u32[]{:S(2)}, u32[]{:S(2)}) %collective-permute-start.34) | collective-permute-done | bytes 524320 | tf_op jit(solution)/shard_map/ppermute | solution.py:23
  150.9 2.5 collective-permute-start.23
  154.1 8.4 %product.3 = (f32[128,2048]{1,0:T(8,128)}, f32[128,2048]{1,0:T(8,128)}) custom-call(s32[2]{0:T(128)} %pad_add_fusion.1.place_ref, bf16[256,1280]{1,0:T(8,128)(2,1)} %copy-done, bf16[256,1280]{1,0:T(8,128)(2,1)} %copy-done.9, bf16[2048,2560]{1,0:T(8,128)(2,1)} %refs_3_.5, bf16[2048,2560]{1,0:T(8,128)(2,1)} %refs_3_.5, ...), custom_call_target="tpu_custom_call" | custom-call | flops 2684354560 | bytes 10485760 | tf_op jit(solution)/shard_map/product/pallas_call | solution.py:130
  162.5 3.3 %gather_parts.3 = (s16[32,2176]{1,0:T(8,128)(2,1)}, s16[32,2176]{1,0:T(8,128)(2,1)}, s16[32,2176]{1,0:T(8,128)(2,1)}, s16[32,2176]{1,0:T(8,128)(2,1)}) custom-call(s32[2]{0:T(128)} %pad_add_fusion.place_ref, f32[4,32,2048]{2,1,0:T(8,128)} %bitcast.156, bf16[4,32,2048]{2,1,0:T(8,128)(2,1)} %bitcast.160, bf16[4,32,2048]{2,1,0:T(8,128)(2,1)} %bitcast.75.refs_2_, ...), custom_call_target="tpu_custom_call" | custom-call | flops 3145728 | bytes 3145728 | tf_op jit(solution)/shard_map/gather_parts/pallas_call | solution.py:313
  167.6 3.4 %gather_parts.2 = (s16[32,2176]{1,0:T(8,128)(2,1)}, s16[32,2176]{1,0:T(8,128)(2,1)}, s16[32,2176]{1,0:T(8,128)(2,1)}, s16[32,2176]{1,0:T(8,128)(2,1)}) custom-call(s32[2]{0:T(128)} %pad_add_fusion.place_ref, f32[4,32,2048]{2,1,0:T(8,128)} %bitcast.155, bf16[4,32,2048]{2,1,0:T(8,128)(2,1)} %bitcast.158, bf16[4,32,2048]{2,1,0:T(8,128)(2,1)} %bitcast.159, ...), custom_call_target="tpu_custom_call" | custom-call | flops 3145728 | bytes 3145728 | tf_op jit(solution)/shard_map/gather_parts/pallas_call | solution.py:313
  174.6 2.6 collective-permute-start.37
  178.6 11.3 %collective-permute-done.37.refs_2_ = s16[32,2176]{1,0:T(8,128)(2,1)S(1)} collective-permute-done((s16[32,2176]{1,0:T(8,128)(2,1)S(1)}, s16[32,2176]{1,0:T(8,128)(2,1)S(1)}, u32[]{:S(2)}, u32[]{:S(2)}) %collective-permute-start.37) | collective-permute-done | bytes 139296 | tf_op jit(solution)/shard_map/ppermute | solution.py:23
  189.9 3.5 %collective-permute-done.38.refs_3_ = s16[32,2176]{1,0:T(8,128)(2,1)S(1)} collective-permute-done((s16[32,2176]{1,0:T(8,128)(2,1)S(1)}, s16[32,2176]{1,0:T(8,128)(2,1)S(1)}, u32[]{:S(2)}, u32[]{:S(2)}) %collective-permute-start.38) | collective-permute-done | bytes 139296 | tf_op jit(solution)/shard_map/ppermute | solution.py:23
  194.1 2.9 %cross_sections.3 = (s16[32,2176]{1,0:T(8,128)(2,1)}, s16[32,2176]{1,0:T(8,128)(2,1)}, s16[32,2176]{1,0:T(8,128)(2,1)}, s16[32,2176]{1,0:T(8,128)(2,1)}, f32[2,2,2048]{2,1,0:T(2,128)}) custom-call(s16[32,2176]{1,0:T(8,128)(2,1)} %get-tuple-element.68.refs_0_, s16[32,2176]{1,0:T(8,128)(2,1)} %copy-done.18, s16[32,2176]{1,0:T(8,128)(2,1)} %copy-done.21, ...), custom_call_target="tpu_custom_call" | custom-call | flops 10485760 | bytes 1572864 | tf_op jit(solution)/shard_map/cross_sections/pallas_call | solution.py:404
  197.8 3.1 %cross_sections.2 = (s16[32,2176]{1,0:T(8,128)(2,1)}, s16[32,2176]{1,0:T(8,128)(2,1)}, s16[32,2176]{1,0:T(8,128)(2,1)}, s16[32,2176]{1,0:T(8,128)(2,1)}, f32[2,2,2048]{2,1,0:T(2,128)}) custom-call(s16[32,2176]{1,0:T(8,128)(2,1)} %get-tuple-element.49.refs_0_, s16[32,2176]{1,0:T(8,128)(2,1)} %copy-done.17, s16[32,2176]{1,0:T(8,128)(2,1)} %copy-done.19, ...), custom_call_target="tpu_custom_call" | custom-call | flops 10485760 | bytes 1572864 | tf_op jit(solution)/shard_map/cross_sections/pallas_call | solution.py:404
  206.9 2.8 %collective-permute-start.25 = (s16[32,2176]{1,0:T(8,128)(2,1)}, s16[32,2176]{1,0:T(8,128)(2,1)S(1)}, u32[]{:S(2)}, u32[]{:S(2)}) collective-permute-start(s16[32,2176]{1,0:T(8,128)(2,1)} %get-tuple-element.60), channel_id=1, source_target_pairs={{0,2},{1,3},{2,0},{3,1},{4,6},{5,7},{6,4},{7,5},{8,10},{9,11},{10,... | collective-permute-start | bytes 417800 | tf_op jit(solution)/shard_map/ppermute | solution.py:23
  211.0 6.5 %collective-permute-done.44 = f32[2,2,1024]{2,1,0:T(2,128)S(1)} collective-permute-done((f32[2,2,1024]{2,1,0:T(2,128)S(1)}, f32[2,2,1024]{2,1,0:T(2,128)S(1)}, u32[]{:S(2)}, u32[]{:S(2)}) %collective-permute-start.44) | collective-permute-done | bytes 16416 | tf_op jit(solution)/shard_map/ppermute | solution.py:23
  220.0 7.5 %collective-permute-done.26 = s16[32,2176]{1,0:T(8,128)(2,1)S(1)} collective-permute-done((s16[32,2176]{1,0:T(8,128)(2,1)S(1)}, s16[32,2176]{1,0:T(8,128)(2,1)S(1)}, u32[]{:S(2)}, u32[]{:S(2)}) %collective-permute-start.26) | collective-permute-done | bytes 139296 | tf_op jit(solution)/shard_map/ppermute | solution.py:23
  227.5 2.6 collective-permute-done.27
  235.9 10.4 %backward_local.2 = (bf16[256,2048]{1,0:T(8,128)(2,1)}, f32[7,16,64]{2,1,0:T(8,128)}, f32[4,8,128]{2,1,0:T(8,128)}, f32[8,128]{1,0:T(8,128)}) custom-call(s32[2]{0:T(128)} %pad_add_fusion.place_ref, s16[128,2176]{1,0:T(8,128)(2,1)} %copy-done.6, s16[128,2176]{1,0:T(8,128)(2,1)} %copy-done.11, ...), custom_call_target="tpu_custom_call", output_to_operand_aliasing={{0}: (12, {})} | custom-call | flops 23068672 | bytes 13631488 | tf_op jit(solution)/shard_map/backward_local/pallas_call | solution.py:519
  247.2 10.3 %backward_local.3 = (bf16[256,2048]{1,0:T(8,128)(2,1)}, f32[7,16,64]{2,1,0:T(8,128)}, f32[4,8,128]{2,1,0:T(8,128)}, f32[8,128]{1,0:T(8,128)}) custom-call(s32[2]{0:T(128)} %pad_add_fusion.place_ref, s16[128,2176]{1,0:T(8,128)(2,1)} %copy-done.7, s16[128,2176]{1,0:T(8,128)(2,1)} %copy-done.10, ...), custom_call_target="tpu_custom_call", output_to_operand_aliasing={{0}: (12, {})} | custom-call | flops 23068672 | bytes 13631488 | tf_op jit(solution)/shard_map/backward_local/pallas_call | solution.py:519
  264.1 3.1 %collective-permute-done.48 = f32[14,1024]{1,0:T(8,128)S(1)} collective-permute-done((f32[14,1024]{1,0:T(8,128)S(1)}, f32[14,1024]{1,0:T(8,128)S(1)}, u32[]{:S(2)}, u32[]{:S(2)}) %collective-permute-start.48) | collective-permute-done | bytes 57376 | tf_op jit(solution)/shard_map/ppermute | solution.py:23
  (280 shorter events, 62.9 us)
Async XLA Ops:
  1.8 30.4 %collective-permute-start.19 = (f32[2,3,1024]{2,1,0:T(4,128)S(1)}, f32[2,3,1024]{2,1,0:T(4,128)S(1)}, u32[]{:S(2)}, u32[]{:S(2)}) collective-permute-start(f32[2,3,1024]{2,1,0:T(4,128)S(1)} %get-tuple-element.123), channel_id=1, source_target_pairs={{0,4},{1,5},{2,6},{3,7},{4,0},{5,1},{6,2},{7,3},{8,12},{9,13},{10,... | collective-permute-start | bytes 73736 | tf_op jit(solution)/shard_map/ppermute | solution.py:23
  4.4 28.3 %collective-permute-start.18 = (f32[2,3,1024]{2,1,0:T(4,128)S(1)}, f32[2,3,1024]{2,1,0:T(4,128)S(1)}, u32[]{:S(2)}, u32[]{:S(2)}) collective-permute-start(f32[2,3,1024]{2,1,0:T(4,128)S(1)} %get-tuple-element.123), channel_id=1, source_target_pairs={{0,2},{1,3},{2,0},{3,1},{4,6},{5,7},{6,4},{7,5},{8,10},{9,11},{10,... | collective-permute-start | bytes 73736 | tf_op jit(solution)/shard_map/ppermute | solution.py:23
  4.9 31.7 %collective-permute-start.20 = (f32[2,3,1024]{2,1,0:T(4,128)S(1)}, f32[2,3,1024]{2,1,0:T(4,128)S(1)}, u32[]{:S(2)}, u32[]{:S(2)}) collective-permute-start(f32[2,3,1024]{2,1,0:T(4,128)S(1)} %get-tuple-element.123), channel_id=1, source_target_pairs={{0,6},{1,7},{2,4},{3,5},{4,2},{5,3},{6,0},{7,1},{8,14},{9,15},{10,... | collective-permute-start | bytes 73736 | tf_op jit(solution)/shard_map/ppermute | solution.py:23
  7.2 34.5 %collective-permute-start.4 = (bf16[128,1280]{1,0:T(8,128)(2,1)S(1)}, bf16[128,1280]{1,0:T(8,128)(2,1)S(1)}, u32[]{:S(2)}, u32[]{:S(2)}) collective-permute-start(bf16[128,1280]{1,0:T(8,128)(2,1)S(1)} %get-tuple-element.100), channel_id=1, source_target_pairs={{0,4},{1,5},{2,6},{3,7},{4,0},{5,1},{6,2},{7,3},{8,12},{9,13},{10,... | collective-permute-start | bytes 983048 | tf_op jit(solution)/shard_map/ppermute | solution.py:23
  10.7 31.6 %collective-permute-start.3 = (bf16[128,1280]{1,0:T(8,128)(2,1)S(1)}, bf16[128,1280]{1,0:T(8,128)(2,1)S(1)}, u32[]{:S(2)}, u32[]{:S(2)}) collective-permute-start(bf16[128,1280]{1,0:T(8,128)(2,1)S(1)} %get-tuple-element.100), channel_id=1, source_target_pairs={{0,2},{1,3},{2,0},{3,1},{4,6},{5,7},{6,4},{7,5},{8,10},{9,11},{10,... | collective-permute-start | bytes 983048 | tf_op jit(solution)/shard_map/ppermute | solution.py:23
  32.2 27.1 %collective-permute-start.5 = (bf16[128,1280]{1,0:T(8,128)(2,1)S(1)}, bf16[128,1280]{1,0:T(8,128)(2,1)S(1)}, u32[]{:S(2)}, u32[]{:S(2)}) collective-permute-start(bf16[128,1280]{1,0:T(8,128)(2,1)S(1)} %get-tuple-element.100), channel_id=1, source_target_pairs={{0,6},{1,7},{2,4},{3,5},{4,2},{5,3},{6,0},{7,1},{8,14},{9,15},{10,... | collective-permute-start | bytes 983048 | tf_op jit(solution)/shard_map/ppermute | solution.py:23
  32.8 35.0 %collective-permute-start.1 = (bf16[128,1280]{1,0:T(8,128)(2,1)}, bf16[128,1280]{1,0:T(8,128)(2,1)S(1)}, u32[]{:S(2)}, u32[]{:S(2)}) collective-permute-start(bf16[128,1280]{1,0:T(8,128)(2,1)} %get-tuple-element.101), channel_id=1, source_target_pairs={{0,4},{1,5},{2,6},{3,7},{4,0},{5,1},{6,2},{7,3},{8,12},{9,13},{10,... | collective-permute-start | bytes 983048 | tf_op jit(solution)/shard_map/ppermute | solution.py:23
  38.8 30.6 %collective-permute-start = (bf16[128,1280]{1,0:T(8,128)(2,1)}, bf16[128,1280]{1,0:T(8,128)(2,1)S(1)}, u32[]{:S(2)}, u32[]{:S(2)}) collective-permute-start(bf16[128,1280]{1,0:T(8,128)(2,1)} %get-tuple-element.101), channel_id=1, source_target_pairs={{0,2},{1,3},{2,0},{3,1},{4,6},{5,7},{6,4},{7,5},{8,10},{9,11},{10,... | collective-permute-start | bytes 983048 | tf_op jit(solution)/shard_map/ppermute | solution.py:23
  41.7 33.9 %collective-permute-start.2 = (bf16[128,1280]{1,0:T(8,128)(2,1)}, bf16[128,1280]{1,0:T(8,128)(2,1)S(1)}, u32[]{:S(2)}, u32[]{:S(2)}) collective-permute-start(bf16[128,1280]{1,0:T(8,128)(2,1)} %get-tuple-element.101), channel_id=1, source_target_pairs={{0,6},{1,7},{2,4},{3,5},{4,2},{5,3},{6,0},{7,1},{8,14},{9,15},{10,... | collective-permute-start | bytes 983048 | tf_op jit(solution)/shard_map/ppermute | solution.py:23
  42.4 73.9 %collective-permute-start.17 = (s16[256,2176]{1,0:T(8,128)(2,1)}, s16[256,2176]{1,0:T(8,128)(2,1)}, u32[]{:S(2)}, u32[]{:S(2)}) collective-permute-start(s16[256,2176]{1,0:T(8,128)(2,1)} %get-tuple-element.54), channel_id=1, source_target_pairs={{0,1},{1,0},{2,3},{3,2},{4,5},{5,4},{6,7},{7,6},{8,9},{9,8},{10,11... | collective-permute-start | bytes 3342344 | tf_op jit(solution)/shard_map/ppermute | solution.py:23
  59.5 20.1 %collective-permute-start.9 = (bf16[128,1280]{1,0:T(8,128)(2,1)S(1)}, bf16[128,1280]{1,0:T(8,128)(2,1)S(1)}, u32[]{:S(2)}, u32[]{:S(2)}) collective-permute-start(bf16[128,1280]{1,0:T(8,128)(2,1)S(1)} %get-tuple-element.94), channel_id=1, source_target_pairs={{0,24},{8,16},{16,8},{24,0},{1,25},{9,17},{17,9},{25,1},{2,26},{10... | collective-permute-start | bytes 983048 | tf_op jit(solution)/shard_map/ppermute | solution.py:23
  75.9 15.7 %collective-permute-start.31 = (bf16[128,1280]{1,0:T(8,128)(2,1)S(1)}, bf16[128,1280]{1,0:T(8,128)(2,1)S(1)}, u32[]{:S(2)}, u32[]{:S(2)}) collective-permute-start(bf16[128,1280]{1,0:T(8,128)(2,1)S(1)} %get-tuple-element.90), channel_id=1, source_target_pairs={{0,24},{8,16},{16,8},{24,0},{1,25},{9,17},{17,9},{25,1},{2,26},{10... | collective-permute-start | bytes 983048 | tf_op jit(solution)/shard_map/ppermute | solution.py:23
  78.4 13.2 %collective-permute-start.30 = (bf16[128,1280]{1,0:T(8,128)(2,1)S(1)}, bf16[128,1280]{1,0:T(8,128)(2,1)S(1)}, u32[]{:S(2)}, u32[]{:S(2)}) collective-permute-start(bf16[128,1280]{1,0:T(8,128)(2,1)S(1)} %get-tuple-element.91), channel_id=1, source_target_pairs={{0,16},{8,24},{16,0},{24,8},{1,17},{9,25},{17,1},{25,9},{2,18},{10... | collective-permute-start | bytes 983048 | tf_op jit(solution)/shard_map/ppermute | solution.py:23
  91.9 22.7 %collective-permute-start.6 = (bf16[256,1280]{1,0:T(8,128)(2,1)S(1)}, bf16[256,1280]{1,0:T(8,128)(2,1)S(1)}, u32[]{:S(2)}, u32[]{:S(2)}) collective-permute-start(bf16[256,1280]{1,0:T(8,128)(2,1)S(1)} %pad_maximum_fusion.2.refs_0_), channel_id=1, source_target_pairs={{0,1},{1,0},{2,3},{3,2},{4,5},{5,4},{6,7},{7,6},{8,9},{9,8},{10,11... | collective-permute-start | bytes 1966088 | tf_op jit(solution)/shard_map/ppermute | solution.py:23
  101.9 15.2 %collective-permute-start.11 = (bf16[128,2048]{1,0:T(8,128)(2,1)}, bf16[128,2048]{1,0:T(8,128)(2,1)S(1)}, u32[]{:S(2)}, u32[]{:S(2)}) collective-permute-start(bf16[128,2048]{1,0:T(8,128)(2,1)} %get-tuple-element.46), channel_id=1, source_target_pairs={{0,8},{8,0},{16,24},{24,16},{1,9},{9,1},{17,25},{25,17},{2,10},{10... | collective-permute-start | bytes 1572872 | tf_op jit(solution)/shard_map/ppermute | solution.py:23
  112.7 15.2 %collective-permute-start.33 = (bf16[128,2048]{1,0:T(8,128)(2,1)}, bf16[128,2048]{1,0:T(8,128)(2,1)S(1)}, u32[]{:S(2)}, u32[]{:S(2)}) collective-permute-start(bf16[128,2048]{1,0:T(8,128)(2,1)} %get-tuple-element.65), channel_id=1, source_target_pairs={{0,8},{8,0},{16,24},{24,16},{1,9},{9,1},{17,25},{25,17},{2,10},{10... | collective-permute-start | bytes 1572872 | tf_op jit(solution)/shard_map/ppermute | solution.py:23
  113.3 37.6 %collective-permute-start.34 = (bf16[128,2048]{1,0:T(8,128)(2,1)}, bf16[128,2048]{1,0:T(8,128)(2,1)}, u32[]{:S(2)}, u32[]{:S(2)}) collective-permute-start(bf16[128,2048]{1,0:T(8,128)(2,1)} %get-tuple-element.66), channel_id=1, source_target_pairs={{0,16},{8,24},{16,0},{24,8},{1,17},{9,25},{17,1},{25,9},{2,18},{10... | collective-permute-start | bytes 1572872 | tf_op jit(solution)/shard_map/ppermute | solution.py:23
  114.7 38.7 %collective-permute-start.35 = (bf16[128,2048]{1,0:T(8,128)(2,1)}, bf16[128,2048]{1,0:T(8,128)(2,1)}, u32[]{:S(2)}, u32[]{:S(2)}) collective-permute-start(bf16[128,2048]{1,0:T(8,128)(2,1)} %get-tuple-element.67), channel_id=1, source_target_pairs={{0,24},{8,16},{16,8},{24,0},{1,25},{9,17},{17,9},{25,1},{2,26},{10... | collective-permute-start | bytes 1572872 | tf_op jit(solution)/shard_map/ppermute | solution.py:23
  116.3 49.5 %collective-permute-start.12 = (bf16[128,2048]{1,0:T(8,128)(2,1)}, bf16[128,2048]{1,0:T(8,128)(2,1)S(1)}, u32[]{:S(2)}, u32[]{:S(2)}) collective-permute-start(bf16[128,2048]{1,0:T(8,128)(2,1)} %get-tuple-element.47), channel_id=1, source_target_pairs={{0,16},{8,24},{16,0},{24,8},{1,17},{9,25},{17,1},{25,9},{2,18},{10... | collective-permute-start | bytes 1572872 | tf_op jit(solution)/shard_map/ppermute | solution.py:23
  117.0 50.6 %collective-permute-start.13 = (bf16[128,2048]{1,0:T(8,128)(2,1)}, bf16[128,2048]{1,0:T(8,128)(2,1)}, u32[]{:S(2)}, u32[]{:S(2)}) collective-permute-start(bf16[128,2048]{1,0:T(8,128)(2,1)} %get-tuple-element.48), channel_id=1, source_target_pairs={{0,24},{8,16},{16,8},{24,0},{1,25},{9,17},{17,9},{25,1},{2,26},{10... | collective-permute-start | bytes 1572872 | tf_op jit(solution)/shard_map/ppermute | solution.py:23
  127.9 44.1 %collective-permute-start.22 = (s16[64,2176]{1,0:T(8,128)(2,1)}, s16[64,2176]{1,0:T(8,128)(2,1)S(1)}, u32[]{:S(2)}, u32[]{:S(2)}) collective-permute-start(s16[64,2176]{1,0:T(8,128)(2,1)} %get-tuple-element.56), channel_id=1, source_target_pairs={{0,2},{1,3},{2,0},{3,1},{4,6},{5,7},{6,4},{7,5},{8,10},{9,11},{10,... | collective-permute-start | bytes 835592 | tf_op jit(solution)/shard_map/ppermute | solution.py:23
  150.9 23.5 %collective-permute-start.23 = (s16[64,2176]{1,0:T(8,128)(2,1)}, s16[64,2176]{1,0:T(8,128)(2,1)S(1)}, u32[]{:S(2)}, u32[]{:S(2)}) collective-permute-start(s16[64,2176]{1,0:T(8,128)(2,1)} %get-tuple-element.57), channel_id=1, source_target_pairs={{0,4},{1,5},{2,6},{3,7},{4,0},{5,1},{6,2},{7,3},{8,12},{9,13},{10,... | collective-permute-start | bytes 835592 | tf_op jit(solution)/shard_map/ppermute | solution.py:23
  153.4 21.2 %collective-permute-start.24 = (s16[64,2176]{1,0:T(8,128)(2,1)}, s16[64,2176]{1,0:T(8,128)(2,1)S(1)}, u32[]{:S(2)}, u32[]{:S(2)}) collective-permute-start(s16[64,2176]{1,0:T(8,128)(2,1)} %get-tuple-element.58), channel_id=1, source_target_pairs={{0,6},{1,7},{2,4},{3,5},{4,2},{5,3},{6,0},{7,1},{8,14},{9,15},{10,... | collective-permute-start | bytes 835592 | tf_op jit(solution)/shard_map/ppermute | solution.py:23
  171.1 25.9 %collective-permute-start.14 = (s16[32,2176]{1,0:T(8,128)(2,1)}, s16[32,2176]{1,0:T(8,128)(2,1)S(1)}, u32[]{:S(2)}, u32[]{:S(2)}) collective-permute-start(s16[32,2176]{1,0:T(8,128)(2,1)} %get-tuple-element.50), channel_id=1, source_target_pairs={{0,2},{1,3},{2,0},{3,1},{4,6},{5,7},{6,4},{7,5},{8,10},{9,11},{10,... | collective-permute-start | bytes 417800 | tf_op jit(solution)/shard_map/ppermute | solution.py:23
  172.0 25.0 %collective-permute-start.15 = (s16[32,2176]{1,0:T(8,128)(2,1)}, s16[32,2176]{1,0:T(8,128)(2,1)S(1)}, u32[]{:S(2)}, u32[]{:S(2)}) collective-permute-start(s16[32,2176]{1,0:T(8,128)(2,1)} %get-tuple-element.51), channel_id=1, source_target_pairs={{0,4},{1,5},{2,6},{3,7},{4,0},{5,1},{6,2},{7,3},{8,12},{9,13},{10,... | collective-permute-start | bytes 417800 | tf_op jit(solution)/shard_map/ppermute | solution.py:23
  174.3 22.7 %collective-permute-start.16 = (s16[32,2176]{1,0:T(8,128)(2,1)}, s16[32,2176]{1,0:T(8,128)(2,1)S(1)}, u32[]{:S(2)}, u32[]{:S(2)}) collective-permute-start(s16[32,2176]{1,0:T(8,128)(2,1)} %get-tuple-element.52), channel_id=1, source_target_pairs={{0,6},{1,7},{2,4},{3,5},{4,2},{5,3},{6,0},{7,1},{8,14},{9,15},{10,... | collective-permute-start | bytes 417800 | tf_op jit(solution)/shard_map/ppermute | solution.py:23
  174.6 15.3 %collective-permute-start.37 = (s16[32,2176]{1,0:T(8,128)(2,1)S(1)}, s16[32,2176]{1,0:T(8,128)(2,1)S(1)}, u32[]{:S(2)}, u32[]{:S(2)}) collective-permute-start(s16[32,2176]{1,0:T(8,128)(2,1)S(1)} %copy-done.32), channel_id=1, source_target_pairs={{0,4},{1,5},{2,6},{3,7},{4,0},{5,1},{6,2},{7,3},{8,12},{9,13},{10,... | collective-permute-start | bytes 417800 | tf_op jit(solution)/shard_map/ppermute | solution.py:23
  177.2 16.2 %collective-permute-start.38 = (s16[32,2176]{1,0:T(8,128)(2,1)S(1)}, s16[32,2176]{1,0:T(8,128)(2,1)S(1)}, u32[]{:S(2)}, u32[]{:S(2)}) collective-permute-start(s16[32,2176]{1,0:T(8,128)(2,1)S(1)} %copy-done.31), channel_id=1, source_target_pairs={{0,6},{1,7},{2,4},{3,5},{4,2},{5,3},{6,0},{7,1},{8,14},{9,15},{10,... | collective-permute-start | bytes 417800 | tf_op jit(solution)/shard_map/ppermute | solution.py:23
  203.4 26.8 %collective-permute-start.39 = (s16[32,2176]{1,0:T(8,128)(2,1)S(1)}, s16[32,2176]{1,0:T(8,128)(2,1)S(1)}, u32[]{:S(2)}, u32[]{:S(2)}) collective-permute-start(s16[32,2176]{1,0:T(8,128)(2,1)S(1)} %copy-done.28), channel_id=1, source_target_pairs={{0,2},{1,3},{2,0},{3,1},{4,6},{5,7},{6,4},{7,5},{8,10},{9,11},{10,... | collective-permute-start | bytes 417800 | tf_op jit(solution)/shard_map/ppermute | solution.py:23
  205.3 24.9 %collective-permute-start.40 = (s16[32,2176]{1,0:T(8,128)(2,1)S(1)}, s16[32,2176]{1,0:T(8,128)(2,1)S(1)}, u32[]{:S(2)}, u32[]{:S(2)}) collective-permute-start(s16[32,2176]{1,0:T(8,128)(2,1)S(1)} %copy-done.27), channel_id=1, source_target_pairs={{0,4},{1,5},{2,6},{3,7},{4,0},{5,1},{6,2},{7,3},{8,12},{9,13},{10,... | collective-permute-start | bytes 417800 | tf_op jit(solution)/shard_map/ppermute | solution.py:23
  206.4 23.9 %collective-permute-start.41 = (s16[32,2176]{1,0:T(8,128)(2,1)S(1)}, s16[32,2176]{1,0:T(8,128)(2,1)S(1)}, u32[]{:S(2)}, u32[]{:S(2)}) collective-permute-start(s16[32,2176]{1,0:T(8,128)(2,1)S(1)} %copy-done.26), channel_id=1, source_target_pairs={{0,6},{1,7},{2,4},{3,5},{4,2},{5,3},{6,0},{7,1},{8,14},{9,15},{10,... | collective-permute-start | bytes 417800 | tf_op jit(solution)/shard_map/ppermute | solution.py:23
  230.1 16.3 %collective-permute-start.28 = (s16[128,2176]{1,0:T(8,128)(2,1)S(1)}, s16[128,2176]{1,0:T(8,128)(2,1)S(1)}, u32[]{:S(2)}, u32[]{:S(2)}) collective-permute-start(s16[128,2176]{1,0:T(8,128)(2,1)S(1)} %constant_dynamic-update-slice_fusion.10.grad_ref), channel_id=1, source_target_pairs={{0,1},{1,0},{2,3},{3,2},{4,5},{5,4},{6,7},{7,6},{8,9},{9,8},{10,11... | collective-permute-start | bytes 1671176 | tf_op jit(solution)/shard_map/ppermute | solution.py:23
  (51 other events, 484.9 us)

commit v2 on v1

--- a/solution.py
+++ b/solution.py
@@ -120,7 +120,7 @@
         ref[...] = total[index * rows : (index + 1) * rows].astype(ref.dtype)
 
 
-def product(place, tokens, codes, scale, outs, dtype):
+def product(place, tokens, codes, scale, outs):
     ways = len(tokens)
     width = codes.shape[0]
     rows, part = tokens[0].shape
@@ -137,7 +137,8 @@
             + [scale_spec(j) for j in range(ways)],
             out_specs=[pl.BlockSpec((rows // outs, block), lambda i, p: (0, i))] * outs,
         ),
-        out_shape=[jax.ShapeDtypeStruct((rows // outs, width), dtype)] * outs,
+        out_shape=[jax.ShapeDtypeStruct((rows // outs, width), jnp.float32)]
+        + [jax.ShapeDtypeStruct((rows // outs, width), jnp.bfloat16)] * (outs - 1),
         cost_estimate=pl.CostEstimate(
             flops=2 * rows * part * ways * width,
             bytes_accessed=2 * part * ways * width,
@@ -595,19 +596,16 @@
     chunk_rows = rows // chunks
     place = jnp.stack([line, core])
 
-    remote = []
-    near = []
+    gathered = []
     for q in range(chunks):
         own = cotangent[q * chunk_rows : (q + 1) * chunk_rows]
         blocks = jnp.stack([own] + [swap(own, "tensor", m * ways) for m in range(1, groups)])
         arrived = jnp.concatenate(
-            [swap(pick(blocks, level ^ mine ^ m), "dp", m) for m in range(1, groups)],
+            [pick(blocks, level ^ mine)]
+            + [swap(pick(blocks, level ^ mine ^ m), "dp", m) for m in range(1, groups)],
             axis=0,
         )
-        near.append(pick(blocks, level ^ mine))
-        remote.append([arrived] + [swap(arrived, "tensor", m) for m in range(1, ways)])
-    near = jnp.concatenate(near, axis=0)
-    near = [near] + [swap(near, "tensor", m) for m in range(1, ways)]
+        gathered.append([arrived] + [swap(arrived, "tensor", m) for m in range(1, ways)])
 
     scale = jnp.exp2(exponents.astype(jnp.float32)).astype(jnp.bfloat16)
     scale = scale.reshape(-1, 1, part)
@@ -651,10 +649,9 @@
     cross_terms = []
     backs = []
     word_rows = chunk_rows // 16
-    kept = product(column_place, near, codes, scale, chunks, jnp.float32)
     for q in range(chunks):
-        sent = product(column_place, remote[q], codes, scale, groups - 1, jnp.bfloat16)
-        parts = [kept[q]] + [swap(sent[m - 1], "dp", m) for m in range(1, groups)]
+        sent = product(column_place, gathered[q], codes, scale, groups)
+        parts = [sent[0]] + [swap(sent[m], "dp", m) for m in range(1, groups)]
         words = clip_bits[q * word_rows : (q + 1) * word_rows]
         grads = gather_parts(place, parts, words, count)
         grads = [grads[0]] + [swap(grads[m], "tensor", 2 * m) for m in range(1, count)]

time: 270 us -> 289 us (1.070)
  waiting for transfers between devices: 100 us -> 125 us
  Pallas kernels: 80.4 us -> 74.6 us
  starting transfers between devices: 57.3 us -> 52.4 us
  other arithmetic: 7.7 us -> 11.3 us
    ppermute x49 -> x48, waiting for transfers between devices: 100 us -> 125 us  [swap(): return lax.ppermute(value, axis, pairs)]
    pallas_call x3 -> x2, Pallas kernels: 27 us -> 21.4 us  [product(): pl.pallas_call(functools.partial(product_kernel, ways), grid_spec=pltpu.P...]
    ppermute x49 -> x48, starting transfers between devices: 57.3 us -> 52.4 us  [swap(): return lax.ppermute(value, axis, pairs)]
  transfers between devices with their start and end apart: 49 -> 48, of which waited for: 15 -> 19; matrix products, arithmetic and copies ran while one was open for 7% -> 8% of each run, Pallas kernels for 25% -> 21%
where the time goes in v2:
time: 289 us; the launch traced here: 288 us
  waiting for transfers between devices  125 us (43%)
  Pallas kernels  74.6 us (26%)
  starting transfers between devices  52.4 us (18%)
  local copies, waits for them, and re-layouts  22.3 us (8%)
  other arithmetic  11.3 us (4%)
    ppermute x48, waiting for transfers between devices, swap(): return lax.ppermute(value, axis, pairs)  125 us
    ppermute x48, starting transfers between devices, swap(): return lax.ppermute(value, axis, pairs)  52.4 us
    pallas_call x2, Pallas kernels, product(): pl.pallas_call(functools.partial(product_kernel, ways), grid_spec=pltpu.P...  21.4 us
    pallas_call x2, Pallas kernels, backward_local(): pl.pallas_call(functools.partial(backward_kernel, local), grid_spec=pltpu...  20.5 us
    pallas_call x1, Pallas kernels, forward_local(): pl.pallas_call(functools.partial(forward_kernel, local), grid=(rows // bl...  14.5 us
    pallas_call x2, Pallas kernels, gather_parts(): pl.pallas_call(functools.partial(gather_kernel, count), grid_spec=pltpu.P...  6.78 us
    pallas_call x2, Pallas kernels, cross_sections(): pl.pallas_call(functools.partial(cross_kernel, count, bits), grid=(rows /...  6 us
  transfers between devices with their start and end apart: 48, of which 19 were waited for; matrix products, arithmetic and copies ran while one was open for 8% of the time, Pallas kernels for 21%

profile of v2, /device:TPU:8, one launch (start us, length us, event | category | flops | bytes accessed | tf_op | source)
XLA Modules:
  0.0 287.5 jit_solution(467177666236604496)
XLA Ops:
  1.8 2.7 collective-permute-start.15
  7.2 3.5 %collective-permute-start.26 = (bf16[128,1280]{1,0:T(8,128)(2,1)S(1)}, bf16[128,1280]{1,0:T(8,128)(2,1)S(1)}, u32[]{:S(2)}, u32[]{:S(2)}) collective-permute-start(bf16[128,1280]{1,0:T(8,128)(2,1)S(1)} %get-tuple-element.100), channel_id=1, source_target_pairs={{0,4},{1,5},{2,6},{3,7},{4,0},{5,1},{6,2},{7,3},{8,12},{9,13},{10,... | collective-permute-start | bytes 983048 | tf_op jit(solution)/shard_map/ppermute | solution.py:23
  21.0 14.5 %forward_local.1 = (f32[11,256,2048]{2,1,0:T(8,128)}, s16[256,2176]{1,0:T(8,128)(2,1)}) custom-call(bf16[256,2048]{1,0:T(8,128)(2,1)} %act_ref.1, f32[11,2048]{1,0:T(8,128)} %concatenate.78.cos_ref, f32[11,2048]{1,0:T(8,128)} %concatenate.88.sin_ref), custom_call_target="tpu_custom_call" | custom-call | flops 34603008 | bytes 25165824 | tf_op jit(solution)/shard_map/forward_local/pallas_call | solution.py:194
  39.8 12.3 %collective-permute-done.1 = bf16[128,1280]{1,0:T(8,128)(2,1)S(1)} collective-permute-done((bf16[128,1280]{1,0:T(8,128)(2,1)}, bf16[128,1280]{1,0:T(8,128)(2,1)S(1)}, u32[]{:S(2)}, u32[]{:S(2)}) %collective-permute-start.1) | collective-permute-done | bytes 327712 | tf_op jit(solution)/shard_map/ppermute | solution.py:23
  53.7 19.5 %collective-permute-done.2 = bf16[128,1280]{1,0:T(8,128)(2,1)S(1)} collective-permute-done((bf16[128,1280]{1,0:T(8,128)(2,1)}, bf16[128,1280]{1,0:T(8,128)(2,1)S(1)}, u32[]{:S(2)}, u32[]{:S(2)}) %collective-permute-start.2) | collective-permute-done | bytes 327712 | tf_op jit(solution)/shard_map/ppermute | solution.py:23
  73.4 2.5 collective-permute-start.5
  76.4 3.6 %collective-permute-done.27 = bf16[128,1280]{1,0:T(8,128)(2,1)S(1)} collective-permute-done((bf16[128,1280]{1,0:T(8,128)(2,1)S(1)}, bf16[128,1280]{1,0:T(8,128)(2,1)S(1)}, u32[]{:S(2)}, u32[]{:S(2)}) %collective-permute-start.27) | collective-permute-done | bytes 327712 | tf_op jit(solution)/shard_map/ppermute | solution.py:23
  81.8 3.2 %collective-permute-done.5 = bf16[128,1280]{1,0:T(8,128)(2,1)S(1)} collective-permute-done((bf16[128,1280]{1,0:T(8,128)(2,1)S(1)}, bf16[128,1280]{1,0:T(8,128)(2,1)S(1)}, u32[]{:S(2)}, u32[]{:S(2)}) %collective-permute-start.5) | collective-permute-done | bytes 327712 | tf_op jit(solution)/shard_map/ppermute | solution.py:23
  85.0 2.5 collective-permute-start.30
  87.5 4.5 %collective-permute-done.4 = bf16[128,1280]{1,0:T(8,128)(2,1)S(1)} collective-permute-done((bf16[128,1280]{1,0:T(8,128)(2,1)S(1)}, bf16[128,1280]{1,0:T(8,128)(2,1)S(1)}, u32[]{:S(2)}, u32[]{:S(2)}) %collective-permute-start.4) | collective-permute-done | bytes 327712 | tf_op jit(solution)/shard_map/ppermute | solution.py:23
  95.0 4.2 %collective-permute-done.30 = bf16[128,1280]{1,0:T(8,128)(2,1)} collective-permute-done((bf16[128,1280]{1,0:T(8,128)(2,1)S(1)}, bf16[128,1280]{1,0:T(8,128)(2,1)}, u32[]{:S(2)}, u32[]{:S(2)}) %collective-permute-start.30) | collective-permute-done | bytes 327712 | tf_op jit(solution)/shard_map/ppermute | solution.py:23
  99.2 6.5 %collective-permute-done.29 = bf16[128,1280]{1,0:T(8,128)(2,1)} collective-permute-done((bf16[128,1280]{1,0:T(8,128)(2,1)S(1)}, bf16[128,1280]{1,0:T(8,128)(2,1)}, u32[]{:S(2)}, u32[]{:S(2)}) %collective-permute-start.29) | collective-permute-done | bytes 327712 | tf_op jit(solution)/shard_map/ppermute | solution.py:23
  108.5 10.7 %product.2 = (f32[128,2048]{1,0:T(8,128)}, bf16[128,2048]{1,0:T(8,128)(2,1)}, bf16[128,2048]{1,0:T(8,128)(2,1)}, bf16[128,2048]{1,0:T(8,128)(2,1)}) custom-call(s32[2]{0:T(128)} %pad_add_fusion.1.place_ref, bf16[512,1280]{1,0:T(8,128)(2,1)} %copy-done, bf16[512,1280]{1,0:T(8,128)(2,1)} %collective-permute-done.6.refs_1_, bf16[2048,2560]{1,0:T(8,128)(2,1)} %refs_3_.3, ...), custom_call_target="tpu_custom_call" | custom-call | flops 5368709120 | bytes 10485760 | tf_op jit(solution)/shard_map/product/pallas_call | solution.py:130
  120.7 10.7 %product.3 = (f32[128,2048]{1,0:T(8,128)}, bf16[128,2048]{1,0:T(8,128)(2,1)}, bf16[128,2048]{1,0:T(8,128)(2,1)}, bf16[128,2048]{1,0:T(8,128)(2,1)}) custom-call(s32[2]{0:T(128)} %pad_add_fusion.1.place_ref, bf16[512,1280]{1,0:T(8,128)(2,1)} %copy-done.1, bf16[512,1280]{1,0:T(8,128)(2,1)} %collective-permute-done.31.refs_1_, bf16[2048,2560]{1,0:T(8,128)(2,1)} %refs_3_.3, ...), custom_call_target="tpu_custom_call" | custom-call | flops 5368709120 | bytes 10485760 | tf_op jit(solution)/shard_map/product/pallas_call | solution.py:130
  138.3 5.4 %core_forward.1 = (f32[2,2,4,32,1024]{4,3,2,1,0:T(8,128)}, s16[64,2176]{1,0:T(8,128)(2,1)}, s16[64,2176]{1,0:T(8,128)(2,1)}, s16[64,2176]{1,0:T(8,128)(2,1)}, s16[64,2176]{1,0:T(8,128)(2,1)}) custom-call(s32[2]{0:T(128)} %pad_add_fusion.place_ref, f32[11,2,4,32,2048]{4,3,2,1,0:T(8,128)} %bitcast.152, s16[2,4,32,2176]{3,2,1,0:T(8,128)(2,1)} %bitcast.43.other_ref, ...), custom_call_target="tpu_custom_call" | custom-call | flops 5242880 | bytes 6291456 | tf_op jit(solution)/shard_map/core_forward/pallas_call | solution.py:257
  146.7 11.6 %collective-permute-done.33 = bf16[128,2048]{1,0:T(8,128)(2,1)S(1)} collective-permute-done((bf16[128,2048]{1,0:T(8,128)(2,1)}, bf16[128,2048]{1,0:T(8,128)(2,1)S(1)}, u32[]{:S(2)}, u32[]{:S(2)}) %collective-permute-start.33) | collective-permute-done | bytes 524320 | tf_op jit(solution)/shard_map/ppermute | solution.py:23
  158.9 2.4 collective-permute-start.9
  161.3 3.3 %gather_parts.3 = (s16[32,2176]{1,0:T(8,128)(2,1)}, s16[32,2176]{1,0:T(8,128)(2,1)}, s16[32,2176]{1,0:T(8,128)(2,1)}, s16[32,2176]{1,0:T(8,128)(2,1)}) custom-call(s32[2]{0:T(128)} %pad_add_fusion.place_ref, f32[4,32,2048]{2,1,0:T(8,128)} %bitcast.156, bf16[4,32,2048]{2,1,0:T(8,128)(2,1)} %bitcast.160, bf16[4,32,2048]{2,1,0:T(8,128)(2,1)} %bitcast.161, ...), custom_call_target="tpu_custom_call" | custom-call | flops 3145728 | bytes 3145728 | tf_op jit(solution)/shard_map/gather_parts/pallas_call | solution.py:314
  164.6 15.0 %collective-permute-done.8 = bf16[128,2048]{1,0:T(8,128)(2,1)S(1)} collective-permute-done((bf16[128,2048]{1,0:T(8,128)(2,1)}, bf16[128,2048]{1,0:T(8,128)(2,1)S(1)}, u32[]{:S(2)}, u32[]{:S(2)}) %collective-permute-start.8) | collective-permute-done | bytes 524320 | tf_op jit(solution)/shard_map/ppermute | solution.py:23
  181.2 3.5 %gather_parts.2 = (s16[32,2176]{1,0:T(8,128)(2,1)}, s16[32,2176]{1,0:T(8,128)(2,1)}, s16[32,2176]{1,0:T(8,128)(2,1)}, s16[32,2176]{1,0:T(8,128)(2,1)}) custom-call(s32[2]{0:T(128)} %pad_add_fusion.place_ref, f32[4,32,2048]{2,1,0:T(8,128)} %bitcast.155, bf16[4,32,2048]{2,1,0:T(8,128)(2,1)} %bitcast.158, bf16[4,32,2048]{2,1,0:T(8,128)(2,1)} %bitcast.159, ...), custom_call_target="tpu_custom_call" | custom-call | flops 3145728 | bytes 3145728 | tf_op jit(solution)/shard_map/gather_parts/pallas_call | solution.py:314
  188.2 2.9 %collective-permute-start.36 = (s16[32,2176]{1,0:T(8,128)(2,1)S(1)}, s16[32,2176]{1,0:T(8,128)(2,1)S(1)}, u32[]{:S(2)}, u32[]{:S(2)}) collective-permute-start(s16[32,2176]{1,0:T(8,128)(2,1)S(1)} %copy-done.39), channel_id=1, source_target_pairs={{0,4},{1,5},{2,6},{3,7},{4,0},{5,1},{6,2},{7,3},{8,12},{9,13},{10,... | collective-permute-start | bytes 417800 | tf_op jit(solution)/shard_map/ppermute | solution.py:23
  193.2 15.0 %collective-permute-done.36.refs_2_ = s16[32,2176]{1,0:T(8,128)(2,1)S(1)} collective-permute-done((s16[32,2176]{1,0:T(8,128)(2,1)S(1)}, s16[32,2176]{1,0:T(8,128)(2,1)S(1)}, u32[]{:S(2)}, u32[]{:S(2)}) %collective-permute-start.36) | collective-permute-done | bytes 139296 | tf_op jit(solution)/shard_map/ppermute | solution.py:23
  208.2 3.5 %collective-permute-done.37.refs_3_ = s16[32,2176]{1,0:T(8,128)(2,1)S(1)} collective-permute-done((s16[32,2176]{1,0:T(8,128)(2,1)S(1)}, s16[32,2176]{1,0:T(8,128)(2,1)S(1)}, u32[]{:S(2)}, u32[]{:S(2)}) %collective-permute-start.37) | collective-permute-done | bytes 139296 | tf_op jit(solution)/shard_map/ppermute | solution.py:23
  212.3 3.0 %cross_sections.3 = (s16[32,2176]{1,0:T(8,128)(2,1)}, s16[32,2176]{1,0:T(8,128)(2,1)}, s16[32,2176]{1,0:T(8,128)(2,1)}, s16[32,2176]{1,0:T(8,128)(2,1)}, f32[2,2,2048]{2,1,0:T(2,128)}) custom-call(s16[32,2176]{1,0:T(8,128)(2,1)} %get-tuple-element.68.refs_0_, s16[32,2176]{1,0:T(8,128)(2,1)} %copy-done.18, s16[32,2176]{1,0:T(8,128)(2,1)} %copy-done.21, ...), custom_call_target="tpu_custom_call" | custom-call | flops 10485760 | bytes 1572864 | tf_op jit(solution)/shard_map/cross_sections/pallas_call | solution.py:405
  216.1 3.0 %cross_sections.2 = (s16[32,2176]{1,0:T(8,128)(2,1)}, s16[32,2176]{1,0:T(8,128)(2,1)}, s16[32,2176]{1,0:T(8,128)(2,1)}, s16[32,2176]{1,0:T(8,128)(2,1)}, f32[2,2,2048]{2,1,0:T(2,128)}) custom-call(s16[32,2176]{1,0:T(8,128)(2,1)} %get-tuple-element.49.refs_0_, s16[32,2176]{1,0:T(8,128)(2,1)} %copy-done.17, s16[32,2176]{1,0:T(8,128)(2,1)} %copy-done.19, ...), custom_call_target="tpu_custom_call" | custom-call | flops 10485760 | bytes 1572864 | tf_op jit(solution)/shard_map/cross_sections/pallas_call | solution.py:405
  225.2 2.9 collective-permute-start.21
  228.3 7.8 %collective-permute-done.43 = f32[2,2,1024]{2,1,0:T(2,128)S(1)} collective-permute-done((f32[2,2,1024]{2,1,0:T(2,128)S(1)}, f32[2,2,1024]{2,1,0:T(2,128)S(1)}, u32[]{:S(2)}, u32[]{:S(2)}) %collective-permute-start.43) | collective-permute-done | bytes 16416 | tf_op jit(solution)/shard_map/ppermute | solution.py:23
  238.9 7.0 %collective-permute-done.22 = s16[32,2176]{1,0:T(8,128)(2,1)S(1)} collective-permute-done((s16[32,2176]{1,0:T(8,128)(2,1)S(1)}, s16[32,2176]{1,0:T(8,128)(2,1)S(1)}, u32[]{:S(2)}, u32[]{:S(2)}) %collective-permute-start.22) | collective-permute-done | bytes 139296 | tf_op jit(solution)/shard_map/ppermute | solution.py:23
  245.9 4.1 %collective-permute-done.23 = s16[32,2176]{1,0:T(8,128)(2,1)S(1)} collective-permute-done((s16[32,2176]{1,0:T(8,128)(2,1)S(1)}, s16[32,2176]{1,0:T(8,128)(2,1)S(1)}, u32[]{:S(2)}, u32[]{:S(2)}) %collective-permute-start.23) | collective-permute-done | bytes 139296 | tf_op jit(solution)/shard_map/ppermute | solution.py:23
  255.9 10.3 %backward_local.2 = (bf16[256,2048]{1,0:T(8,128)(2,1)}, f32[7,16,64]{2,1,0:T(8,128)}, f32[4,8,128]{2,1,0:T(8,128)}, f32[8,128]{1,0:T(8,128)}) custom-call(s32[2]{0:T(128)} %pad_add_fusion.place_ref, s16[128,2176]{1,0:T(8,128)(2,1)} %copy-done.5, s16[128,2176]{1,0:T(8,128)(2,1)} %copy-done.9, ...), custom_call_target="tpu_custom_call", output_to_operand_aliasing={{0}: (12, {})} | custom-call | flops 23068672 | bytes 13631488 | tf_op jit(solution)/shard_map/backward_local/pallas_call | solution.py:520
  267.0 10.3 %backward_local.3 = (bf16[256,2048]{1,0:T(8,128)(2,1)}, f32[7,16,64]{2,1,0:T(8,128)}, f32[4,8,128]{2,1,0:T(8,128)}, f32[8,128]{1,0:T(8,128)}) custom-call(s32[2]{0:T(128)} %pad_add_fusion.place_ref, s16[128,2176]{1,0:T(8,128)(2,1)} %copy-done.6, s16[128,2176]{1,0:T(8,128)(2,1)} %copy-done.8, ...), custom_call_target="tpu_custom_call", output_to_operand_aliasing={{0}: (12, {})} | custom-call | flops 23068672 | bytes 13631488 | tf_op jit(solution)/shard_map/backward_local/pallas_call | solution.py:520
  283.9 2.9 collective-permute-done.47
  (286 shorter events, 71.4 us)
Async XLA Ops:
  1.8 33.7 %collective-permute-start.15 = (f32[2,3,1024]{2,1,0:T(4,128)S(1)}, f32[2,3,1024]{2,1,0:T(4,128)S(1)}, u32[]{:S(2)}, u32[]{:S(2)}) collective-permute-start(f32[2,3,1024]{2,1,0:T(4,128)S(1)} %get-tuple-element.123), channel_id=1, source_target_pairs={{0,4},{1,5},{2,6},{3,7},{4,0},{5,1},{6,2},{7,3},{8,12},{9,13},{10,... | collective-permute-start | bytes 73736 | tf_op jit(solution)/shard_map/ppermute | solution.py:23
  4.4 31.6 %collective-permute-start.14 = (f32[2,3,1024]{2,1,0:T(4,128)S(1)}, f32[2,3,1024]{2,1,0:T(4,128)S(1)}, u32[]{:S(2)}, u32[]{:S(2)}) collective-permute-start(f32[2,3,1024]{2,1,0:T(4,128)S(1)} %get-tuple-element.123), channel_id=1, source_target_pairs={{0,2},{1,3},{2,0},{3,1},{4,6},{5,7},{6,4},{7,5},{8,10},{9,11},{10,... | collective-permute-start | bytes 73736 | tf_op jit(solution)/shard_map/ppermute | solution.py:23
  4.9 32.7 %collective-permute-start.16 = (f32[2,3,1024]{2,1,0:T(4,128)S(1)}, f32[2,3,1024]{2,1,0:T(4,128)S(1)}, u32[]{:S(2)}, u32[]{:S(2)}) collective-permute-start(f32[2,3,1024]{2,1,0:T(4,128)S(1)} %get-tuple-element.123), channel_id=1, source_target_pairs={{0,6},{1,7},{2,4},{3,5},{4,2},{5,3},{6,0},{7,1},{8,14},{9,15},{10,... | collective-permute-start | bytes 73736 | tf_op jit(solution)/shard_map/ppermute | solution.py:23
  7.2 66.2 %collective-permute-start.26 = (bf16[128,1280]{1,0:T(8,128)(2,1)S(1)}, bf16[128,1280]{1,0:T(8,128)(2,1)S(1)}, u32[]{:S(2)}, u32[]{:S(2)}) collective-permute-start(bf16[128,1280]{1,0:T(8,128)(2,1)S(1)} %get-tuple-element.100), channel_id=1, source_target_pairs={{0,4},{1,5},{2,6},{3,7},{4,0},{5,1},{6,2},{7,3},{8,12},{9,13},{10,... | collective-permute-start | bytes 983048 | tf_op jit(solution)/shard_map/ppermute | solution.py:23
  10.7 65.2 %collective-permute-start.25 = (bf16[128,1280]{1,0:T(8,128)(2,1)S(1)}, bf16[128,1280]{1,0:T(8,128)(2,1)S(1)}, u32[]{:S(2)}, u32[]{:S(2)}) collective-permute-start(bf16[128,1280]{1,0:T(8,128)(2,1)S(1)} %get-tuple-element.100), channel_id=1, source_target_pairs={{0,2},{1,3},{2,0},{3,1},{4,6},{5,7},{6,4},{7,5},{8,10},{9,11},{10,... | collective-permute-start | bytes 983048 | tf_op jit(solution)/shard_map/ppermute | solution.py:23
  35.5 16.6 %collective-permute-start.1 = (bf16[128,1280]{1,0:T(8,128)(2,1)}, bf16[128,1280]{1,0:T(8,128)(2,1)S(1)}, u32[]{:S(2)}, u32[]{:S(2)}) collective-permute-start(bf16[128,1280]{1,0:T(8,128)(2,1)} %get-tuple-element.101), channel_id=1, source_target_pairs={{0,4},{1,5},{2,6},{3,7},{4,0},{5,1},{6,2},{7,3},{8,12},{9,13},{10,... | collective-permute-start | bytes 983048 | tf_op jit(solution)/shard_map/ppermute | solution.py:23
  36.1 17.6 %collective-permute-start = (bf16[128,1280]{1,0:T(8,128)(2,1)}, bf16[128,1280]{1,0:T(8,128)(2,1)S(1)}, u32[]{:S(2)}, u32[]{:S(2)}) collective-permute-start(bf16[128,1280]{1,0:T(8,128)(2,1)} %get-tuple-element.101), channel_id=1, source_target_pairs={{0,2},{1,3},{2,0},{3,1},{4,6},{5,7},{6,4},{7,5},{8,10},{9,11},{10,... | collective-permute-start | bytes 983048 | tf_op jit(solution)/shard_map/ppermute | solution.py:23
  37.6 35.5 %collective-permute-start.2 = (bf16[128,1280]{1,0:T(8,128)(2,1)}, bf16[128,1280]{1,0:T(8,128)(2,1)S(1)}, u32[]{:S(2)}, u32[]{:S(2)}) collective-permute-start(bf16[128,1280]{1,0:T(8,128)(2,1)} %get-tuple-element.101), channel_id=1, source_target_pairs={{0,6},{1,7},{2,4},{3,5},{4,2},{5,3},{6,0},{7,1},{8,14},{9,15},{10,... | collective-permute-start | bytes 983048 | tf_op jit(solution)/shard_map/ppermute | solution.py:23
  52.1 28.0 %collective-permute-start.27 = (bf16[128,1280]{1,0:T(8,128)(2,1)S(1)}, bf16[128,1280]{1,0:T(8,128)(2,1)S(1)}, u32[]{:S(2)}, u32[]{:S(2)}) collective-permute-start(bf16[128,1280]{1,0:T(8,128)(2,1)S(1)} %get-tuple-element.100), channel_id=1, source_target_pairs={{0,6},{1,7},{2,4},{3,5},{4,2},{5,3},{6,0},{7,1},{8,14},{9,15},{10,... | collective-permute-start | bytes 983048 | tf_op jit(solution)/shard_map/ppermute | solution.py:23
  53.7 81.3 %collective-permute-start.13 = (s16[256,2176]{1,0:T(8,128)(2,1)}, s16[256,2176]{1,0:T(8,128)(2,1)}, u32[]{:S(2)}, u32[]{:S(2)}) collective-permute-start(s16[256,2176]{1,0:T(8,128)(2,1)} %get-tuple-element.54), channel_id=1, source_target_pairs={{0,1},{1,0},{2,3},{3,2},{4,5},{5,4},{6,7},{7,6},{8,9},{9,8},{10,11... | collective-permute-start | bytes 3342344 | tf_op jit(solution)/shard_map/ppermute | solution.py:23
  73.1 20.8 %collective-permute-start.17 = (f32[4,2,3,1024]{3,2,1,0:T(4,128)S(1)}, f32[4,2,3,1024]{3,2,1,0:T(4,128)S(1)}, u32[]{:S(2)}, u32[]{:S(2)}) collective-permute-start(f32[4,2,3,1024]{3,2,1,0:T(4,128)S(1)} %broadcast_select_fusion), channel_id=1, source_target_pairs={{0,1},{1,0},{2,3},{3,2},{4,5},{5,4},{6,7},{7,6},{8,9},{9,8},{10,11... | collective-permute-start | bytes 294920 | tf_op jit(solution)/shard_map/ppermute | solution.py:23
  75.9 16.0 %collective-permute-start.4 = (bf16[128,1280]{1,0:T(8,128)(2,1)S(1)}, bf16[128,1280]{1,0:T(8,128)(2,1)S(1)}, u32[]{:S(2)}, u32[]{:S(2)}) collective-permute-start(bf16[128,1280]{1,0:T(8,128)(2,1)S(1)} %get-tuple-element.96), channel_id=1, source_target_pairs={{0,16},{8,24},{16,0},{24,8},{1,17},{9,25},{17,1},{25,9},{2,18},{10... | collective-permute-start | bytes 983048 | tf_op jit(solution)/shard_map/ppermute | solution.py:23
  85.0 14.2 %collective-permute-start.30 = (bf16[128,1280]{1,0:T(8,128)(2,1)S(1)}, bf16[128,1280]{1,0:T(8,128)(2,1)}, u32[]{:S(2)}, u32[]{:S(2)}) collective-permute-start(bf16[128,1280]{1,0:T(8,128)(2,1)S(1)} %get-tuple-element.91), channel_id=1, source_target_pairs={{0,24},{8,16},{16,8},{24,0},{1,25},{9,17},{17,9},{25,1},{2,26},{10... | collective-permute-start | bytes 983048 | tf_op jit(solution)/shard_map/ppermute | solution.py:23
  94.0 14.5 %collective-permute-start.6 = (bf16[512,1280]{1,0:T(8,128)(2,1)S(1)}, bf16[512,1280]{1,0:T(8,128)(2,1)}, u32[]{:S(2)}, u32[]{:S(2)}) collective-permute-start(bf16[512,1280]{1,0:T(8,128)(2,1)S(1)} %pad_maximum_fusion.1.refs_0_), channel_id=1, source_target_pairs={{0,1},{1,0},{2,3},{3,2},{4,5},{5,4},{6,7},{7,6},{8,9},{9,8},{10,11... | collective-permute-start | bytes 3932168 | tf_op jit(solution)/shard_map/ppermute | solution.py:23
  119.2 24.6 %collective-permute-start.7 = (bf16[128,2048]{1,0:T(8,128)(2,1)}, bf16[128,2048]{1,0:T(8,128)(2,1)S(1)}, u32[]{:S(2)}, u32[]{:S(2)}) collective-permute-start(bf16[128,2048]{1,0:T(8,128)(2,1)} %get-tuple-element.46), channel_id=1, source_target_pairs={{0,8},{8,0},{16,24},{24,16},{1,9},{9,1},{17,25},{25,17},{2,10},{10... | collective-permute-start | bytes 1572872 | tf_op jit(solution)/shard_map/ppermute | solution.py:23
  131.5 15.0 %collective-permute-start.32 = (bf16[128,2048]{1,0:T(8,128)(2,1)}, bf16[128,2048]{1,0:T(8,128)(2,1)S(1)}, u32[]{:S(2)}, u32[]{:S(2)}) collective-permute-start(bf16[128,2048]{1,0:T(8,128)(2,1)} %get-tuple-element.65), channel_id=1, source_target_pairs={{0,8},{8,0},{16,24},{24,16},{1,9},{9,1},{17,25},{25,17},{2,10},{10... | collective-permute-start | bytes 1572872 | tf_op jit(solution)/shard_map/ppermute | solution.py:23
  132.0 26.2 %collective-permute-start.33 = (bf16[128,2048]{1,0:T(8,128)(2,1)}, bf16[128,2048]{1,0:T(8,128)(2,1)S(1)}, u32[]{:S(2)}, u32[]{:S(2)}) collective-permute-start(bf16[128,2048]{1,0:T(8,128)(2,1)} %get-tuple-element.66), channel_id=1, source_target_pairs={{0,16},{8,24},{16,0},{24,8},{1,17},{9,25},{17,1},{25,9},{2,18},{10... | collective-permute-start | bytes 1572872 | tf_op jit(solution)/shard_map/ppermute | solution.py:23
  133.4 25.4 %collective-permute-start.34 = (bf16[128,2048]{1,0:T(8,128)(2,1)}, bf16[128,2048]{1,0:T(8,128)(2,1)}, u32[]{:S(2)}, u32[]{:S(2)}) collective-permute-start(bf16[128,2048]{1,0:T(8,128)(2,1)} %get-tuple-element.67), channel_id=1, source_target_pairs={{0,24},{8,16},{16,8},{24,0},{1,25},{9,17},{17,9},{25,1},{2,26},{10... | collective-permute-start | bytes 1572872 | tf_op jit(solution)/shard_map/ppermute | solution.py:23
  135.0 44.7 %collective-permute-start.8 = (bf16[128,2048]{1,0:T(8,128)(2,1)}, bf16[128,2048]{1,0:T(8,128)(2,1)S(1)}, u32[]{:S(2)}, u32[]{:S(2)}) collective-permute-start(bf16[128,2048]{1,0:T(8,128)(2,1)} %get-tuple-element.47), channel_id=1, source_target_pairs={{0,16},{8,24},{16,0},{24,8},{1,17},{9,25},{17,1},{25,9},{2,18},{10... | collective-permute-start | bytes 1572872 | tf_op jit(solution)/shard_map/ppermute | solution.py:23
  144.6 42.0 %collective-permute-start.18 = (s16[64,2176]{1,0:T(8,128)(2,1)}, s16[64,2176]{1,0:T(8,128)(2,1)S(1)}, u32[]{:S(2)}, u32[]{:S(2)}) collective-permute-start(s16[64,2176]{1,0:T(8,128)(2,1)} %get-tuple-element.56), channel_id=1, source_target_pairs={{0,2},{1,3},{2,0},{3,1},{4,6},{5,7},{6,4},{7,5},{8,10},{9,11},{10,... | collective-permute-start | bytes 835592 | tf_op jit(solution)/shard_map/ppermute | solution.py:23
  146.5 40.2 %collective-permute-start.19 = (s16[64,2176]{1,0:T(8,128)(2,1)}, s16[64,2176]{1,0:T(8,128)(2,1)S(1)}, u32[]{:S(2)}, u32[]{:S(2)}) collective-permute-start(s16[64,2176]{1,0:T(8,128)(2,1)} %get-tuple-element.57), channel_id=1, source_target_pairs={{0,4},{1,5},{2,6},{3,7},{4,0},{5,1},{6,2},{7,3},{8,12},{9,13},{10,... | collective-permute-start | bytes 835592 | tf_op jit(solution)/shard_map/ppermute | solution.py:23
  158.2 29.9 %collective-permute-start.20 = (s16[64,2176]{1,0:T(8,128)(2,1)}, s16[64,2176]{1,0:T(8,128)(2,1)S(1)}, u32[]{:S(2)}, u32[]{:S(2)}) collective-permute-start(s16[64,2176]{1,0:T(8,128)(2,1)} %get-tuple-element.58), channel_id=1, source_target_pairs={{0,6},{1,7},{2,4},{3,5},{4,2},{5,3},{6,0},{7,1},{8,14},{9,15},{10,... | collective-permute-start | bytes 835592 | tf_op jit(solution)/shard_map/ppermute | solution.py:23
  158.9 21.5 %collective-permute-start.9 = (bf16[128,2048]{1,0:T(8,128)(2,1)}, bf16[128,2048]{1,0:T(8,128)(2,1)S(1)}, u32[]{:S(2)}, u32[]{:S(2)}) collective-permute-start(bf16[128,2048]{1,0:T(8,128)(2,1)} %get-tuple-element.48), channel_id=1, source_target_pairs={{0,24},{8,16},{16,8},{24,0},{1,25},{9,17},{17,9},{25,1},{2,26},{10... | collective-permute-start | bytes 1572872 | tf_op jit(solution)/shard_map/ppermute | solution.py:23
  184.6 30.7 %collective-permute-start.10 = (s16[32,2176]{1,0:T(8,128)(2,1)}, s16[32,2176]{1,0:T(8,128)(2,1)S(1)}, u32[]{:S(2)}, u32[]{:S(2)}) collective-permute-start(s16[32,2176]{1,0:T(8,128)(2,1)} %get-tuple-element.50), channel_id=1, source_target_pairs={{0,2},{1,3},{2,0},{3,1},{4,6},{5,7},{6,4},{7,5},{8,10},{9,11},{10,... | collective-permute-start | bytes 417800 | tf_op jit(solution)/shard_map/ppermute | solution.py:23
  186.6 28.7 %collective-permute-start.11 = (s16[32,2176]{1,0:T(8,128)(2,1)}, s16[32,2176]{1,0:T(8,128)(2,1)S(1)}, u32[]{:S(2)}, u32[]{:S(2)}) collective-permute-start(s16[32,2176]{1,0:T(8,128)(2,1)} %get-tuple-element.51), channel_id=1, source_target_pairs={{0,4},{1,5},{2,6},{3,7},{4,0},{5,1},{6,2},{7,3},{8,12},{9,13},{10,... | collective-permute-start | bytes 417800 | tf_op jit(solution)/shard_map/ppermute | solution.py:23
  186.7 28.6 %collective-permute-start.12 = (s16[32,2176]{1,0:T(8,128)(2,1)}, s16[32,2176]{1,0:T(8,128)(2,1)S(1)}, u32[]{:S(2)}, u32[]{:S(2)}) collective-permute-start(s16[32,2176]{1,0:T(8,128)(2,1)} %get-tuple-element.52), channel_id=1, source_target_pairs={{0,6},{1,7},{2,4},{3,5},{4,2},{5,3},{6,0},{7,1},{8,14},{9,15},{10,... | collective-permute-start | bytes 417800 | tf_op jit(solution)/shard_map/ppermute | solution.py:23
  188.2 20.0 %collective-permute-start.36 = (s16[32,2176]{1,0:T(8,128)(2,1)S(1)}, s16[32,2176]{1,0:T(8,128)(2,1)S(1)}, u32[]{:S(2)}, u32[]{:S(2)}) collective-permute-start(s16[32,2176]{1,0:T(8,128)(2,1)S(1)} %copy-done.39), channel_id=1, source_target_pairs={{0,4},{1,5},{2,6},{3,7},{4,0},{5,1},{6,2},{7,3},{8,12},{9,13},{10,... | collective-permute-start | bytes 417800 | tf_op jit(solution)/shard_map/ppermute | solution.py:23
  191.1 20.5 %collective-permute-start.37 = (s16[32,2176]{1,0:T(8,128)(2,1)S(1)}, s16[32,2176]{1,0:T(8,128)(2,1)S(1)}, u32[]{:S(2)}, u32[]{:S(2)}) collective-permute-start(s16[32,2176]{1,0:T(8,128)(2,1)S(1)} %copy-done.38), channel_id=1, source_target_pairs={{0,6},{1,7},{2,4},{3,5},{4,2},{5,3},{6,0},{7,1},{8,14},{9,15},{10,... | collective-permute-start | bytes 417800 | tf_op jit(solution)/shard_map/ppermute | solution.py:23
  221.7 28.5 %collective-permute-start.38 = (s16[32,2176]{1,0:T(8,128)(2,1)S(1)}, s16[32,2176]{1,0:T(8,128)(2,1)S(1)}, u32[]{:S(2)}, u32[]{:S(2)}) collective-permute-start(s16[32,2176]{1,0:T(8,128)(2,1)S(1)} %copy-done.35), channel_id=1, source_target_pairs={{0,2},{1,3},{2,0},{3,1},{4,6},{5,7},{6,4},{7,5},{8,10},{9,11},{10,... | collective-permute-start | bytes 417800 | tf_op jit(solution)/shard_map/ppermute | solution.py:23
  223.7 26.5 %collective-permute-start.39 = (s16[32,2176]{1,0:T(8,128)(2,1)S(1)}, s16[32,2176]{1,0:T(8,128)(2,1)S(1)}, u32[]{:S(2)}, u32[]{:S(2)}) collective-permute-start(s16[32,2176]{1,0:T(8,128)(2,1)S(1)} %copy-done.34), channel_id=1, source_target_pairs={{0,4},{1,5},{2,6},{3,7},{4,0},{5,1},{6,2},{7,3},{8,12},{9,13},{10,... | collective-permute-start | bytes 417800 | tf_op jit(solution)/shard_map/ppermute | solution.py:23
  224.7 25.6 %collective-permute-start.40 = (s16[32,2176]{1,0:T(8,128)(2,1)S(1)}, s16[32,2176]{1,0:T(8,128)(2,1)S(1)}, u32[]{:S(2)}, u32[]{:S(2)}) collective-permute-start(s16[32,2176]{1,0:T(8,128)(2,1)S(1)} %copy-done.33), channel_id=1, source_target_pairs={{0,6},{1,7},{2,4},{3,5},{4,2},{5,3},{6,0},{7,1},{8,14},{9,15},{10,... | collective-permute-start | bytes 417800 | tf_op jit(solution)/shard_map/ppermute | solution.py:23
  250.1 16.1 %collective-permute-start.24 = (s16[128,2176]{1,0:T(8,128)(2,1)S(1)}, s16[128,2176]{1,0:T(8,128)(2,1)S(1)}, u32[]{:S(2)}, u32[]{:S(2)}) collective-permute-start(s16[128,2176]{1,0:T(8,128)(2,1)S(1)} %constant_dynamic-update-slice_fusion.grad_ref), channel_id=1, source_target_pairs={{0,1},{1,0},{2,3},{3,2},{4,5},{5,4},{6,7},{7,6},{8,9},{9,8},{10,11... | collective-permute-start | bytes 1671176 | tf_op jit(solution)/shard_map/ppermute | solution.py:23
  (57 other events, 533.5 us)

commit v3 on v2

--- a/solution.py
+++ b/solution.py
@@ -101,29 +101,37 @@
 
 
 def product_kernel(ways, place_ref, *refs):
-    token_refs = refs[:ways]
-    code_refs = refs[ways : 2 * ways]
-    scale_refs = refs[2 * ways : 3 * ways]
-    out_refs = refs[3 * ways :]
+    outs = (len(refs) - 3 * ways) // (ways + 1)
+    token_refs = refs[: ways * outs]
+    code_refs = refs[ways * outs : ways * (outs + 1)]
+    scale_refs = refs[ways * (outs + 1) : ways * (outs + 2)]
+    out_refs = refs[ways * (outs + 2) : -ways]
+    joined_refs = refs[-ways:]
+    rows = out_refs[0].shape[0]
+
+    @pl.when(pl.program_id(0) == 0)
+    def _():
+        for way, joined in enumerate(joined_refs):
+            for index in range(outs):
+                joined[pl.ds(index * rows, rows), :] = token_refs[way * outs + index][...]
+
     total = None
-    for tokens, codes, scale in zip(token_refs, code_refs, scale_refs):
-        weight = codes[...] * scale[0]
+    for joined, codes, scale in zip(joined_refs, code_refs, scale_refs):
         part = lax.dot_general(
-            tokens[...],
-            weight,
+            joined[...],
+            codes[...] * scale[0],
             (((1,), (1,)), ((), ())),
             preferred_element_type=jnp.float32,
         )
         total = part if total is None else total + part
-    rows = out_refs[0].shape[0]
     for index, ref in enumerate(out_refs):
         ref[...] = total[index * rows : (index + 1) * rows].astype(ref.dtype)
 
 
-def product(place, tokens, codes, scale, outs):
-    ways = len(tokens)
+def product(place, tokens, codes, scale):
+    ways, outs = len(tokens), len(tokens[0])
     width = codes.shape[0]
-    rows, part = tokens[0].shape
+    rows, part = tokens[0][0].shape
     block = min(width, 512)
     code_spec = lambda j: pl.BlockSpec((block, part), lambda i, p: (i, p[0] ^ j))
     scale_spec = lambda j: pl.BlockSpec((1, 1, part), lambda i, p: (p[1] + (p[0] ^ j), 0, 0))
@@ -132,20 +140,21 @@
         grid_spec=pltpu.PrefetchScalarGridSpec(
             num_scalar_prefetch=1,
             grid=(width // block,),
-            in_specs=[pl.BlockSpec((rows, part), lambda i, p: (0, 0))] * ways
+            in_specs=[pl.BlockSpec((rows, part), lambda i, p: (0, 0))] * (ways * outs)
             + [code_spec(j) for j in range(ways)]
             + [scale_spec(j) for j in range(ways)],
-            out_specs=[pl.BlockSpec((rows // outs, block), lambda i, p: (0, i))] * outs,
-        ),
-        out_shape=[jax.ShapeDtypeStruct((rows // outs, width), jnp.float32)]
-        + [jax.ShapeDtypeStruct((rows // outs, width), jnp.bfloat16)] * (outs - 1),
+            out_specs=[pl.BlockSpec((rows, block), lambda i, p: (0, i))] * outs,
+            scratch_shapes=[pltpu.VMEM((rows * outs, part), jnp.bfloat16)] * ways,
+        ),
+        out_shape=[jax.ShapeDtypeStruct((rows, width), jnp.float32)]
+        + [jax.ShapeDtypeStruct((rows, width), jnp.bfloat16)] * (outs - 1),
         cost_estimate=pl.CostEstimate(
-            flops=2 * rows * part * ways * width,
+            flops=2 * rows * outs * part * ways * width,
             bytes_accessed=2 * part * ways * width,
             transcendentals=0,
         ),
         name="product",
-    )(place, *tokens, *[codes] * ways, *[scale] * ways)
+    )(place, *[x for way in tokens for x in way], *[codes] * ways, *[scale] * ways)
 
 
 def forward_kernel(local, act_ref, cos_ref, sin_ref, states_ref, code_ref):
@@ -423,11 +432,13 @@
     return outs[:count], outs[count]
 
 
-def backward_kernel(
-    local, place_ref, grad_ref, other_ref, states_ref, pair_ref, trig_ref, cos_ref, sin_ref,
-    hot_ref, lane_in, tile_in, core_in, whole_ref,
-    out_ref, lane_out, tile_out, core_out, lane_sum, tile_sum, core_sum,
-):
+def backward_kernel(local, count, per, place_ref, *refs):
+    grad_refs = refs[:count]
+    other_refs = refs[count : 2 * count]
+    states_ref, pair_ref, trig_ref, cos_ref, sin_ref, hot_ref, term_in, _ = refs[
+        2 * count : 2 * count + 8
+    ]
+    out_ref, term_out, grad_ref, other_ref, lane_sum, tile_sum, core_sum = refs[2 * count + 8 :]
     rows, width = out_ref.shape
     tiles = width // LANES
     half = width // 2
@@ -439,6 +450,14 @@
         lane_sum[...] = jnp.zeros_like(lane_sum)
         tile_sum[...] = jnp.zeros_like(tile_sum)
         core_sum[...] = jnp.zeros_like(core_sum)
+
+    for piece in range(count):
+
+        @pl.when(index // per == piece)
+        def _():
+            at = pl.ds(pl.multiple_of((index % per) * rows, rows), rows)
+            grad_ref[...] = grad_refs[piece][at, :]
+            other_ref[...] = other_refs[piece][at, :]
 
     def folded(value):
         return jnp.sum(value.reshape(STEP // 8, 8, LANES), axis=0)
@@ -481,7 +500,7 @@
                 signed = sin_ref[section : section + 1, tile_at(tile)]
                 other = lane_partner(value, section)
                 state = states_ref[section, at, tile_at(tile)]
-                lane_sum[section, tile] += folded(other * state)
+                lane_sum[section, tile % 2, tile // 2] += folded(other * state)
                 value = cosine * value - signed * other
             out_ref[at, tile_at(tile)] = value.astype(out_ref.dtype)
         return carry
@@ -491,23 +510,27 @@
     @pl.when(index == pl.num_programs(0) - 1)
     def _():
         for section in range(LANE_BITS):
-            summed = jnp.sum(lane_sum[section], axis=1)
-            lane_out[section] = lane_in[section] + lax.dot_general(
-                summed,
-                hot_ref[section],
-                (((1,), (1,)), ((), ())),
-                precision=HIGH,
-                preferred_element_type=jnp.float32,
-            )
-        for section in range(local - LANE_BITS):
-            tile_out[section] = tile_in[section] + jnp.sum(tile_sum[section], axis=1)
-        core_out[...] = core_in[...] + jnp.sum(core_sum[...], axis=1)
+            terms = term_in[section]
+            for parity in range(2):
+                terms += lax.dot_general(
+                    jnp.sum(lane_sum[section, parity], axis=1),
+                    hot_ref[section, parity],
+                    (((1,), (1,)), ((), ())),
+                    precision=HIGH,
+                    preferred_element_type=jnp.float32,
+                )
+            term_out[section] = terms
+        for section in range(LANE_BITS, local):
+            term_out[section] = term_in[section] + jnp.sum(tile_sum[section - LANE_BITS], axis=1)
+        flip = (1 - 2 * place_ref[1]).astype(jnp.float32)
+        term_out[local] = term_in[local] + flip * jnp.sum(core_sum[...], axis=1)
 
 
 def backward_local(
-    place, grad, other, states, pair, trig, cos_table, sin_table, hot, sums, whole, chunk, count,
+    place, grads, others, states, pair, trig, cos_table, sin_table, hot, terms, whole, chunk
 ):
-    depth = grad.shape[0] // count
+    count = len(grads)
+    depth = grads[0].shape[0]
     local, rows, width = states.shape
     tiles = width // LANES
     high = local - LANE_BITS
@@ -516,42 +539,46 @@
     per = depth // block
     fixed = lambda shape: pl.BlockSpec(shape, lambda i, p: (0,) * len(shape))
     row_of = lambda i, p: (base + (p[0] ^ (i // per))) * per + i % per
-    shapes = [(LANE_BITS, tiles, LANES // 2), (high, tiles // 2, LANES), (tiles // 2, LANES)]
     return pl.pallas_call(
-        functools.partial(backward_kernel, local),
+        functools.partial(backward_kernel, local, count, per),
         grid_spec=pltpu.PrefetchScalarGridSpec(
             num_scalar_prefetch=1,
             grid=(count * per,),
-            in_specs=[
-                pl.BlockSpec((block, width + LANES), lambda i, p: (i, 0)),
-                pl.BlockSpec((block, width + LANES), lambda i, p: (i, 0)),
+            in_specs=[fixed((depth, width + LANES))] * (2 * count)
+            + [
                 pl.BlockSpec((local, block, width), lambda i, p: (0, row_of(i, p), 0)),
                 pl.BlockSpec((2, block, width // 2), lambda i, p: (0, row_of(i, p), 0)),
                 fixed((2, width)),
                 fixed((local, width)),
                 fixed((local, width)),
                 fixed(hot.shape),
-            ]
-            + [fixed(shape) for shape in shapes]
-            + [pl.BlockSpec(memory_space=pl.ANY)],
-            out_specs=[pl.BlockSpec((block, width), lambda i, p: (row_of(i, p), 0))]
-            + [fixed(shape) for shape in shapes],
+                fixed(terms.shape),
+                pl.BlockSpec(memory_space=pl.ANY),
+            ],
+            out_specs=[
+                pl.BlockSpec((block, width), lambda i, p: (row_of(i, p), 0)),
+                fixed(terms.shape),
+            ],
             scratch_shapes=[
-                pltpu.VMEM((LANE_BITS, tiles, 8, LANES), jnp.float32),
+                pltpu.VMEM((block, width + LANES), jnp.int16),
+                pltpu.VMEM((block, width + LANES), jnp.int16),
+                pltpu.VMEM((LANE_BITS, 2, tiles // 2, 8, LANES), jnp.float32),
                 pltpu.VMEM((high, tiles // 2, 8, LANES), jnp.float32),
                 pltpu.VMEM((tiles // 2, 8, LANES), jnp.float32),
             ],
         ),
-        out_shape=[jax.ShapeDtypeStruct((rows, width), jnp.bfloat16)]
-        + [jax.ShapeDtypeStruct(shape, jnp.float32) for shape in shapes],
-        input_output_aliases={12: 0},
+        out_shape=[
+            jax.ShapeDtypeStruct((rows, width), jnp.bfloat16),
+            jax.ShapeDtypeStruct(terms.shape, jnp.float32),
+        ],
+        input_output_aliases={2 * count + 8: 0},
         cost_estimate=pl.CostEstimate(
             flops=8 * local * depth * count * width,
             bytes_accessed=4 * (local + 2) * depth * count * width,
             transcendentals=0,
         ),
         name="backward_local",
-    )(place, grad, other, states, pair, trig, cos_table, sin_table, hot, *sums, whole)
+    )(place, *grads, *others, states, pair, trig, cos_table, sin_table, hot, terms, whole)
 
 
 def tree_sum(parts):
@@ -600,12 +627,13 @@
     for q in range(chunks):
         own = cotangent[q * chunk_rows : (q + 1) * chunk_rows]
         blocks = jnp.stack([own] + [swap(own, "tensor", m * ways) for m in range(1, groups)])
-        arrived = jnp.concatenate(
-            [pick(blocks, level ^ mine)]
-            + [swap(pick(blocks, level ^ mine ^ m), "dp", m) for m in range(1, groups)],
-            axis=0,
+        arrived = [pick(blocks, level ^ mine)] + [
+            swap(pick(blocks, level ^ mine ^ m), "dp", m) for m in range(1, groups)
+        ]
+        gathered.append(
+            [arrived]
+            + [[swap(x, "tensor", m) for x in arrived] for m in range(1, ways)]
         )
-        gathered.append([arrived] + [swap(arrived, "tensor", m) for m in range(1, ways)])
 
     scale = jnp.exp2(exponents.astype(jnp.float32)).astype(jnp.bfloat16)
     scale = scale.reshape(-1, 1, part)
@@ -639,18 +667,17 @@
 
     hot, signs = lane_selectors(LANE_BITS)
     hot = -hot * signs[:, None, :]
-    tiles = width // LANES
-    sums = [
-        jnp.zeros((LANE_BITS, tiles, LANES // 2), jnp.float32),
-        jnp.zeros((local - LANE_BITS, tiles // 2, LANES), jnp.float32),
-        jnp.zeros((tiles // 2, LANES), jnp.float32),
-    ]
+    empty = jnp.zeros_like(hot)
+    hot = jnp.stack(
+        [jnp.concatenate([hot, empty], axis=1), jnp.concatenate([empty, hot], axis=1)], axis=1
+    )
+    local_terms = jnp.zeros((local + 1, share // LANES, LANES), jnp.float32)
     whole = jnp.zeros((rows, width), jnp.bfloat16)
     cross_terms = []
     backs = []
     word_rows = chunk_rows // 16
     for q in range(chunks):
-        sent = product(column_place, gathered[q], codes, scale, groups)
+        sent = product(column_place, gathered[q], codes, scale)
         parts = [sent[0]] + [swap(sent[m], "dp", m) for m in range(1, groups)]
         words = clip_bits[q * word_rows : (q + 1) * word_rows]
         grads = gather_parts(place, parts, words, count)
@@ -660,12 +687,11 @@
         backs.append([grads[0]] + [swap(grads[m], "tensor", 2 * m) for m in range(1, count)])
 
     for q in range(chunks):
-        grad = jnp.concatenate(backs[q], axis=0)
-        outs = backward_local(
-            place, grad, swap(grad, "tensor", 1), states,
-            pair_states, core_trig, cos_table, sin_table, hot, sums, whole, q, count,
+        others = [swap(grad, "tensor", 1) for grad in backs[q]]
+        whole, local_terms = backward_local(
+            place, backs[q], others, states, pair_states, core_trig,
+            cos_table, sin_table, hot, local_terms, whole, q,
         )
-        whole, sums = outs[0], outs[1:]
 
     terms = functools.reduce(jnp.add, cross_terms)
     natural = jnp.stack(
@@ -681,16 +707,10 @@
     natural = jnp.moveaxis(natural.reshape(cross - 1, devices, share), 1, 0)
     owned = scatter_shares(natural, me, cross)
 
-    final = jnp.concatenate(
-        [
-            sums[0].reshape(LANE_BITS, share),
-            sums[1].reshape(local - LANE_BITS, share),
-            sums[2].reshape(1, share) * flip,
-            owned,
-        ],
-        axis=0,
-    )
+    owned = owned.reshape(cross - 1, share // LANES, LANES)
+    final = jnp.concatenate([local_terms, owned], axis=0)
     angle_grad = tree_sum([final] + [swap(final, "dp", m) for m in range(1, groups)])
+    angle_grad = angle_grad.reshape(sections, share)
     return (whole, angle_grad)
 
 

time: 289 us -> 283 us (0.979)
  waiting for transfers between devices: 125 us -> 119 us
  other arithmetic: 11.3 us -> 6.66 us
  Pallas kernels: 74.6 us -> 77.6 us
    ppermute x48 -> x60, waiting for transfers between devices: 125 us -> 119 us  [swap(): return lax.ppermute(value, axis, pairs)]
    unnamed x89 -> x103, local copies, waits for them, and re-layouts: 5.17 us -> 7.14 us
    ppermute x48 -> x60, starting transfers between devices: 52.4 us -> 53.4 us  [swap(): return lax.ppermute(value, axis, pairs)]
  transfers between devices with their start and end apart: 48 -> 60, of which waited for: 19 -> 23; matrix products, arithmetic and copies ran while one was open for 8% -> 6% of each run, Pallas kernels for 21% -> 22%
where the time goes in v3:
time: 283 us; the launch traced here: 281 us
  waiting for transfers between devices  119 us (42%)
  Pallas kernels  77.6 us (27%)
  starting transfers between devices  53.4 us (19%)
  local copies, waits for them, and re-layouts  21.7 us (8%)
  other arithmetic  6.66 us (2%)
    ppermute x60, waiting for transfers between devices, swap(): return lax.ppermute(value, axis, pairs)  119 us
    ppermute x60, starting transfers between devices, swap(): return lax.ppermute(value, axis, pairs)  53.4 us
    pallas_call x2, Pallas kernels, backward_local(): pl.pallas_call(functools.partial(backward_kernel, local, count, per), gri...  23.4 us
    pallas_call x2, Pallas kernels, product(): pl.pallas_call(functools.partial(product_kernel, ways), grid_spec=pltpu.P...  21.5 us
    pallas_call x1, Pallas kernels, forward_local(): pl.pallas_call(functools.partial(forward_kernel, local), grid=(rows // bl...  14.5 us
    unnamed x103, local copies, waits for them, and re-layouts  7.14 us
    pallas_call x2, Pallas kernels, gather_parts(): pl.pallas_call(functools.partial(gather_kernel, count), grid_spec=pltpu.P...  6.75 us
    pallas_call x2, Pallas kernels, cross_sections(): pl.pallas_call(functools.partial(cross_kernel, count, bits), grid=(rows /...  5.98 us
  transfers between devices with their start and end apart: 60, of which 23 were waited for; matrix products, arithmetic and copies ran while one was open for 6% of the time, Pallas kernels for 22%

profile of v3, /device:TPU:8, one launch (start us, length us, event | category | flops | bytes accessed | tf_op | source)
XLA Modules:
  0.0 281.0 jit_solution(12103629519856821423)
XLA Ops:
  1.8 2.7 collective-permute-start.18
  7.2 3.5 %collective-permute-start.32 = (bf16[128,1280]{1,0:T(8,128)(2,1)}, bf16[128,1280]{1,0:T(8,128)(2,1)S(1)}, u32[]{:S(2)}, u32[]{:S(2)}) collective-permute-start(bf16[128,1280]{1,0:T(8,128)(2,1)} %get-tuple-element.92), channel_id=1, source_target_pairs={{0,4},{1,5},{2,6},{3,7},{4,0},{5,1},{6,2},{7,3},{8,12},{9,13},{10,... | collective-permute-start | bytes 983048 | tf_op jit(solution)/shard_map/ppermute | solution.py:23
  17.7 14.5 %forward_local.1 = (f32[11,256,2048]{2,1,0:T(8,128)}, s16[256,2176]{1,0:T(8,128)(2,1)}) custom-call(bf16[256,2048]{1,0:T(8,128)(2,1)} %act_ref.1, f32[11,2048]{1,0:T(8,128)} %concatenate.71.cos_ref.refs_11_, f32[11,2048]{1,0:T(8,128)} %concatenate.81.sin_ref.refs_12_), custom_call_target="tpu_custom_call" | custom-call | flops 34603008 | bytes 25165824 | tf_op jit(solution)/shard_map/forward_local/pallas_call | solution.py:203
  32.7 3.8 %collective-permute-start.1 = (bf16[128,1280]{1,0:T(8,128)(2,1)S(1)}, bf16[128,1280]{1,0:T(8,128)(2,1)S(1)}, u32[]{:S(2)}, u32[]{:S(2)}) collective-permute-start(bf16[128,1280]{1,0:T(8,128)(2,1)S(1)} %get-tuple-element.93), channel_id=1, source_target_pairs={{0,4},{1,5},{2,6},{3,7},{4,0},{5,1},{6,2},{7,3},{8,12},{9,13},{10,... | collective-permute-start | bytes 983048 | tf_op jit(solution)/shard_map/ppermute | solution.py:23
  39.9 19.5 %collective-permute-done.33 = bf16[128,1280]{1,0:T(8,128)(2,1)S(1)} collective-permute-done((bf16[128,1280]{1,0:T(8,128)(2,1)}, bf16[128,1280]{1,0:T(8,128)(2,1)S(1)}, u32[]{:S(2)}, u32[]{:S(2)}) %collective-permute-start.33) | collective-permute-done | bytes 327712 | tf_op jit(solution)/shard_map/ppermute | solution.py:23
  59.7 2.5 collective-permute-start.36
  62.7 5.2 %collective-permute-done.1 = bf16[128,1280]{1,0:T(8,128)(2,1)S(1)} collective-permute-done((bf16[128,1280]{1,0:T(8,128)(2,1)S(1)}, bf16[128,1280]{1,0:T(8,128)(2,1)S(1)}, u32[]{:S(2)}, u32[]{:S(2)}) %collective-permute-start.1) | collective-permute-done | bytes 327712 | tf_op jit(solution)/shard_map/ppermute | solution.py:23
  67.9 7.9 %collective-permute-done.2 = bf16[128,1280]{1,0:T(8,128)(2,1)S(1)} collective-permute-done((bf16[128,1280]{1,0:T(8,128)(2,1)S(1)}, bf16[128,1280]{1,0:T(8,128)(2,1)S(1)}, u32[]{:S(2)}, u32[]{:S(2)}) %collective-permute-start.2) | collective-permute-done | bytes 327712 | tf_op jit(solution)/shard_map/ppermute | solution.py:23
  76.1 2.5 collective-permute-start.5
  82.4 5.4 %collective-permute-done.5.refs_3_ = bf16[128,1280]{1,0:T(8,128)(2,1)} collective-permute-done((bf16[128,1280]{1,0:T(8,128)(2,1)S(1)}, bf16[128,1280]{1,0:T(8,128)(2,1)}, u32[]{:S(2)}, u32[]{:S(2)}) %collective-permute-start.5) | collective-permute-done | bytes 327712 | tf_op jit(solution)/shard_map/ppermute | solution.py:23
  87.8 4.0 %collective-permute-done.4.refs_2_ = bf16[128,1280]{1,0:T(8,128)(2,1)} collective-permute-done((bf16[128,1280]{1,0:T(8,128)(2,1)S(1)}, bf16[128,1280]{1,0:T(8,128)(2,1)}, u32[]{:S(2)}, u32[]{:S(2)}) %collective-permute-start.4) | collective-permute-done | bytes 327712 | tf_op jit(solution)/shard_map/ppermute | solution.py:23
  91.8 3.1 %collective-permute-done.3.refs_1_ = bf16[128,1280]{1,0:T(8,128)(2,1)} collective-permute-done((bf16[128,1280]{1,0:T(8,128)(2,1)S(1)}, bf16[128,1280]{1,0:T(8,128)(2,1)}, u32[]{:S(2)}, u32[]{:S(2)}) %collective-permute-start.3) | collective-permute-done | bytes 327712 | tf_op jit(solution)/shard_map/ppermute | solution.py:23
  94.9 3.9 %collective-permute-done.34.refs_1_ = bf16[128,1280]{1,0:T(8,128)(2,1)S(1)} collective-permute-done((bf16[128,1280]{1,0:T(8,128)(2,1)S(1)}, bf16[128,1280]{1,0:T(8,128)(2,1)S(1)}, u32[]{:S(2)}, u32[]{:S(2)}) %collective-permute-start.34) | collective-permute-done | bytes 327712 | tf_op jit(solution)/shard_map/ppermute | solution.py:23
  101.3 10.7 %product.2 = (f32[128,2048]{1,0:T(8,128)}, bf16[128,2048]{1,0:T(8,128)(2,1)}, bf16[128,2048]{1,0:T(8,128)(2,1)}, bf16[128,2048]{1,0:T(8,128)(2,1)}) custom-call(s32[2]{0:T(128)} %pad_add_fusion.1.place_ref, bf16[128,1280]{1,0:T(8,128)(2,1)} %copy-done.1, bf16[128,1280]{1,0:T(8,128)(2,1)} %collective-permute-done.3.refs_1_, ...), custom_call_target="tpu_custom_call" | custom-call | flops 5368709120 | bytes 10485760 | tf_op jit(solution)/shard_map/product/pallas_call | solution.py:138
  114.3 10.8 %product.3 = (f32[128,2048]{1,0:T(8,128)}, bf16[128,2048]{1,0:T(8,128)(2,1)}, bf16[128,2048]{1,0:T(8,128)(2,1)}, bf16[128,2048]{1,0:T(8,128)(2,1)}) custom-call(s32[2]{0:T(128)} %pad_add_fusion.1.place_ref, bf16[128,1280]{1,0:T(8,128)(2,1)} %copy-done, bf16[128,1280]{1,0:T(8,128)(2,1)} %copy-done.11, bf16[128,1280]{1,0:T(8,128)(2,1)} %collective-permute-done.35.refs_2_, ...), custom_call_target="tpu_custom_call" | custom-call | flops 5368709120 | bytes 10485760 | tf_op jit(solution)/shard_map/product/pallas_call | solution.py:138
  126.2 2.4 collective-permute-start.43
  131.1 5.5 %core_forward.1 = (f32[2,2,4,32,1024]{4,3,2,1,0:T(8,128)}, s16[64,2176]{1,0:T(8,128)(2,1)}, s16[64,2176]{1,0:T(8,128)(2,1)}, s16[64,2176]{1,0:T(8,128)(2,1)}, s16[64,2176]{1,0:T(8,128)(2,1)}) custom-call(s32[2]{0:T(128)} %pad_add_fusion.place_ref, f32[11,2,4,32,2048]{4,3,2,1,0:T(8,128)} %bitcast.159, s16[2,4,32,2176]{3,2,1,0:T(8,128)(2,1)} %bitcast.162, ...), custom_call_target="tpu_custom_call" | custom-call | flops 5242880 | bytes 6291456 | tf_op jit(solution)/shard_map/core_forward/pallas_call | solution.py:266
  141.0 22.3 %collective-permute-done.42 = bf16[128,2048]{1,0:T(8,128)(2,1)} collective-permute-done((bf16[128,2048]{1,0:T(8,128)(2,1)}, bf16[128,2048]{1,0:T(8,128)(2,1)}, u32[]{:S(2)}, u32[]{:S(2)}) %collective-permute-start.42) | collective-permute-done | bytes 524320 | tf_op jit(solution)/shard_map/ppermute | solution.py:23
  165.1 3.3 %gather_parts.3 = (s16[32,2176]{1,0:T(8,128)(2,1)}, s16[32,2176]{1,0:T(8,128)(2,1)}, s16[32,2176]{1,0:T(8,128)(2,1)}, s16[32,2176]{1,0:T(8,128)(2,1)}) custom-call(s32[2]{0:T(128)} %pad_add_fusion.place_ref, f32[4,32,2048]{2,1,0:T(8,128)} %bitcast.164, bf16[4,32,2048]{2,1,0:T(8,128)(2,1)} %bitcast.168, bf16[4,32,2048]{2,1,0:T(8,128)(2,1)} %bitcast.78.refs_2_, ...), custom_call_target="tpu_custom_call" | custom-call | flops 3145728 | bytes 3145728 | tf_op jit(solution)/shard_map/gather_parts/pallas_call | solution.py:323
  168.4 4.6 %collective-permute-done.11 = bf16[128,2048]{1,0:T(8,128)(2,1)S(1)} collective-permute-done((bf16[128,2048]{1,0:T(8,128)(2,1)}, bf16[128,2048]{1,0:T(8,128)(2,1)S(1)}, u32[]{:S(2)}, u32[]{:S(2)}) %collective-permute-start.11) | collective-permute-done | bytes 524320 | tf_op jit(solution)/shard_map/ppermute | solution.py:23
  174.5 3.4 %gather_parts.2 = (s16[32,2176]{1,0:T(8,128)(2,1)}, s16[32,2176]{1,0:T(8,128)(2,1)}, s16[32,2176]{1,0:T(8,128)(2,1)}, s16[32,2176]{1,0:T(8,128)(2,1)}) custom-call(s32[2]{0:T(128)} %pad_add_fusion.place_ref, f32[4,32,2048]{2,1,0:T(8,128)} %bitcast.163, bf16[4,32,2048]{2,1,0:T(8,128)(2,1)} %bitcast.166, bf16[4,32,2048]{2,1,0:T(8,128)(2,1)} %bitcast.167, ...), custom_call_target="tpu_custom_call" | custom-call | flops 3145728 | bytes 3145728 | tf_op jit(solution)/shard_map/gather_parts/pallas_call | solution.py:323
  181.8 3.8 %collective-permute-start.45 = (s16[32,2176]{1,0:T(8,128)(2,1)S(1)}, s16[32,2176]{1,0:T(8,128)(2,1)S(1)}, u32[]{:S(2)}, u32[]{:S(2)}) collective-permute-start(s16[32,2176]{1,0:T(8,128)(2,1)S(1)} %copy-done.48), channel_id=1, source_target_pairs={{0,4},{1,5},{2,6},{3,7},{4,0},{5,1},{6,2},{7,3},{8,12},{9,13},{10,... | collective-permute-start | bytes 417800 | tf_op jit(solution)/shard_map/ppermute | solution.py:23
  186.6 15.8 %collective-permute-done.45.refs_2_ = s16[32,2176]{1,0:T(8,128)(2,1)S(1)} collective-permute-done((s16[32,2176]{1,0:T(8,128)(2,1)S(1)}, s16[32,2176]{1,0:T(8,128)(2,1)S(1)}, u32[]{:S(2)}, u32[]{:S(2)}) %collective-permute-start.45) | collective-permute-done | bytes 139296 | tf_op jit(solution)/shard_map/ppermute | solution.py:23
  202.4 2.4 collective-permute-done.46.refs_3_
  205.5 3.0 %cross_sections.3 = (s16[32,2176]{1,0:T(8,128)(2,1)}, s16[32,2176]{1,0:T(8,128)(2,1)}, s16[32,2176]{1,0:T(8,128)(2,1)}, s16[32,2176]{1,0:T(8,128)(2,1)}, f32[2,2,2048]{2,1,0:T(2,128)}) custom-call(s16[32,2176]{1,0:T(8,128)(2,1)} %get-tuple-element.64.refs_0_, s16[32,2176]{1,0:T(8,128)(2,1)} %copy-done.18, s16[32,2176]{1,0:T(8,128)(2,1)} %copy-done.21, ...), custom_call_target="tpu_custom_call" | custom-call | flops 10485760 | bytes 1572864 | tf_op jit(solution)/shard_map/cross_sections/pallas_call | solution.py:414
  209.2 3.0 %cross_sections.2 = (s16[32,2176]{1,0:T(8,128)(2,1)}, s16[32,2176]{1,0:T(8,128)(2,1)}, s16[32,2176]{1,0:T(8,128)(2,1)}, s16[32,2176]{1,0:T(8,128)(2,1)}, f32[2,2,2048]{2,1,0:T(2,128)}) custom-call(s16[32,2176]{1,0:T(8,128)(2,1)} %get-tuple-element.45.refs_0_, s16[32,2176]{1,0:T(8,128)(2,1)} %copy-done.17, s16[32,2176]{1,0:T(8,128)(2,1)} %copy-done.19, ...), custom_call_target="tpu_custom_call" | custom-call | flops 10485760 | bytes 1572864 | tf_op jit(solution)/shard_map/cross_sections/pallas_call | solution.py:414
  215.8 3.8 %collective-permute-done.54 = f32[4,2,1024]{2,1,0:T(2,128)S(1)} collective-permute-done((f32[4,2,1024]{2,1,0:T(2,128)S(1)}, f32[4,2,1024]{2,1,0:T(2,128)S(1)}, u32[]{:S(2)}, u32[]{:S(2)}) %collective-permute-start.54) | collective-permute-done | bytes 32800 | tf_op jit(solution)/shard_map/ppermute | solution.py:23
  223.3 2.8 collective-permute-start.24
  230.0 10.5 %collective-permute-done.49.refs_3_ = s16[32,2176]{1,0:T(8,128)(2,1)S(1)} collective-permute-done((s16[32,2176]{1,0:T(8,128)(2,1)S(1)}, s16[32,2176]{1,0:T(8,128)(2,1)S(1)}, u32[]{:S(2)}, u32[]{:S(2)}) %collective-permute-start.49) | collective-permute-done | bytes 139296 | tf_op jit(solution)/shard_map/ppermute | solution.py:23
  242.2 2.8 collective-permute-done.26.refs_3_
  248.1 11.8 %backward_local.2 = (bf16[256,2048]{1,0:T(8,128)(2,1)}, f32[12,8,128]{2,1,0:T(8,128)}) custom-call(s32[2]{0:T(128)} %pad_add_fusion.place_ref, s16[32,2176]{1,0:T(8,128)(2,1)} %get-tuple-element.68.refs_0_, s16[32,2176]{1,0:T(8,128)(2,1)} %copy-done.26, s16[32,2176]{1,0:T(8,128)(2,1)} %copy-done.27, ...), custom_call_target="tpu_custom_call", output_to_operand_aliasing={{0}: (16, {})} | custom-call | flops 23068672 | bytes 13631488 | tf_op jit(solution)/shard_map/backward_local/pallas_call | solution.py:542
  260.7 11.6 %backward_local.3 = (bf16[256,2048]{1,0:T(8,128)(2,1)}, f32[12,8,128]{2,1,0:T(8,128)}) custom-call(s32[2]{0:T(128)} %pad_add_fusion.place_ref, s16[32,2176]{1,0:T(8,128)(2,1)} %get-tuple-element.55.refs_0_, s16[32,2176]{1,0:T(8,128)(2,1)} %copy-done.25, s16[32,2176]{1,0:T(8,128)(2,1)} %copy-done.28, ...), custom_call_target="tpu_custom_call", output_to_operand_aliasing={{0}: (16, {})} | custom-call | flops 23068672 | bytes 13631488 | tf_op jit(solution)/shard_map/backward_local/pallas_call | solution.py:542
  (318 shorter events, 66.6 us)
Async XLA Ops:
  1.8 30.4 %collective-permute-start.18 = (f32[2,3,1024]{2,1,0:T(4,128)S(1)}, f32[2,3,1024]{2,1,0:T(4,128)S(1)}, u32[]{:S(2)}, u32[]{:S(2)}) collective-permute-start(f32[2,3,1024]{2,1,0:T(4,128)S(1)} %get-tuple-element.117), channel_id=1, source_target_pairs={{0,4},{1,5},{2,6},{3,7},{4,0},{5,1},{6,2},{7,3},{8,12},{9,13},{10,... | collective-permute-start | bytes 73736 | tf_op jit(solution)/shard_map/ppermute | solution.py:23
  4.4 28.3 %collective-permute-start.17 = (f32[2,3,1024]{2,1,0:T(4,128)S(1)}, f32[2,3,1024]{2,1,0:T(4,128)S(1)}, u32[]{:S(2)}, u32[]{:S(2)}) collective-permute-start(f32[2,3,1024]{2,1,0:T(4,128)S(1)} %get-tuple-element.117), channel_id=1, source_target_pairs={{0,2},{1,3},{2,0},{3,1},{4,6},{5,7},{6,4},{7,5},{8,10},{9,11},{10,... | collective-permute-start | bytes 73736 | tf_op jit(solution)/shard_map/ppermute | solution.py:23
  4.9 31.7 %collective-permute-start.19 = (f32[2,3,1024]{2,1,0:T(4,128)S(1)}, f32[2,3,1024]{2,1,0:T(4,128)S(1)}, u32[]{:S(2)}, u32[]{:S(2)}) collective-permute-start(f32[2,3,1024]{2,1,0:T(4,128)S(1)} %get-tuple-element.117), channel_id=1, source_target_pairs={{0,6},{1,7},{2,4},{3,5},{4,2},{5,3},{6,0},{7,1},{8,14},{9,15},{10,... | collective-permute-start | bytes 73736 | tf_op jit(solution)/shard_map/ppermute | solution.py:23
  7.2 32.1 %collective-permute-start.32 = (bf16[128,1280]{1,0:T(8,128)(2,1)}, bf16[128,1280]{1,0:T(8,128)(2,1)S(1)}, u32[]{:S(2)}, u32[]{:S(2)}) collective-permute-start(bf16[128,1280]{1,0:T(8,128)(2,1)} %get-tuple-element.92), channel_id=1, source_target_pairs={{0,4},{1,5},{2,6},{3,7},{4,0},{5,1},{6,2},{7,3},{8,12},{9,13},{10,... | collective-permute-start | bytes 983048 | tf_op jit(solution)/shard_map/ppermute | solution.py:23
  10.7 29.2 %collective-permute-start.31 = (bf16[128,1280]{1,0:T(8,128)(2,1)}, bf16[128,1280]{1,0:T(8,128)(2,1)S(1)}, u32[]{:S(2)}, u32[]{:S(2)}) collective-permute-start(bf16[128,1280]{1,0:T(8,128)(2,1)} %get-tuple-element.92), channel_id=1, source_target_pairs={{0,2},{1,3},{2,0},{3,1},{4,6},{5,7},{6,4},{7,5},{8,10},{9,11},{10,... | collective-permute-start | bytes 983048 | tf_op jit(solution)/shard_map/ppermute | solution.py:23
  32.1 27.3 %collective-permute-start.33 = (bf16[128,1280]{1,0:T(8,128)(2,1)}, bf16[128,1280]{1,0:T(8,128)(2,1)S(1)}, u32[]{:S(2)}, u32[]{:S(2)}) collective-permute-start(bf16[128,1280]{1,0:T(8,128)(2,1)} %get-tuple-element.92), channel_id=1, source_target_pairs={{0,6},{1,7},{2,4},{3,5},{4,2},{5,3},{6,0},{7,1},{8,14},{9,15},{10,... | collective-permute-start | bytes 983048 | tf_op jit(solution)/shard_map/ppermute | solution.py:23
  32.7 35.1 %collective-permute-start.1 = (bf16[128,1280]{1,0:T(8,128)(2,1)S(1)}, bf16[128,1280]{1,0:T(8,128)(2,1)S(1)}, u32[]{:S(2)}, u32[]{:S(2)}) collective-permute-start(bf16[128,1280]{1,0:T(8,128)(2,1)S(1)} %get-tuple-element.93), channel_id=1, source_target_pairs={{0,4},{1,5},{2,6},{3,7},{4,0},{5,1},{6,2},{7,3},{8,12},{9,13},{10,... | collective-permute-start | bytes 983048 | tf_op jit(solution)/shard_map/ppermute | solution.py:23
  38.7 29.1 %collective-permute-start = (bf16[128,1280]{1,0:T(8,128)(2,1)S(1)}, bf16[128,1280]{1,0:T(8,128)(2,1)S(1)}, u32[]{:S(2)}, u32[]{:S(2)}) collective-permute-start(bf16[128,1280]{1,0:T(8,128)(2,1)S(1)} %get-tuple-element.93), channel_id=1, source_target_pairs={{0,2},{1,3},{2,0},{3,1},{4,6},{5,7},{6,4},{7,5},{8,10},{9,11},{10,... | collective-permute-start | bytes 983048 | tf_op jit(solution)/shard_map/ppermute | solution.py:23
  39.3 36.5 %collective-permute-start.2 = (bf16[128,1280]{1,0:T(8,128)(2,1)S(1)}, bf16[128,1280]{1,0:T(8,128)(2,1)S(1)}, u32[]{:S(2)}, u32[]{:S(2)}) collective-permute-start(bf16[128,1280]{1,0:T(8,128)(2,1)S(1)} %get-tuple-element.93), channel_id=1, source_target_pairs={{0,6},{1,7},{2,4},{3,5},{4,2},{5,3},{6,0},{7,1},{8,14},{9,15},{10,... | collective-permute-start | bytes 983048 | tf_op jit(solution)/shard_map/ppermute | solution.py:23
  59.7 21.1 %collective-permute-start.36 = (bf16[128,1280]{1,0:T(8,128)(2,1)S(1)}, bf16[128,1280]{1,0:T(8,128)(2,1)}, u32[]{:S(2)}, u32[]{:S(2)}) collective-permute-start(bf16[128,1280]{1,0:T(8,128)(2,1)S(1)} %get-tuple-element.82), channel_id=1, source_target_pairs={{0,24},{8,16},{16,8},{24,0},{1,25},{9,17},{17,9},{25,1},{2,26},{10... | collective-permute-start | bytes 983048 | tf_op jit(solution)/shard_map/ppermute | solution.py:23
  62.2 20.2 %collective-permute-start.35 = (bf16[128,1280]{1,0:T(8,128)(2,1)S(1)}, bf16[128,1280]{1,0:T(8,128)(2,1)}, u32[]{:S(2)}, u32[]{:S(2)}) collective-permute-start(bf16[128,1280]{1,0:T(8,128)(2,1)S(1)} %get-tuple-element.83), channel_id=1, source_target_pairs={{0,16},{8,24},{16,0},{24,8},{1,17},{9,25},{17,1},{25,9},{2,18},{10... | collective-permute-start | bytes 983048 | tf_op jit(solution)/shard_map/ppermute | solution.py:23
  79.1 15.7 %collective-permute-start.3 = (bf16[128,1280]{1,0:T(8,128)(2,1)S(1)}, bf16[128,1280]{1,0:T(8,128)(2,1)}, u32[]{:S(2)}, u32[]{:S(2)}) collective-permute-start(bf16[128,1280]{1,0:T(8,128)(2,1)S(1)} %get-tuple-element.88), channel_id=1, source_target_pairs={{0,8},{8,0},{16,24},{24,16},{1,9},{9,1},{17,25},{25,17},{2,10},{10... | collective-permute-start | bytes 983048 | tf_op jit(solution)/shard_map/ppermute | solution.py:23
  80.8 17.9 %collective-permute-start.34 = (bf16[128,1280]{1,0:T(8,128)(2,1)S(1)}, bf16[128,1280]{1,0:T(8,128)(2,1)S(1)}, u32[]{:S(2)}, u32[]{:S(2)}) collective-permute-start(bf16[128,1280]{1,0:T(8,128)(2,1)S(1)} %get-tuple-element.84), channel_id=1, source_target_pairs={{0,8},{8,0},{16,24},{24,16},{1,9},{9,1},{17,25},{25,17},{2,10},{10... | collective-permute-start | bytes 983048 | tf_op jit(solution)/shard_map/ppermute | solution.py:23
  82.4 16.4 %collective-permute-start.6 = (bf16[128,1280]{1,0:T(8,128)(2,1)S(1)}, bf16[128,1280]{1,0:T(8,128)(2,1)S(1)}, u32[]{:S(2)}, u32[]{:S(2)}) collective-permute-start(bf16[128,1280]{1,0:T(8,128)(2,1)S(1)} %get-tuple-element.89.refs_0_), channel_id=1, source_target_pairs={{0,1},{1,0},{2,3},{3,2},{4,5},{5,4},{6,7},{7,6},{8,9},{9,8},{10,11... | collective-permute-start | bytes 983048 | tf_op jit(solution)/shard_map/ppermute | solution.py:23
  98.8 29.9 %collective-permute-start.16 = (s16[256,2176]{1,0:T(8,128)(2,1)}, s16[256,2176]{1,0:T(8,128)(2,1)S(1)}, u32[]{:S(2)}, u32[]{:S(2)}) collective-permute-start(s16[256,2176]{1,0:T(8,128)(2,1)} %get-tuple-element.50), channel_id=1, source_target_pairs={{0,1},{1,0},{2,3},{3,2},{4,5},{5,4},{6,7},{7,6},{8,9},{9,8},{10,11... | collective-permute-start | bytes 3342344 | tf_op jit(solution)/shard_map/ppermute | solution.py:23
  112.8 23.8 %collective-permute-start.10 = (bf16[128,2048]{1,0:T(8,128)(2,1)}, bf16[128,2048]{1,0:T(8,128)(2,1)S(1)}, u32[]{:S(2)}, u32[]{:S(2)}) collective-permute-start(bf16[128,2048]{1,0:T(8,128)(2,1)} %get-tuple-element.42), channel_id=1, source_target_pairs={{0,8},{8,0},{16,24},{24,16},{1,9},{9,1},{17,25},{25,17},{2,10},{10... | collective-permute-start | bytes 1572872 | tf_op jit(solution)/shard_map/ppermute | solution.py:23
  125.7 37.6 %collective-permute-start.42 = (bf16[128,2048]{1,0:T(8,128)(2,1)}, bf16[128,2048]{1,0:T(8,128)(2,1)}, u32[]{:S(2)}, u32[]{:S(2)}) collective-permute-start(bf16[128,2048]{1,0:T(8,128)(2,1)} %get-tuple-element.62), channel_id=1, source_target_pairs={{0,16},{8,24},{16,0},{24,8},{1,17},{9,25},{17,1},{25,9},{2,18},{10... | collective-permute-start | bytes 1572872 | tf_op jit(solution)/shard_map/ppermute | solution.py:23
  126.2 37.1 %collective-permute-start.43 = (bf16[128,2048]{1,0:T(8,128)(2,1)}, bf16[128,2048]{1,0:T(8,128)(2,1)}, u32[]{:S(2)}, u32[]{:S(2)}) collective-permute-start(bf16[128,2048]{1,0:T(8,128)(2,1)} %get-tuple-element.63), channel_id=1, source_target_pairs={{0,24},{8,16},{16,8},{24,0},{1,25},{9,17},{17,9},{25,1},{2,26},{10... | collective-permute-start | bytes 1572872 | tf_op jit(solution)/shard_map/ppermute | solution.py:23
  128.7 44.3 %collective-permute-start.11 = (bf16[128,2048]{1,0:T(8,128)(2,1)}, bf16[128,2048]{1,0:T(8,128)(2,1)S(1)}, u32[]{:S(2)}, u32[]{:S(2)}) collective-permute-start(bf16[128,2048]{1,0:T(8,128)(2,1)} %get-tuple-element.43), channel_id=1, source_target_pairs={{0,16},{8,24},{16,0},{24,8},{1,17},{9,25},{17,1},{25,9},{2,18},{10... | collective-permute-start | bytes 1572872 | tf_op jit(solution)/shard_map/ppermute | solution.py:23
  136.6 37.1 %collective-permute-start.12 = (bf16[128,2048]{1,0:T(8,128)(2,1)}, bf16[128,2048]{1,0:T(8,128)(2,1)S(1)}, u32[]{:S(2)}, u32[]{:S(2)}) collective-permute-start(bf16[128,2048]{1,0:T(8,128)(2,1)} %get-tuple-element.44), channel_id=1, source_target_pairs={{0,24},{8,16},{16,8},{24,0},{1,25},{9,17},{17,9},{25,1},{2,26},{10... | collective-permute-start | bytes 1572872 | tf_op jit(solution)/shard_map/ppermute | solution.py:23
  141.0 38.9 %collective-permute-start.21 = (s16[64,2176]{1,0:T(8,128)(2,1)}, s16[64,2176]{1,0:T(8,128)(2,1)S(1)}, u32[]{:S(2)}, u32[]{:S(2)}) collective-permute-start(s16[64,2176]{1,0:T(8,128)(2,1)} %get-tuple-element.52), channel_id=1, source_target_pairs={{0,2},{1,3},{2,0},{3,1},{4,6},{5,7},{6,4},{7,5},{8,10},{9,11},{10,... | collective-permute-start | bytes 835592 | tf_op jit(solution)/shard_map/ppermute | solution.py:23
  163.3 17.9 %collective-permute-start.22 = (s16[64,2176]{1,0:T(8,128)(2,1)}, s16[64,2176]{1,0:T(8,128)(2,1)S(1)}, u32[]{:S(2)}, u32[]{:S(2)}) collective-permute-start(s16[64,2176]{1,0:T(8,128)(2,1)} %get-tuple-element.53), channel_id=1, source_target_pairs={{0,4},{1,5},{2,6},{3,7},{4,0},{5,1},{6,2},{7,3},{8,12},{9,13},{10,... | collective-permute-start | bytes 835592 | tf_op jit(solution)/shard_map/ppermute | solution.py:23
  163.3 18.5 %collective-permute-start.23 = (s16[64,2176]{1,0:T(8,128)(2,1)}, s16[64,2176]{1,0:T(8,128)(2,1)S(1)}, u32[]{:S(2)}, u32[]{:S(2)}) collective-permute-start(s16[64,2176]{1,0:T(8,128)(2,1)} %get-tuple-element.54), channel_id=1, source_target_pairs={{0,6},{1,7},{2,4},{3,5},{4,2},{5,3},{6,0},{7,1},{8,14},{9,15},{10,... | collective-permute-start | bytes 835592 | tf_op jit(solution)/shard_map/ppermute | solution.py:23
  178.0 30.5 %collective-permute-start.13 = (s16[32,2176]{1,0:T(8,128)(2,1)}, s16[32,2176]{1,0:T(8,128)(2,1)S(1)}, u32[]{:S(2)}, u32[]{:S(2)}) collective-permute-start(s16[32,2176]{1,0:T(8,128)(2,1)} %get-tuple-element.46), channel_id=1, source_target_pairs={{0,2},{1,3},{2,0},{3,1},{4,6},{5,7},{6,4},{7,5},{8,10},{9,11},{10,... | collective-permute-start | bytes 417800 | tf_op jit(solution)/shard_map/ppermute | solution.py:23
  180.0 28.5 %collective-permute-start.14 = (s16[32,2176]{1,0:T(8,128)(2,1)}, s16[32,2176]{1,0:T(8,128)(2,1)S(1)}, u32[]{:S(2)}, u32[]{:S(2)}) collective-permute-start(s16[32,2176]{1,0:T(8,128)(2,1)} %get-tuple-element.47), channel_id=1, source_target_pairs={{0,4},{1,5},{2,6},{3,7},{4,0},{5,1},{6,2},{7,3},{8,12},{9,13},{10,... | collective-permute-start | bytes 417800 | tf_op jit(solution)/shard_map/ppermute | solution.py:23
  181.2 27.3 %collective-permute-start.15 = (s16[32,2176]{1,0:T(8,128)(2,1)}, s16[32,2176]{1,0:T(8,128)(2,1)S(1)}, u32[]{:S(2)}, u32[]{:S(2)}) collective-permute-start(s16[32,2176]{1,0:T(8,128)(2,1)} %get-tuple-element.48), channel_id=1, source_target_pairs={{0,6},{1,7},{2,4},{3,5},{4,2},{5,3},{6,0},{7,1},{8,14},{9,15},{10,... | collective-permute-start | bytes 417800 | tf_op jit(solution)/shard_map/ppermute | solution.py:23
  181.8 20.6 %collective-permute-start.45 = (s16[32,2176]{1,0:T(8,128)(2,1)S(1)}, s16[32,2176]{1,0:T(8,128)(2,1)S(1)}, u32[]{:S(2)}, u32[]{:S(2)}) collective-permute-start(s16[32,2176]{1,0:T(8,128)(2,1)S(1)} %copy-done.48), channel_id=1, source_target_pairs={{0,4},{1,5},{2,6},{3,7},{4,0},{5,1},{6,2},{7,3},{8,12},{9,13},{10,... | collective-permute-start | bytes 417800 | tf_op jit(solution)/shard_map/ppermute | solution.py:23
  185.6 19.2 %collective-permute-start.46 = (s16[32,2176]{1,0:T(8,128)(2,1)S(1)}, s16[32,2176]{1,0:T(8,128)(2,1)S(1)}, u32[]{:S(2)}, u32[]{:S(2)}) collective-permute-start(s16[32,2176]{1,0:T(8,128)(2,1)S(1)} %copy-done.47), channel_id=1, source_target_pairs={{0,6},{1,7},{2,4},{3,5},{4,2},{5,3},{6,0},{7,1},{8,14},{9,15},{10,... | collective-permute-start | bytes 417800 | tf_op jit(solution)/shard_map/ppermute | solution.py:23
  222.8 17.7 %collective-permute-start.49 = (s16[32,2176]{1,0:T(8,128)(2,1)S(1)}, s16[32,2176]{1,0:T(8,128)(2,1)S(1)}, u32[]{:S(2)}, u32[]{:S(2)}) collective-permute-start(s16[32,2176]{1,0:T(8,128)(2,1)S(1)} %copy-done.44), channel_id=1, source_target_pairs={{0,6},{1,7},{2,4},{3,5},{4,2},{5,3},{6,0},{7,1},{8,14},{9,15},{10,... | collective-permute-start | bytes 417800 | tf_op jit(solution)/shard_map/ppermute | solution.py:23
  223.3 17.1 %collective-permute-start.24 = (s16[32,2176]{1,0:T(8,128)(2,1)}, s16[32,2176]{1,0:T(8,128)(2,1)S(1)}, u32[]{:S(2)}, u32[]{:S(2)}) collective-permute-start(s16[32,2176]{1,0:T(8,128)(2,1)} %get-tuple-element.56), channel_id=1, source_target_pairs={{0,2},{1,3},{2,0},{3,1},{4,6},{5,7},{6,4},{7,5},{8,10},{9,11},{10,... | collective-permute-start | bytes 417800 | tf_op jit(solution)/shard_map/ppermute | solution.py:23
  228.8 16.1 %collective-permute-start.26 = (s16[32,2176]{1,0:T(8,128)(2,1)S(1)}, s16[32,2176]{1,0:T(8,128)(2,1)S(1)}, u32[]{:S(2)}, u32[]{:S(2)}) collective-permute-start(s16[32,2176]{1,0:T(8,128)(2,1)S(1)} %copy-done.42), channel_id=1, source_target_pairs={{0,6},{1,7},{2,4},{3,5},{4,2},{5,3},{6,0},{7,1},{8,14},{9,15},{10,... | collective-permute-start | bytes 417800 | tf_op jit(solution)/shard_map/ppermute | solution.py:23
  242.0 17.9 %collective-permute-start.27 = (s16[32,2176]{1,0:T(8,128)(2,1)S(1)}, s16[32,2176]{1,0:T(8,128)(2,1)S(1)}, u32[]{:S(2)}, u32[]{:S(2)}) collective-permute-start(s16[32,2176]{1,0:T(8,128)(2,1)S(1)} %copy-done.23), channel_id=1, source_target_pairs={{0,1},{1,0},{2,3},{3,2},{4,5},{5,4},{6,7},{7,6},{8,9},{9,8},{10,11... | collective-permute-start | bytes 417800 | tf_op jit(solution)/shard_map/ppermute | solution.py:23
  (78 other events, 760.2 us)
